TPU v7x, 32 devices: a whole 2x2x4 slice. The times are simulated.
32 devices in a mesh: group: 8 (over y, x, core), expert: 4 (over z).
Axes of the slice: x: 2, y: 2, z: 4, core: 2. Of those that a mesh axis runs over, the one named last changes fastest.
Arguments:
- tokens: bfloat16 [8192, 1024], P(('group', 'expert')), may hold values from -6 to 6
- lengths: int32 [8], P('group'), may hold values from 256 to 1024, as said below
- routes: int32 [8192, 8], P(('group', 'expert')), may hold values from 0 to 31, all different within a row; in each aligned block of 256 rows (0 to 255, 256 to 511, ...) at most 96 rows name the same one
- norm_gain1: bfloat16 [1024], P('expert'), may hold values from 0.5 to 1.5
- w_query: bfloat16 [1024, 1024], P('expert'), may hold values from -0.375 to 0.375
- key_projection: bfloat16 [1024, 512], P('expert'), may hold values from -0.1875 to 0.1875
- value_projection: bfloat16 [1024, 512], P('expert'), may hold values from -0.1875 to 0.1875
- w_out: bfloat16 [1024, 1024], P('expert'), may hold values from -1.5 to 1.5
- norm_gain2: bfloat16 [1024], P('expert'), may hold values from 0.5 to 1.5
- w_router: bfloat16 [1024, 32], P('expert'), may hold values from -0.09375 to 0.09375
- w_gate: bfloat16 [32, 1024, 512], P('expert'), may hold values from -0.1875 to 0.1875
- w_up: bfloat16 [32, 1024, 512], P('expert'), may hold values from -0.1875 to 0.1875
- w_down: bfloat16 [32, 512, 1024], P('expert'), may hold values from -1 to 1
- cotangent: bfloat16 [8192, 1024], P(('group', 'expert')), may hold values from -6 to 6
Outputs:
- mixed: bfloat16 [8192, 1024], P(('group', 'expert'))
- grad_tokens: float32 [8192, 1024], P(('group', 'expert'))
- grad_gain1: float32 [1024], P('expert')
- grad_query: float32 [1024, 1024], P('expert')
- grad_key: float32 [1024, 512], P('expert')
- grad_value: float32 [1024, 512], P('expert')
- grad_out: float32 [1024, 1024], P('expert')
- grad_gain2: float32 [1024], P('expert')
- grad_router: float32 [1024, 32], P('expert')
- grad_gate: float32 [32, 1024, 512], P('expert')
- grad_up: float32 [32, 1024, 512], P('expert')
- grad_down: float32 [32, 512, 1024], P('expert')
Inputs may be any that keep to these rules, and one draw needn't show every extreme that they name: The first lengths[s] slots of sequence s are valid; one sequence fills all 1024 slots and one holds 256. `routes`: a slot's 8 experts differ; among the rows of one device at most 96 name one expert, and in every draw some expert is named by exactly 96 of them.
All inputs are finite; a program needn't handle non-finite values.
Results may differ from a plain program's by a relative error of at most 0.028.
Values may be sent and summed in bfloat16 or wider, within the bound.
A program may use at most 256 MiB of HBM per device.

v0:
```python
import jax
import jax.numpy as jnp
from jax import lax
from jax.sharding import PartitionSpec as P

D = 1024
QUERY_HEADS = 16
KEY_VALUE_HEADS = 8
HEAD_DIMENSION = 64
EXPERTS = 32
TOP = 8


EPSILON = 1e-05
NEGATIVE_LARGE = -1e30


def rotary_tables(positions, head_size):
    half_width = head_size // 2
    frequency = 10000.0 ** (-2.0 * jnp.arange(half_width).astype(jnp.float32) / head_size)
    angles = positions.astype(jnp.float32)[:, None] * frequency[None, :]
    return (jnp.cos(angles)[:, None, :], jnp.sin(angles)[:, None, :])


def apply_rotation(tensor_in, cosine_lookup, sine_lookup):
    half_width = tensor_in.shape[-1] // 2
    first_half = tensor_in[..., :half_width]
    second_half = tensor_in[..., half_width:]
    return jnp.concatenate(
        [
            first_half * cosine_lookup - second_half * sine_lookup,
            second_half * cosine_lookup + first_half * sine_lookup,
        ],
        axis=-1,
    )


def per_device(
    tokens,
    lengths,
    routes,
    norm_gain1,
    w_query,
    key_projection,
    value_projection,
    w_out,
    norm_gain2,
    w_router,
    w_gate,
    w_up,
    w_down,
    cotangent,
):
    count_of_rows = tokens.shape[0]
    devices_here = lax.axis_size("expert")
    my_index = lax.axis_index("expert")
    sequence_tokens = count_of_rows * devices_here
    capacity = 3 * count_of_rows * TOP // (2 * EXPERTS)
    group_of_heads = QUERY_HEADS // KEY_VALUE_HEADS
    score_scale = HEAD_DIMENSION ** (-0.5)
    brain_float = jnp.bfloat16
    single_float = jnp.float32
    gain_one, query_weight, key_weight, value_weight, out_weight, gain_two, router_weight = (
        lax.all_gather(norm_gain1, "expert", axis=0, tiled=True),
        lax.all_gather(w_query, "expert", axis=0, tiled=True),
        lax.all_gather(key_projection, "expert", axis=0, tiled=True),
        lax.all_gather(value_projection, "expert", axis=0, tiled=True),
        lax.all_gather(w_out, "expert", axis=0, tiled=True),
        lax.all_gather(norm_gain2, "expert", axis=0, tiled=True),
        lax.all_gather(w_router, "expert", axis=0, tiled=True),
    )
    gain_one = gain_one.astype(single_float)
    gain_two = gain_two.astype(single_float)
    length = lengths[0]
    positions = my_index * count_of_rows + jnp.arange(count_of_rows, dtype=jnp.int32)
    cosine_lookup, sine_lookup = rotary_tables(positions, HEAD_DIMENSION)
    token_f32 = tokens.astype(single_float)
    inverse_one = lax.rsqrt(jnp.mean(token_f32 * token_f32, axis=-1, keepdims=True) + EPSILON)
    unit_one = token_f32 * inverse_one
    pre_attention_norm = (unit_one * gain_one).astype(brain_float)
    query_pre = jnp.dot(pre_attention_norm, query_weight, preferred_element_type=single_float)
    unrotated_key = jnp.dot(pre_attention_norm, key_weight, preferred_element_type=single_float)
    value_pre = jnp.dot(pre_attention_norm, value_weight, preferred_element_type=single_float)
    query_rows = apply_rotation(
        query_pre.reshape(count_of_rows, QUERY_HEADS, HEAD_DIMENSION), cosine_lookup, sine_lookup
    ).astype(brain_float)
    query_rows = query_rows.reshape(count_of_rows, KEY_VALUE_HEADS, group_of_heads, HEAD_DIMENSION)
    local_keys = apply_rotation(
        unrotated_key.reshape(count_of_rows, KEY_VALUE_HEADS, HEAD_DIMENSION),
        cosine_lookup,
        sine_lookup,
    ).astype(brain_float)
    local_keys = local_keys.reshape(count_of_rows, KEY_VALUE_HEADS * HEAD_DIMENSION)
    local_values = value_pre.astype(brain_float)
    key_portion = lax.all_gather(local_keys, "expert", axis=0, tiled=True).reshape(
        -1, KEY_VALUE_HEADS, HEAD_DIMENSION
    )
    value_portion = lax.all_gather(local_values, "expert", axis=0, tiled=True).reshape(
        -1, KEY_VALUE_HEADS, HEAD_DIMENSION
    )
    key_count = key_portion.shape[0]
    running_maximum = jnp.full(
        (KEY_VALUE_HEADS, group_of_heads, count_of_rows), NEGATIVE_LARGE, single_float
    )
    scores = (
        jnp.einsum("qhgd,khd->hgqk", query_rows, key_portion, preferred_element_type=single_float)
        * score_scale
    )
    columns = jnp.arange(key_count, dtype=jnp.int32)
    allowed = (columns[None, :] <= positions[:, None]) & (columns[None, :] < length)
    masked = jnp.where(allowed, scores, NEGATIVE_LARGE)
    new_max = jnp.maximum(running_maximum, jnp.max(masked, axis=-1))
    block_weights = jnp.where(allowed, jnp.exp(masked - new_max[..., None]), 0.0)
    new_sum = jnp.sum(block_weights, axis=-1)
    new_acc = jnp.einsum(
        "hgqk,khd->hgqd",
        block_weights.astype(brain_float),
        value_portion,
        preferred_element_type=single_float,
    )
    final_state = (new_max, new_sum, new_acc)
    running_maximum, running_sum, running_acc = final_state
    mixed_f32 = running_acc / running_sum[..., None]
    log_total = running_maximum + jnp.log(running_sum)
    mixed_low = (
        jnp.transpose(mixed_f32, (2, 0, 1, 3))
        .reshape(count_of_rows, QUERY_HEADS * HEAD_DIMENSION)
        .astype(brain_float)
    )
    residual = token_f32 + jnp.dot(mixed_low, out_weight, preferred_element_type=single_float)
    inverse_two = lax.rsqrt(jnp.mean(residual * residual, axis=-1, keepdims=True) + EPSILON)
    unit_two = residual * inverse_two
    second_norm = (unit_two * gain_two).astype(brain_float)
    logits = jnp.dot(second_norm, router_weight, preferred_element_type=single_float)
    expert_ids = jnp.arange(EXPERTS, dtype=jnp.int32)
    route_hot = routes[:, :, None] == expert_ids[None, None, :]
    chosen = jnp.sum(jnp.where(route_hot, logits[:, None, :], 0.0), axis=-1)
    gate_weights = jax.nn.softmax(chosen, axis=-1)
    flat_routes = routes.reshape(-1)
    one_hot = (flat_routes[:, None] == expert_ids[None, :]).astype(jnp.int32)
    slot_rank = jnp.sum((jnp.cumsum(one_hot, axis=0) - one_hot) * one_hot, axis=-1)
    slot_index = flat_routes * capacity + slot_rank
    copies = jnp.repeat(second_norm, TOP, axis=0)
    send_buffer = jnp.zeros((EXPERTS * capacity, D), brain_float).at[slot_index].set(copies)
    send_buffer = send_buffer.reshape(EXPERTS, capacity, D)
    received = lax.all_to_all(send_buffer, "expert", split_axis=0, concat_axis=1, tiled=True)
    gate_pre = jnp.einsum("erd,edf->erf", received, w_gate, preferred_element_type=single_float)
    up_pre = jnp.einsum("erd,edf->erf", received, w_up, preferred_element_type=single_float)
    sigmoid_gate = jax.nn.sigmoid(gate_pre)
    silu_gate = gate_pre * sigmoid_gate
    activation = (silu_gate * up_pre).astype(brain_float)
    expert_out = jnp.einsum(
        "erf,efd->erd", activation, w_down, preferred_element_type=single_float
    ).astype(brain_float)
    returned = lax.all_to_all(expert_out, "expert", split_axis=1, concat_axis=0, tiled=True)
    picked = returned.reshape(EXPERTS * capacity, D)[slot_index].reshape(count_of_rows, TOP, D)
    expert_sum = jnp.einsum("qk,qkd->qd", gate_weights, picked, preferred_element_type=single_float)
    mixed = (residual + expert_sum).astype(brain_float)
    valid_rows = (positions < length).astype(single_float)[:, None]
    grad_output = cotangent.astype(single_float) * valid_rows
    grad_gates = jnp.einsum("qd,qkd->qk", grad_output, picked, preferred_element_type=single_float)
    grad_chosen = gate_weights * (
        grad_gates - jnp.sum(gate_weights * grad_gates, axis=-1, keepdims=True)
    )
    grad_logits = jnp.sum(jnp.where(route_hot, grad_chosen[:, :, None], 0.0), axis=1).astype(
        brain_float
    )
    slot_grads = (
        (gate_weights[:, :, None] * grad_output[:, None, :])
        .astype(brain_float)
        .reshape(count_of_rows * TOP, D)
    )
    grad_buffer = jnp.zeros((EXPERTS * capacity, D), brain_float).at[slot_index].set(slot_grads)
    grad_buffer = grad_buffer.reshape(EXPERTS, capacity, D)
    grad_received = lax.all_to_all(grad_buffer, "expert", split_axis=0, concat_axis=1, tiled=True)
    grad_activation = jnp.einsum(
        "erd,efd->erf", grad_received, w_down, preferred_element_type=single_float
    )
    grad_down = jnp.einsum(
        "erf,erd->efd", activation, grad_received, preferred_element_type=single_float
    )
    grad_gate_pre = (
        grad_activation * up_pre * sigmoid_gate * (1.0 + gate_pre * (1.0 - sigmoid_gate))
    ).astype(brain_float)
    grad_up_pre = (grad_activation * silu_gate).astype(brain_float)
    grad_inputs = (
        jnp.einsum("erf,edf->erd", grad_gate_pre, w_gate, preferred_element_type=single_float)
        + jnp.einsum("erf,edf->erd", grad_up_pre, w_up, preferred_element_type=single_float)
    ).astype(brain_float)
    grad_gate = jnp.einsum(
        "erd,erf->edf", received, grad_gate_pre, preferred_element_type=single_float
    )
    grad_up = jnp.einsum("erd,erf->edf", received, grad_up_pre, preferred_element_type=single_float)
    grad_returned = lax.all_to_all(grad_inputs, "expert", split_axis=1, concat_axis=0, tiled=True)
    grad_picked = grad_returned.reshape(EXPERTS * capacity, D)[slot_index].reshape(
        count_of_rows, TOP, D
    )
    grad_second = jnp.sum(grad_picked, axis=1, dtype=single_float)
    grad_second = grad_second + jnp.dot(
        grad_logits, router_weight.T, preferred_element_type=single_float
    )
    grad_router = jnp.dot(second_norm.T, grad_logits, preferred_element_type=single_float)
    scaled_two = grad_second * gain_two
    grad_gain2 = jnp.sum(grad_second * unit_two, axis=0)
    grad_residual = grad_output + inverse_two * (
        scaled_two - unit_two * jnp.mean(scaled_two * unit_two, axis=-1, keepdims=True)
    )
    grad_attn = grad_residual.astype(brain_float)
    grad_out = jnp.dot(mixed_low.T, grad_attn, preferred_element_type=single_float)
    mixed_gradient = jnp.dot(grad_attn, out_weight.T, preferred_element_type=single_float).astype(
        brain_float
    )
    head_gradient = mixed_gradient.reshape(
        count_of_rows, KEY_VALUE_HEADS, group_of_heads, HEAD_DIMENSION
    )
    delta = jnp.einsum(
        "qhgd,hgqd->hgq", head_gradient, mixed_f32, preferred_element_type=single_float
    )
    key_again, value_again = (
        lax.all_gather(local_keys, "expert", axis=0, tiled=True),
        lax.all_gather(local_values, "expert", axis=0, tiled=True),
    )

    def key_block(grad_query_acc, block_number):
        first_key = block_number * count_of_rows
        key_portion = lax.dynamic_slice_in_dim(key_again, first_key, count_of_rows, 0).reshape(
            count_of_rows, KEY_VALUE_HEADS, HEAD_DIMENSION
        )
        value_portion = lax.dynamic_slice_in_dim(value_again, first_key, count_of_rows, 0).reshape(
            count_of_rows, KEY_VALUE_HEADS, HEAD_DIMENSION
        )
        accum = grad_query_acc
        scores = (
            jnp.einsum(
                "qhgd,khd->hgqk", query_rows, key_portion, preferred_element_type=single_float
            )
            * score_scale
        )
        columns = first_key + jnp.arange(count_of_rows, dtype=jnp.int32)
        allowed = (columns[None, :] <= positions[:, None]) & (columns[None, :] < length)
        masked = jnp.where(allowed, scores, NEGATIVE_LARGE)
        probability = jnp.where(allowed, jnp.exp(masked - log_total[..., None]), 0.0)
        grad_prob = jnp.einsum(
            "qhgd,khd->hgqk", head_gradient, value_portion, preferred_element_type=single_float
        )
        grad_scores = (probability * (grad_prob - delta[..., None])).astype(brain_float)
        accum = accum + jnp.einsum(
            "hgqk,khd->hgqd", grad_scores, key_portion, preferred_element_type=single_float
        )
        key_gradient_rows = jnp.einsum(
            "hgqk,qhgd->khd", grad_scores, query_rows, preferred_element_type=single_float
        )
        value_gradient_rows = jnp.einsum(
            "hgqk,qhgd->khd",
            probability.astype(brain_float),
            head_gradient,
            preferred_element_type=single_float,
        )
        accum, key_gradient_rows, value_gradient_rows = (
            accum,
            key_gradient_rows.reshape(count_of_rows, KEY_VALUE_HEADS * HEAD_DIMENSION),
            value_gradient_rows.reshape(count_of_rows, KEY_VALUE_HEADS * HEAD_DIMENSION),
        )
        return (accum, (key_gradient_rows, value_gradient_rows))

    grad_query_acc, (key_contributions, value_contributions) = lax.scan(
        key_block,
        jnp.zeros((KEY_VALUE_HEADS, group_of_heads, count_of_rows, HEAD_DIMENSION), single_float),
        jnp.arange(devices_here, dtype=jnp.int32),
    )
    own_key_gradient, grad_value_own = (
        lax.psum_scatter(
            key_contributions.reshape(sequence_tokens, KEY_VALUE_HEADS * HEAD_DIMENSION).astype(
                jnp.bfloat16
            ),
            "expert",
            scatter_dimension=0,
            tiled=True,
        ).astype(jnp.float32),
        lax.psum_scatter(
            value_contributions.reshape(sequence_tokens, KEY_VALUE_HEADS * HEAD_DIMENSION).astype(
                jnp.bfloat16
            ),
            "expert",
            scatter_dimension=0,
            tiled=True,
        ).astype(jnp.float32),
    )
    grad_query_rows = (
        jnp.transpose(grad_query_acc, (2, 0, 1, 3)).reshape(
            count_of_rows, QUERY_HEADS, HEAD_DIMENSION
        )
        * score_scale
    )
    grad_query_pre = (
        apply_rotation(grad_query_rows, cosine_lookup, -sine_lookup)
        .reshape(count_of_rows, QUERY_HEADS * HEAD_DIMENSION)
        .astype(brain_float)
    )
    unrotated_key_gradient = apply_rotation(
        own_key_gradient.reshape(count_of_rows, KEY_VALUE_HEADS, HEAD_DIMENSION) * score_scale,
        cosine_lookup,
        -sine_lookup,
    )
    unrotated_key_gradient = unrotated_key_gradient.reshape(
        count_of_rows, KEY_VALUE_HEADS * HEAD_DIMENSION
    ).astype(brain_float)
    grad_value_pre = grad_value_own.astype(brain_float)
    grad_query = jnp.dot(pre_attention_norm.T, grad_query_pre, preferred_element_type=single_float)
    grad_key = jnp.dot(
        pre_attention_norm.T, unrotated_key_gradient, preferred_element_type=single_float
    )
    grad_value = jnp.dot(pre_attention_norm.T, grad_value_pre, preferred_element_type=single_float)
    grad_first = (
        jnp.dot(grad_query_pre, query_weight.T, preferred_element_type=single_float)
        + jnp.dot(unrotated_key_gradient, key_weight.T, preferred_element_type=single_float)
        + jnp.dot(grad_value_pre, value_weight.T, preferred_element_type=single_float)
    )
    scaled_one = grad_first * gain_one
    grad_gain1 = jnp.sum(grad_first * unit_one, axis=0)
    grad_tokens = grad_residual + inverse_one * (
        scaled_one - unit_one * jnp.mean(scaled_one * unit_one, axis=-1, keepdims=True)
    )
    share_gain1, share_query, share_key, share_value, share_out, share_gain2, share_router = (
        lax.psum_scatter(
            grad_gain1.astype(jnp.bfloat16), "expert", scatter_dimension=0, tiled=True
        ).astype(jnp.float32),
        lax.psum_scatter(
            grad_query.astype(jnp.bfloat16), "expert", scatter_dimension=0, tiled=True
        ).astype(jnp.float32),
        lax.psum_scatter(
            grad_key.astype(jnp.bfloat16), "expert", scatter_dimension=0, tiled=True
        ).astype(jnp.float32),
        lax.psum_scatter(
            grad_value.astype(jnp.bfloat16), "expert", scatter_dimension=0, tiled=True
        ).astype(jnp.float32),
        lax.psum_scatter(
            grad_out.astype(jnp.bfloat16), "expert", scatter_dimension=0, tiled=True
        ).astype(jnp.float32),
        lax.psum_scatter(
            grad_gain2.astype(jnp.bfloat16), "expert", scatter_dimension=0, tiled=True
        ).astype(jnp.float32),
        lax.psum_scatter(
            grad_router.astype(jnp.bfloat16), "expert", scatter_dimension=0, tiled=True
        ).astype(jnp.float32),
    )
    share_gain1, share_query, share_key, share_value, share_out, share_gain2, share_router = (
        lax.psum(share_gain1.astype(jnp.bfloat16), "group").astype(jnp.float32),
        lax.psum(share_query.astype(jnp.bfloat16), "group").astype(jnp.float32),
        lax.psum(share_key.astype(jnp.bfloat16), "group").astype(jnp.float32),
        lax.psum(share_value.astype(jnp.bfloat16), "group").astype(jnp.float32),
        lax.psum(share_out.astype(jnp.bfloat16), "group").astype(jnp.float32),
        lax.psum(share_gain2.astype(jnp.bfloat16), "group").astype(jnp.float32),
        lax.psum(share_router.astype(jnp.bfloat16), "group").astype(jnp.float32),
    )
    part_gate, part_up, part_down = (
        lax.psum_scatter(
            grad_gate.astype(jnp.bfloat16), "group", scatter_dimension=1, tiled=True
        ).astype(jnp.float32),
        lax.psum_scatter(
            grad_up.astype(jnp.bfloat16), "group", scatter_dimension=1, tiled=True
        ).astype(jnp.float32),
        lax.psum_scatter(
            grad_down.astype(jnp.bfloat16), "group", scatter_dimension=2, tiled=True
        ).astype(jnp.float32),
    )
    whole_gate, whole_up, whole_down = (
        lax.all_gather(part_gate.astype(jnp.bfloat16), "group", axis=1, tiled=True).astype(
            part_gate.dtype
        ),
        lax.all_gather(part_up.astype(jnp.bfloat16), "group", axis=1, tiled=True).astype(
            part_up.dtype
        ),
        lax.all_gather(part_down.astype(jnp.bfloat16), "group", axis=2, tiled=True).astype(
            part_down.dtype
        ),
    )
    return (
        mixed,
        grad_tokens,
        share_gain1,
        share_query,
        share_key,
        share_value,
        share_out,
        share_gain2,
        share_router,
        whole_gate,
        whole_up,
        whole_down,
    )


def solution(mesh):
    return jax.shard_map(
        per_device,
        mesh=mesh,
        in_specs=(
            P(("group", "expert"), None),
            P("group"),
            P(("group", "expert"), None),
            P("expert"),
            P("expert", None),
            P("expert", None),
            P("expert", None),
            P("expert", None),
            P("expert"),
            P("expert", None),
            P("expert", None, None),
            P("expert", None, None),
            P("expert", None, None),
            P(("group", "expert"), None),
        ),
        out_specs=(
            P(("group", "expert"), None),
            P(("group", "expert"), None),
            P("expert"),
            P("expert", None),
            P("expert", None),
            P("expert", None),
            P("expert", None),
            P("expert"),
            P("expert", None),
            P("expert", None, None),
            P("expert", None, None),
            P("expert", None, None),
        ),
        check_vma=False,
    )
```

profile of v0, /device:TPU:0, one launch (start us, length us, event | category | flops | bytes accessed | tf_op | source)
XLA Modules:
  0.0 1736.9 jit_solution(3671113527267333503)
XLA Ops:
  24.9 15.5 all-gather.12.cloned.1.call-done
  43.2 26.1 %all-gather.18.cloned.1.call-done = bf16[1024,512]{1,0:T(8,128)(2,1)} async-done(((bf16[256,512]{1,0:T(8,128)(2,1)}), bf16[1024,512]{1,0:T(8,128)(2,1)}) %all-gather.18.cloned.1.call-update) | async-done | bytes 1048592 | tf_op jit(solution)/shard_map/all_gather | solution.py:67
  93.5 22.5 %all-gather.16.cloned.1.call-done = bf16[1024,1024]{1,0:T(8,128)(2,1)} async-done(((bf16[256,1024]{1,0:T(8,128)(2,1)}), bf16[1024,1024]{1,0:T(8,128)(2,1)}) %all-gather.16.cloned.1.call-update) | async-done | bytes 2097168 | tf_op jit(solution)/shard_map/all_gather | solution.py:65
  118.7 28.0 %all-gather.14.cloned.1.call-done = bf16[1024,512]{0,1:T(8,128)(2,1)} async-done(((bf16[256,512]{0,1:T(8,128)(2,1)}), bf16[1024,512]{0,1:T(8,128)(2,1)}) %all-gather.14.cloned.1.call-update) | async-done | bytes 1048592 | tf_op jit(solution)/shard_map/all_gather | solution.py:95
  155.6 19.4 %all-gather.20.cloned.1.call-done = bf16[1024,512]{1,0:T(8,128)(2,1)} async-done(((bf16[256,512]{1,0:T(8,128)(2,1)}), bf16[1024,512]{1,0:T(8,128)(2,1)}) %all-gather.20.cloned.1.call-update) | async-done | bytes 1048592 | tf_op jit(solution)/shard_map/all_gather | solution.py:98
  192.7 28.8 %all-gather.22.cloned.1.call-done = bf16[1024,1024]{1,0:T(8,128)(2,1)} async-done(((bf16[256,1024]{1,0:T(8,128)(2,1)}), bf16[1024,1024]{1,0:T(8,128)(2,1)}) %all-gather.22.cloned.1.call-update) | async-done | bytes 2097168 | tf_op jit(solution)/shard_map/all_gather | solution.py:68
  238.8 145.2 %all_to_all.66 = bf16[32,96,1024]{2,1,0:T(8,128)(2,1)} all-to-all(bf16[32,96,1024]{2,1,0:T(8,128)(2,1)} %bitcast.277), channel_id=1, replica_groups=mesh['group'=8,'expert'=4] {'expert'}, dimensions={0} | all-to-all | bytes 12582912 | tf_op jit(solution)/shard_map/all_to_all | solution.py:146
  423.4 143.3 %all_gather.46 = bf16[1024,32]{0,1:T(8,128)(2,1)S(1)} all-gather(bf16[256,32]{0,1:T(8,128)(2,1)S(1)} %copy-done.39), channel_id=1, replica_groups=mesh['group'=8,'expert'=4] {'expert'}, dimensions={0}, use_global_device_ids=true | all-gather | bytes 81920 | tf_op jit(solution)/shard_map/all_gather | solution.py:70
  610.8 139.6 %all_to_all.67 = bf16[32,96,1024]{2,1,0:T(8,128)(2,1)S(1)} all-to-all(bf16[32,96,1024]{2,1,0:T(8,128)(2,1)} %bitcast.274), channel_id=1, replica_groups=mesh['group'=8,'expert'=4] {'expert'}, dimensions={0} | all-to-all | bytes 12582912 | tf_op jit(solution)/shard_map/all_to_all | solution.py:175
  811.8 131.5 %all-to-all-done.3 = bf16[8,384,1024]{2,0,1:T(8,128)(2,1)} async-done(((bf16[8,384,1024]{2,0,1:T(8,128)(2,1)}), bf16[8,384,1024]{2,0,1:T(8,128)(2,1)}, u32[]{:S(2)}, u32[]{:S(2)}) %all-to-all-start.3) | async-done | bytes 6291488 | tf_op jit(solution)/shard_map/all_to_all | solution.py:194
  977.7 61.1 %while.15 = (s32[]{:T(128)}, f32[8,2,256,64]{2,3,1,0:T(8,128)}, bf16[4,256,512]{2,1,0:T(8,128)(2,1)}, bf16[4,256,512]{2,1,0:T(8,128)(2,1)}, s32[4]{0:T(128)S(1)}...) while((s32[]{:T(128)}, f32[8,2,256,64]{2,3,1,0:T(8,128)}, ...), condition=%wide.region_17.18_spmd.clone, body=%wide.region_16.17_spmd.clone.sunk | while | flops 684327936 | bytes 44552992 | solution.py:266
  1046.0 19.4 %reduce-scatter.13.cloned.1.call-done = bf16[256,512]{1,0:T(8,128)(2,1)} async-done(((bf16[1024,512]{1,0:T(8,128)(2,1)}), bf16[256,512]{1,0:T(8,128)(2,1)}) %reduce-scatter.13.cloned.1.call-update) | async-done | bytes 262160 | tf_op jit(solution)/shard_map/reduce_scatter | solution.py:272
  1068.3 25.2 %reduce-scatter.15.cloned.1.call-done = bf16[256,512]{1,0:T(8,128)(2,1)} async-done(((bf16[1024,512]{1,0:T(8,128)(2,1)}), bf16[256,512]{1,0:T(8,128)(2,1)}) %reduce-scatter.15.cloned.1.call-update) | async-done | bytes 262160 | tf_op jit(solution)/shard_map/reduce_scatter | solution.py:280
  1158.9 24.1 %reduce-scatter.23.cloned.1.call-done = bf16[256,1024]{1,0:T(8,128)(2,1)} async-done(((bf16[1024,1024]{1,0:T(8,128)(2,1)}), bf16[256,1024]{1,0:T(8,128)(2,1)}) %reduce-scatter.23.cloned.1.call-update) | async-done | bytes 524304 | tf_op jit(solution)/shard_map/reduce_scatter | solution.py:337
  1183.0 29.4 %reduce-scatter.19.cloned.1.call-done = bf16[256,512]{1,0:T(8,128)(2,1)} async-done(((bf16[1024,512]{1,0:T(8,128)(2,1)}), bf16[256,512]{1,0:T(8,128)(2,1)}) %reduce-scatter.19.cloned.1.call-update) | async-done | bytes 262160 | tf_op jit(solution)/shard_map/reduce_scatter | solution.py:331
  1212.4 28.5 %reduce-scatter.21.cloned.1.call-done = bf16[256,512]{1,0:T(8,128)(2,1)} async-done(((bf16[1024,512]{1,0:T(8,128)(2,1)}), bf16[256,512]{1,0:T(8,128)(2,1)}) %reduce-scatter.21.cloned.1.call-update) | async-done | bytes 262160 | tf_op jit(solution)/shard_map/reduce_scatter | solution.py:334
  1241.0 73.9 %reduce-scatter.27.cloned.1.call-done = bf16[8,128,512]{2,1,0:T(8,128)(2,1)} async-done(((bf16[8,1024,512]{2,1,0:T(8,128)(2,1)}), bf16[8,128,512]{2,1,0:T(8,128)(2,1)}) %reduce-scatter.27.cloned.1.call-update) | async-done | bytes 1048592 | tf_op jit(solution)/shard_map/reduce_scatter | solution.py:357
  1314.9 75.2 %reduce-scatter.29.cloned.1.call-done = bf16[8,128,512]{2,1,0:T(8,128)(2,1)} async-done(((bf16[8,1024,512]{2,1,0:T(8,128)(2,1)}), bf16[8,128,512]{2,1,0:T(8,128)(2,1)}) %reduce-scatter.29.cloned.1.call-update) | async-done | bytes 1048592 | tf_op jit(solution)/shard_map/reduce_scatter | solution.py:360
  1390.4 75.1 %reduce-scatter.31.cloned.1.call-done = bf16[128,4096]{1,0:T(8,128)(2,1)} async-done(((bf16[1024,4096]{1,0:T(8,128)(2,1)}), bf16[128,4096]{1,0:T(8,128)(2,1)}) %reduce-scatter.31.cloned.1.call-update) | async-done | bytes 1048592
  1489.9 23.1 %all-reduce.2 = (bf16[256]{0:T(256)(128)(2,1)S(1)}, bf16[256]{0:T(256)(128)(2,1)S(1)}, bf16[256,32]{0,1:T(8,128)(2,1)S(1)}) all-reduce(bf16[256]{0:T(256)(128)(2,1)S(1)} %dynamic-slice.1, bf16[256]{0:T(256)(128)(2,1)S(1)} %dynamic-slice.3, ...), channel_id=1, replica_groups=mesh['group'=8,'expert'=4] {'group'}, use_global_device_ids=true, to_apply=%region_23.24 | all-reduce | flops 8704 | bytes 34816 | tf_op jit(solution)/shard_map/psum | solution.py:348
  1516.0 32.3 %all-reduce.7.cloned.1.call-done = (bf16[256,1024]{1,0:T(8,128)(2,1)}, bf16[256,512]{1,0:T(8,128)(2,1)}, bf16[256,512]{1,0:T(8,128)(2,1)}, bf16[256,1024]{1,0:T(8,128)(2,1)}) async-done(((bf16[256,1024]{1,0:T(8,128)(2,1)}, bf16[256,512]{1,0:T(8,128)(2,1)}, bf16[256,512]{1,0:T(8,128)(2,1)}, bf16[256,1024]{1,0:T(8,128)(2,1)}), (bf16[256,1024]{1,0:T(8,128)(2,1)}, bf16[256,512]{1,0:T(8,128)(2,1)}, ...) | async-done | bytes 1572880 | tf_op jit(solution)/shard_map/psum | solution.py:349
  1556.2 47.5 %all-gather.24.cloned.1.call-done = bf16[8,1024,512]{2,1,0:T(8,128)(2,1)} async-done(((bf16[8,128,512]{2,1,0:T(8,128)(2,1)}), bf16[8,1024,512]{2,1,0:T(8,128)(2,1)}) %all-gather.24.cloned.1.call-update) | async-done | bytes 8388624 | tf_op jit(solution)/shard_map/all_gather | solution.py:368
  1616.0 43.9 %all-gather.26.cloned.1.call-done = bf16[8,1024,512]{2,1,0:T(8,128)(2,1)} async-done(((bf16[8,128,512]{2,1,0:T(8,128)(2,1)}), bf16[8,1024,512]{2,1,0:T(8,128)(2,1)}) %all-gather.26.cloned.1.call-update) | async-done | bytes 8388624 | tf_op jit(solution)/shard_map/all_gather | solution.py:371
  1672.1 46.0 %all-gather.28.cloned.1.call-done = bf16[8,512,1024]{2,1,0:T(8,128)(2,1)} async-done(((bf16[8,512,128]{2,1,0:T(8,128)(2,1)}), bf16[8,512,1024]{2,1,0:T(8,128)(2,1)}) %all-gather.28.cloned.1.call-update) | async-done | bytes 8388624 | tf_op jit(solution)/shard_map/all_gather | solution.py:374
  (326 shorter events, 473.9 us)
Async XLA Ops:
  7.2 33.1 %all-gather.12.cloned.1.call-start = ((), (), s32[]{:S(2)}) async-start(), calls=%async_computation.14 | async-start | bytes 1310720 | tf_op jit(solution)/shard_map/all_gather | solution.py:66
  7.9 61.3 %all-gather.18.cloned.1.call-start = ((), (), s32[]{:S(2)}) async-start(), calls=%async_computation.17 | async-start | bytes 1310720 | tf_op jit(solution)/shard_map/all_gather | solution.py:67
  8.7 107.2 %all-gather.16.cloned.1.call-start = ((), (), s32[]{:S(2)}) async-start(), calls=%async_computation.16 | async-start | bytes 2621440 | tf_op jit(solution)/shard_map/all_gather | solution.py:65
  9.4 137.3 %all-gather.14.cloned.1.call-start = ((), (), s32[]{:S(2)}) async-start(), calls=%async_computation.15 | async-start | bytes 1310720 | tf_op jit(solution)/shard_map/all_gather | solution.py:95
  43.1 131.9 %all-gather.20.cloned.1.call-start = ((), (), s32[]{:S(2)}) async-start(), calls=%async_computation.18 | async-start | bytes 1310720 | tf_op jit(solution)/shard_map/all_gather | solution.py:98
  71.9 149.6 %all-gather.22.cloned.1.call-start = ((), (), s32[]{:S(2)}) async-start(), calls=%async_computation.19 | async-start | bytes 2621440 | tf_op jit(solution)/shard_map/all_gather | solution.py:68
  225.0 342.0 %copy-start.12 = (bf16[256,1024]{1,0:T(8,128)(2,1)}, bf16[256,1024]{1,0:T(8,128)(2,1)S(1)}, u32[]{:S(2)}) copy-start(bf16[256,1024]{1,0:T(8,128)(2,1)S(1)} %multiply_convert_fusion.3) | copy-start | bytes 1572868
  418.1 149.4 %all-to-all-start.1 = ((bf16[8,384,1024]{2,0,1:T(8,128)(2,1)}), bf16[8,384,1024]{2,0,1:T(8,128)(2,1)}, u32[]{:S(2)}, u32[]{:S(2)}) async-start(bf16[8,384,1024]{2,0,1:T(8,128)(2,1)} %copy.112), calls=%async_computation.1 | async-start | bytes 12582912 | tf_op jit(solution)/shard_map/all_to_all | solution.py:155
  801.5 141.8 %all-to-all-start.3 = ((bf16[8,384,1024]{2,0,1:T(8,128)(2,1)}), bf16[8,384,1024]{2,0,1:T(8,128)(2,1)}, u32[]{:S(2)}, u32[]{:S(2)}) async-start(bf16[8,384,1024]{2,0,1:T(8,128)(2,1)} %copy.116), calls=%async_computation.3 | async-start | bytes 12582912 | tf_op jit(solution)/shard_map/all_to_all | solution.py:194
  806.8 258.5 %reduce-scatter.13.cloned.1.call-start = ((), (), s32[]{:S(2)}) async-start(), calls=%async_computation.20 | async-start | bytes 1310720 | tf_op jit(solution)/shard_map/reduce_scatter | solution.py:272
  1038.9 54.6 %reduce-scatter.15.cloned.1.call-start = ((), (), s32[]{:S(2)}) async-start(), calls=%async_computation.21 | async-start | bytes 1310720 | tf_op jit(solution)/shard_map/reduce_scatter | solution.py:280
  1039.6 119.3 %reduce-scatter.17.cloned.1.call-start = ((), (), s32[]{:S(2)}) async-start(), calls=%async_computation.22 | async-start | bytes 2621440 | tf_op jit(solution)/shard_map/reduce_scatter | solution.py:328
  1043.4 139.5 %reduce-scatter.23.cloned.1.call-start = ((), (), s32[]{:S(2)}) async-start(), calls=%async_computation.25 | async-start | bytes 2621440 | tf_op jit(solution)/shard_map/reduce_scatter | solution.py:337
  1046.0 166.4 %reduce-scatter.19.cloned.1.call-start = ((), (), s32[]{:S(2)}) async-start(), calls=%async_computation.23 | async-start | bytes 1310720 | tf_op jit(solution)/shard_map/reduce_scatter | solution.py:331
  1068.3 172.6 %reduce-scatter.21.cloned.1.call-start = ((), (), s32[]{:S(2)}) async-start(), calls=%async_computation.24 | async-start | bytes 1310720 | tf_op jit(solution)/shard_map/reduce_scatter | solution.py:334
  1096.0 218.8 %reduce-scatter.27.cloned.1.call-start = ((), (), s32[]{:S(2)}) async-start(), calls=%async_computation.27 | async-start | bytes 9437184 | tf_op jit(solution)/shard_map/reduce_scatter | solution.py:357
  1107.7 282.4 %reduce-scatter.29.cloned.1.call-start = ((), (), s32[]{:S(2)}) async-start(), calls=%async_computation.29 | async-start | bytes 9437184 | tf_op jit(solution)/shard_map/reduce_scatter | solution.py:360
  1119.5 346.0 %reduce-scatter.31.cloned.1.call-start = ((), (), s32[]{:S(2)}) async-start(), calls=%async_computation.32 | async-start | bytes 9437184
  1157.0 313.9 %copy-start.41 = (u32[32]{0:T(128)S(1)}, u32[32]{0:T(128)}, u32[]{:S(2)}) copy-start(u32[32]{0:T(128)} %constant.74) | copy-start | bytes 388
  1157.0 332.9 %reduce-scatter.25.cloned.1.call-start = ((), (), s32[]{:S(2)}) async-start(), calls=%async_computation.26 | async-start | bytes 81920 | tf_op jit(solution)/shard_map/reduce_scatter | solution.py:343
  1158.8 389.5 %all-reduce.7.cloned.1.call-start = ((), (), s32[]{:S(2)}) async-start(), calls=%async_computation.33 | async-start | bytes 3145728 | tf_op jit(solution)/shard_map/psum | solution.py:349
  1240.9 362.8 %all-gather.24.cloned.1.call-start = ((), (), s32[]{:S(2)}) async-start(), calls=%async_computation.28 | async-start | bytes 9437184 | tf_op jit(solution)/shard_map/all_gather | solution.py:368
  1314.9 345.0 %all-gather.26.cloned.1.call-start = ((), (), s32[]{:S(2)}) async-start(), calls=%async_computation.30 | async-start | bytes 9437184 | tf_op jit(solution)/shard_map/all_gather | solution.py:371
  1390.2 327.9 %all-gather.28.cloned.1.call-start = ((), (), s32[]{:S(2)}) async-start(), calls=%async_computation.31 | async-start | bytes 9437184 | tf_op jit(solution)/shard_map/all_gather | solution.py:374
  (45 other events, 1655.5 us)
Sparse Core Ops, SparseCore 0:
  9.6 30.6 all-gather.11
  41.9 27.3 all-gather.17
  70.9 45.0 all-gather.15
  117.9 28.7 all-gather.13
  148.7 26.2 all-gather.19
  176.4 45.0 all-gather.21
  1039.0 26.3 reduce-scatter.12
  1067.7 25.7 reduce-scatter.14
  1095.8 42.1 reduce-scatter.16
  1140.1 42.8 reduce-scatter.22
  1185.8 26.4 reduce-scatter.18
  1215.1 25.7 reduce-scatter.20
  1244.9 69.8 reduce-scatter.26
  1318.7 71.3 reduce-scatter.28
  1394.0 71.4 reduce-scatter.30
  1468.2 19.3 reduce-scatter.24
  1491.0 57.2 all-reduce.6
  1550.1 53.5 all-gather.23
  1605.6 54.2 all-gather.25
  1662.2 55.8 all-gather.27
where the time goes:
time: 1750 us; the launch traced here: 1740 us
  waiting for transfers between devices  796 us (45%)
  blocking collectives  485 us (28%)
  matrix products  185 us (11%)
  local copies, waits for them, and re-layouts  140 us (8%)
  other arithmetic  98.7 us (6%)
    all_to_all x1, blocking collectives, per_device(): lax.all_to_all(send_buffer, 'expert', split_axis=0, concat_axis=1, tiled=...  145 us
    all_gather x1, blocking collectives, per_device(): lax.all_gather(w_router, 'expert', axis=0, tiled=True)  143 us
    all_to_all x1, blocking collectives, per_device(): lax.all_to_all(grad_buffer, 'expert', split_axis=0, concat_axis=1, tiled=...  140 us
    all_to_all x1, waiting for transfers between devices, per_device(): lax.all_to_all(grad_inputs, 'expert', split_axis=1, concat_axis=0, tiled=...  131 us
    unnamed x21, waiting for transfers between devices  78.6 us
    reduce_scatter x1, waiting for transfers between devices, per_device(): lax.psum_scatter(grad_up.astype(jnp.bfloat16), 'group', scatter_dimension...  75.2 us
    reduce_scatter x1, waiting for transfers between devices, per_device(): lax.psum_scatter(grad_gate.astype(jnp.bfloat16), 'group', scatter_dimensi...  73.9 us
    all_gather x1, waiting for transfers between devices, per_device(): lax.all_gather(part_gate.astype(jnp.bfloat16), 'group', axis=1, tiled=True)  47.5 us
  transfers between devices with their start and end apart: 22, of which 19 were waited for; matrix products, arithmetic and copies ran while one was open for 10% of the time, Pallas kernels for 0%

commit v1 on v0

v1 whole, which is shorter than its diff:
```python
import functools

import jax
import jax.numpy as jnp
from jax import lax
from jax.experimental import pallas as pl
from jax.experimental.pallas import tpu as pltpu
from jax.sharding import PartitionSpec as P

D = 1024
QUERY_HEADS = 16
KEY_VALUE_HEADS = 8
HEAD_DIMENSION = 64
EXPERTS = 32
TOP = 8
FF = 512
LANES = 128

EPSILON = 1e-05
NEGATIVE_LARGE = -1e30
BF = jnp.bfloat16
F32 = jnp.float32


def rotary_tables(positions, head_size):
    half_width = head_size // 2
    frequency = 10000.0 ** (-2.0 * jnp.arange(half_width).astype(F32) / head_size)
    angles = positions.astype(F32)[:, None] * frequency[None, :]
    return (jnp.cos(angles)[:, None, :], jnp.sin(angles)[:, None, :])


def apply_rotation(tensor_in, cosine_lookup, sine_lookup):
    half_width = tensor_in.shape[-1] // 2
    first_half = tensor_in[..., :half_width]
    second_half = tensor_in[..., half_width:]
    return jnp.concatenate(
        [
            first_half * cosine_lookup - second_half * sine_lookup,
            second_half * cosine_lookup + first_half * sine_lookup,
        ],
        axis=-1,
    )


def dot(a, b):
    return jnp.dot(a, b, preferred_element_type=F32)


def dot_nt(a, b):
    return lax.dot_general(a, b, (((1,), (1,)), ((), ())), preferred_element_type=F32)


def dot_tn(a, b):
    return lax.dot_general(a, b, (((0,), (0,)), ((), ())), preferred_element_type=F32)


def expert_kernel(
    sizes,
    x_ref,
    ct_ref,
    router_t_ref,
    rank_row_ref,
    rank_col_ref,
    w_gate_ref,
    w_up_ref,
    w_down_ref,
    y_ref,
    gs_ref,
    grad_gate_ref,
    grad_up_ref,
    grad_down_ref,
    xs_ref,
    g_ref,
    gate_slot_ref,
    dots_ref,
):
    blocks, rows, local, capacity = sizes
    slots = local * capacity
    step = pl.program_id(0)
    base = lax.axis_index("expert") * local

    @pl.when(step == 0)
    def _():
        logits = dot_nt(router_t_ref[...], x_ref[...])
        hot = rank_row_ref[...] < 200.0
        top = jnp.max(jnp.where(hot, logits, NEGATIVE_LARGE), axis=0, keepdims=True)
        weight = jnp.where(hot, jnp.exp(jnp.minimum(logits - top, 0.0)), 0.0)
        gates = weight / jnp.sum(weight, axis=0, keepdims=True)
        expert_id = lax.broadcasted_iota(jnp.int32, gates.shape, 0)
        slot_id = lax.broadcasted_iota(jnp.int32, (capacity, rows), 0).astype(F32)
        rank_rows, gate_rows = [], []
        for e in range(local):
            mine = expert_id == base + e
            rank_rows.append(jnp.sum(jnp.where(mine, rank_row_ref[...], 0.0), 0, keepdims=True))
            gate_rows.append(jnp.sum(jnp.where(mine, gates, 0.0), 0, keepdims=True))
        for b in range(blocks):
            here = slice(b * rows, (b + 1) * rows)
            pieces = []
            for e in range(local):
                taken = jnp.broadcast_to(rank_rows[e][:, here], (capacity, rows)) == slot_id
                gate = jnp.sum(jnp.where(taken, gate_rows[e][:, here], 0.0), 1, keepdims=True)
                gate_slot_ref[b, e * capacity : (e + 1) * capacity, :] = gate
                pieces.append(jnp.where(taken, 1.0, 0.0).astype(BF))
            pick = jnp.concatenate(pieces, axis=0)
            xs_ref[b] = dot(pick, x_ref[here, :]).astype(BF)
            g_ref[b] = dot(pick, ct_ref[here, :]).astype(BF)

    here = pl.ds(pl.multiple_of(step * capacity, capacity), capacity)
    xs = jnp.concatenate([xs_ref[b, here, :] for b in range(blocks)], axis=0)
    g = jnp.concatenate([g_ref[b, here, :] for b in range(blocks)], axis=0).astype(F32)
    gate_slot = jnp.concatenate([gate_slot_ref[b, here, :] for b in range(blocks)], axis=0)
    w_gate, w_up, w_down = w_gate_ref[0], w_up_ref[0], w_down_ref[0]
    gate_pre = dot(xs, w_gate)
    up_pre = dot(xs, w_up)
    sigmoid = jax.nn.sigmoid(gate_pre)
    silu = gate_pre * sigmoid
    activation = (silu * up_pre).astype(BF)
    expert_out = dot(activation, w_down).astype(BF).astype(F32)
    slot_dot = jnp.sum(g * expert_out, axis=1, keepdims=True)
    grad_out = (gate_slot * g).astype(BF)
    scaled_out = (gate_slot * expert_out).astype(BF)
    grad_down_ref[0] = dot_tn(activation, grad_out).astype(BF)
    grad_activation = dot_nt(grad_out, w_down)
    grad_gate_pre = (
        grad_activation * up_pre * sigmoid * (1.0 + gate_pre * (1.0 - sigmoid))
    ).astype(BF)
    grad_up_pre = (grad_activation * silu).astype(BF)
    grad_gate_ref[0] = dot_tn(xs, grad_gate_pre).astype(BF)
    grad_up_ref[0] = dot_tn(xs, grad_up_pre).astype(BF)
    grad_in = (dot_nt(grad_gate_pre, w_gate) + dot_nt(grad_up_pre, w_up)).astype(BF)
    lane = lax.broadcasted_iota(jnp.int32, (blocks * capacity, LANES), 1)
    high = slot_dot.astype(BF).astype(F32)
    middle = (slot_dot - high).astype(BF).astype(F32)
    low = slot_dot - high - middle
    mine = base + step
    dots = jnp.where(lane == mine, high, 0.0)
    dots = jnp.where(lane == mine + EXPERTS, middle, dots)
    dots = jnp.where(lane == mine + 2 * EXPERTS, low, dots).astype(BF)
    for b in range(blocks):
        part = slice(b * capacity, (b + 1) * capacity)
        xs_ref[b, here, :] = grad_in[part]
        g_ref[b, here, :] = scaled_out[part]
        dots_ref[b, here, :] = dots[part]

    @pl.when(step == local - 1)
    def _():
        slot_expert = lax.broadcasted_iota(jnp.int32, (EXPERTS, slots), 1) // capacity
        spread_row = lax.broadcasted_iota(jnp.int32, (EXPERTS, slots), 0)
        spread = jnp.where(spread_row == slot_expert + base, 1.0, 0.0).astype(BF)
        slot_rank = (lax.broadcasted_iota(jnp.int32, (rows, slots), 1) % capacity).astype(F32)
        for b in range(blocks):
            there = slice(b * rows, (b + 1) * rows)
            ranks = dot(rank_col_ref[there, :], spread)
            put = jnp.where(ranks == slot_rank, 1.0, 0.0).astype(BF)
            y_ref[there, :] = dot(put, g_ref[b]).astype(BF)
            gs_ref[there, :D] = dot(put, xs_ref[b]).astype(BF)
            gs_ref[there, D:] = dot(put, dots_ref[b]).astype(BF)


def run_experts(x_all, ct_all, router_t, rank_row, rank_col, w_gate, w_up, w_down, rows, capacity):
    total = x_all.shape[0]
    blocks, local = total // rows, w_gate.shape[0]
    slots = local * capacity
    sizes = (blocks, rows, local, capacity)
    whole = lambda shape: pl.BlockSpec(
        shape, lambda e: (0,) * len(shape), pipeline_mode=pl.Buffered(1)
    )
    per = lambda shape: pl.BlockSpec((1,) + shape, lambda e: (e, 0, 0))
    flops = 2 * total * D * slots * 4 // blocks + 18 * blocks * slots * D * FF
    return pl.pallas_call(
        functools.partial(expert_kernel, sizes),
        grid=(local,),
        out_shape=(
            jax.ShapeDtypeStruct((total, D), BF),
            jax.ShapeDtypeStruct((total, D + LANES), BF),
            jax.ShapeDtypeStruct((local, D, FF), BF),
            jax.ShapeDtypeStruct((local, D, FF), BF),
            jax.ShapeDtypeStruct((local, FF, D), BF),
        ),
        in_specs=[
            whole((total, D)),
            whole((total, D)),
            whole((EXPERTS, D)),
            whole((EXPERTS, total)),
            whole((total, EXPERTS)),
            per((D, FF)),
            per((D, FF)),
            per((FF, D)),
        ],
        out_specs=(
            whole((total, D)),
            whole((total, D + LANES)),
            per((D, FF)),
            per((D, FF)),
            per((FF, D)),
        ),
        scratch_shapes=[
            pltpu.VMEM((blocks, slots, D), BF),
            pltpu.VMEM((blocks, slots, D), BF),
            pltpu.VMEM((blocks, slots, 1), F32),
            pltpu.VMEM((blocks, slots, LANES), BF),
        ],
        compiler_params=pltpu.CompilerParams(
            dimension_semantics=("arbitrary",), vmem_limit_bytes=62 * 1024 * 1024
        ),
        cost_estimate=pl.CostEstimate(
            flops=flops, bytes_accessed=2 * (6 * local * D * FF + 4 * total * D), transcendentals=0
        ),
        name="experts",
    )(x_all, ct_all, router_t, rank_row, rank_col, w_gate, w_up, w_down)


def gather_rows(value):
    return lax.all_gather(value, "expert", axis=0, tiled=True)


def scatter_rows(value):
    return lax.psum_scatter(value, "expert", scatter_dimension=0, tiled=True)


def per_device(
    tokens,
    lengths,
    routes,
    norm_gain1,
    w_query,
    key_projection,
    value_projection,
    w_out,
    norm_gain2,
    w_router,
    w_gate,
    w_up,
    w_down,
    cotangent,
):
    rows = tokens.shape[0]
    my_index = lax.axis_index("expert")
    capacity = 3 * rows * TOP // (2 * EXPERTS)
    group_of_heads = QUERY_HEADS // KEY_VALUE_HEADS
    score_scale = HEAD_DIMENSION ** (-0.5)
    query_width, key_width = w_query.shape[1], key_projection.shape[1]
    length = lengths[0]
    positions = my_index * rows + jnp.arange(rows, dtype=jnp.int32)
    valid_rows = (positions < length)[:, None]
    grad_output = jnp.where(valid_rows, cotangent, jnp.zeros_like(cotangent))

    qkv_weight = gather_rows(jnp.concatenate([w_query, key_projection, value_projection], axis=1))
    small = jnp.concatenate([norm_gain1[:, None], norm_gain2[:, None], w_router], axis=1)
    small = gather_rows(small)
    gain_one = small[:, 0].astype(F32)
    gain_two = small[:, 1].astype(F32)
    router_weight = small[:, 2:]
    out_weight = gather_rows(w_out)

    expert_ids = jnp.arange(EXPERTS, dtype=jnp.int32)
    hot = jnp.any(routes[:, :, None] == expert_ids, axis=1)
    row_id = jnp.arange(rows, dtype=jnp.int32)
    earlier = (row_id[None, :] < row_id[:, None]).astype(BF)
    rank = jnp.where(hot, dot(earlier, hot.astype(BF)), 255.0).astype(BF)
    rank_all = gather_rows(rank)
    rank_row = rank_all.T.astype(F32)
    ct_all = gather_rows(grad_output)

    cosine_lookup, sine_lookup = rotary_tables(positions, HEAD_DIMENSION)
    token_f32 = tokens.astype(F32)
    inverse_one = lax.rsqrt(jnp.mean(token_f32 * token_f32, axis=-1, keepdims=True) + EPSILON)
    unit_one = token_f32 * inverse_one
    first_norm = (unit_one * gain_one).astype(BF)
    qkv = dot(first_norm, qkv_weight)
    query_pre = qkv[:, :query_width]
    unrotated_key = qkv[:, query_width : query_width + key_width]
    value_pre = qkv[:, query_width + key_width :]
    query_rows = apply_rotation(
        query_pre.reshape(rows, QUERY_HEADS, HEAD_DIMENSION), cosine_lookup, sine_lookup
    ).astype(BF)
    query_rows = query_rows.reshape(rows, KEY_VALUE_HEADS, group_of_heads, HEAD_DIMENSION)
    local_keys = apply_rotation(
        unrotated_key.reshape(rows, KEY_VALUE_HEADS, HEAD_DIMENSION), cosine_lookup, sine_lookup
    ).astype(BF)
    local_keys = local_keys.reshape(rows, key_width)
    kv_all = gather_rows(jnp.concatenate([local_keys, value_pre.astype(BF)], axis=1))
    key_portion = kv_all[:, :key_width].reshape(-1, KEY_VALUE_HEADS, HEAD_DIMENSION)
    value_portion = kv_all[:, key_width:].reshape(-1, KEY_VALUE_HEADS, HEAD_DIMENSION)
    key_count = kv_all.shape[0]
    scores = (
        jnp.einsum("qhgd,khd->hgqk", query_rows, key_portion, preferred_element_type=F32)
        * score_scale
    )
    columns = jnp.arange(key_count, dtype=jnp.int32)
    allowed = (columns[None, :] <= positions[:, None]) & (columns[None, :] < length)
    masked = jnp.where(allowed, scores, NEGATIVE_LARGE)
    maximum = jnp.max(masked, axis=-1)
    weights = jnp.where(allowed, jnp.exp(masked - maximum[..., None]), 0.0)
    total = jnp.sum(weights, axis=-1)
    mixed_f32 = (
        jnp.einsum(
            "hgqk,khd->hgqd", weights.astype(BF), value_portion, preferred_element_type=F32
        )
        / total[..., None]
    )
    log_total = maximum + jnp.log(total)
    mixed_low = jnp.transpose(mixed_f32, (2, 0, 1, 3)).reshape(rows, query_width).astype(BF)
    residual = token_f32 + dot(mixed_low, out_weight)
    inverse_two = lax.rsqrt(jnp.mean(residual * residual, axis=-1, keepdims=True) + EPSILON)
    unit_two = residual * inverse_two
    second_norm = (unit_two * gain_two).astype(BF)
    x_all = gather_rows(second_norm)

    y_part, gs_part, grad_gate, grad_up, grad_down = run_experts(
        x_all, ct_all, router_weight.T, rank_row, rank_all, w_gate, w_up, w_down, rows, capacity
    )
    gs = scatter_rows(gs_part).astype(F32)
    expert_sum = scatter_rows(y_part).astype(F32)
    mixed = (residual + expert_sum).astype(BF)

    logits = dot(second_norm, router_weight)
    chosen = jnp.where(hot, logits, NEGATIVE_LARGE)
    gate_weights = jnp.where(hot, jnp.exp(chosen - jnp.max(chosen, axis=-1, keepdims=True)), 0.0)
    gate_weights = gate_weights / jnp.sum(gate_weights, axis=-1, keepdims=True)
    grad_gates = gs[:, D : D + EXPERTS] + gs[:, D + EXPERTS : D + 2 * EXPERTS]
    grad_gates = grad_gates + gs[:, D + 2 * EXPERTS : D + 3 * EXPERTS]
    grad_logits = (
        gate_weights * (grad_gates - jnp.sum(gate_weights * grad_gates, axis=-1, keepdims=True))
    ).astype(BF)
    grad_second = gs[:, :D] + dot_nt(grad_logits, router_weight)
    grad_router = dot_tn(second_norm, grad_logits)
    scaled_two = grad_second * gain_two
    grad_gain2 = jnp.sum(grad_second * unit_two, axis=0)
    grad_residual = grad_output.astype(F32) + inverse_two * (
        scaled_two - unit_two * jnp.mean(scaled_two * unit_two, axis=-1, keepdims=True)
    )
    grad_attn = grad_residual.astype(BF)
    grad_out = dot_tn(mixed_low, grad_attn)
    mixed_gradient = dot_nt(grad_attn, out_weight).astype(BF)
    head_gradient = mixed_gradient.reshape(rows, KEY_VALUE_HEADS, group_of_heads, HEAD_DIMENSION)
    delta = jnp.einsum("qhgd,hgqd->hgq", head_gradient, mixed_f32, preferred_element_type=F32)
    probability = jnp.where(allowed, jnp.exp(masked - log_total[..., None]), 0.0)
    grad_prob = jnp.einsum(
        "qhgd,khd->hgqk", head_gradient, value_portion, preferred_element_type=F32
    )
    grad_scores = (probability * (grad_prob - delta[..., None])).astype(BF)
    grad_query_acc = jnp.einsum(
        "hgqk,khd->qhgd", grad_scores, key_portion, preferred_element_type=F32
    )
    key_gradient = jnp.einsum(
        "hgqk,qhgd->khd", grad_scores, query_rows, preferred_element_type=F32
    ).reshape(key_count, key_width)
    value_gradient = jnp.einsum(
        "hgqk,qhgd->khd", probability.astype(BF), head_gradient, preferred_element_type=F32
    ).reshape(key_count, key_width)
    kv_gradient = scatter_rows(
        jnp.concatenate([key_gradient.astype(BF), value_gradient.astype(BF)], axis=1)
    )
    own_key_gradient = kv_gradient[:, :key_width].astype(F32)
    grad_query_rows = grad_query_acc.reshape(rows, QUERY_HEADS, HEAD_DIMENSION) * score_scale
    grad_query_pre = (
        apply_rotation(grad_query_rows, cosine_lookup, -sine_lookup)
        .reshape(rows, query_width)
        .astype(BF)
    )
    grad_key_pre = apply_rotation(
        own_key_gradient.reshape(rows, KEY_VALUE_HEADS, HEAD_DIMENSION) * score_scale,
        cosine_lookup,
        -sine_lookup,
    )
    grad_key_pre = grad_key_pre.reshape(rows, key_width).astype(BF)
    grad_qkv_pre = jnp.concatenate(
        [grad_query_pre, grad_key_pre, kv_gradient[:, key_width:]], axis=1
    )
    grad_qkv = dot_tn(first_norm, grad_qkv_pre)
    grad_first = dot_nt(grad_qkv_pre, qkv_weight)
    scaled_one = grad_first * gain_one
    grad_gain1 = jnp.sum(grad_first * unit_one, axis=0)
    grad_tokens = grad_residual + inverse_one * (
        scaled_one - unit_one * jnp.mean(scaled_one * unit_one, axis=-1, keepdims=True)
    )
    grad_small = jnp.concatenate([grad_gain1[:, None], grad_gain2[:, None], grad_router], axis=1)

    share_qkv = lax.psum(scatter_rows(grad_qkv.astype(BF)), "group").astype(F32)
    share_out = lax.psum(scatter_rows(grad_out.astype(BF)), "group").astype(F32)
    share_small = lax.psum(scatter_rows(grad_small.astype(BF)), "group").astype(F32)

    def sum_over_groups(value, axis):
        part = lax.psum_scatter(value, "group", scatter_dimension=axis, tiled=True)
        return lax.all_gather(part, "group", axis=axis, tiled=True).astype(F32)

    return (
        mixed,
        grad_tokens,
        share_small[:, 0],
        share_qkv[:, :query_width],
        share_qkv[:, query_width : query_width + key_width],
        share_qkv[:, query_width + key_width :],
        share_out,
        share_small[:, 1],
        share_small[:, 2:],
        sum_over_groups(grad_gate, 1),
        sum_over_groups(grad_up, 1),
        sum_over_groups(grad_down, 1),
    )


def solution(mesh):
    rows = P(("group", "expert"), None)
    vector, matrix, stack = P("expert"), P("expert", None), P("expert", None, None)
    return jax.shard_map(
        per_device,
        mesh=mesh,
        in_specs=(
            rows,
            P("group"),
            rows,
            vector,
            matrix,
            matrix,
            matrix,
            matrix,
            vector,
            matrix,
            stack,
            stack,
            stack,
            rows,
        ),
        out_specs=(
            rows,
            rows,
            vector,
            matrix,
            matrix,
            matrix,
            matrix,
            vector,
            matrix,
            stack,
            stack,
            stack,
        ),
        check_vma=False,
    )
```

time: 1750 us -> 1130 us (0.65)
  blocking collectives: 485 us -> 54.5 us
  matrix products: 185 us -> 62.6 us
  local copies, waits for them, and re-layouts: 140 us -> 21.8 us
  Pallas kernels: 0 us -> 52.8 us
  waiting for transfers between devices: 796 us -> 846 us
  other arithmetic: 98.7 us -> 67.6 us
    all_to_all x2 -> x0, blocking collectives: 285 us -> none  [the longest x1 145 us: per_device(): lax.all_to_all(send_buffer, 'expert', split_axis=0, concat_axis=1, tiled=...]
    reduce_scatter x9, waiting for transfers between devices: 276 us -> 476 us  [the longest x6 250 us: scatter_rows(): return lax.psum_scatter(value, 'expert', scatter_dimension=0, tiled=True)]
    all_gather x3 -> x2, blocking collectives: 165 us -> 31.2 us  [gather_rows(): return lax.all_gather(value, 'expert', axis=0, tiled=True)]
    all_to_all x2 -> x0, waiting for transfers between devices: 131 us -> none  [the longest x1 131 us: per_device(): lax.all_to_all(grad_inputs, 'expert', split_axis=1, concat_axis=0, tiled=...]
    dot_general x47 -> x15, matrix products: 177 us -> 54.9 us  [the longest x1 8.67 us: per_device(): jnp.einsum('qhgd,khd->hgqk', head_gradient, value_portion, preferred_elem...]
    unnamed x21 -> x18, waiting for transfers between devices: 78.6 us -> 3.45 us
    all_gather x9 -> x8, waiting for transfers between devices: 277 us -> 331 us  [the longest x5 194 us: gather_rows(): return lax.all_gather(value, 'expert', axis=0, tiled=True)]
    pallas_call x0 -> x1, Pallas kernels: none -> 52.8 us  [run_experts(): pl.pallas_call(functools.partial(expert_kernel, sizes), grid=(local,), ou...]
  transfers between devices with their start and end apart: 22 -> 18, of which waited for: 19 -> 18; matrix products, arithmetic and copies ran while one was open for 10% -> 9% of each run, Pallas kernels for 0% -> 0%
where the time goes in v1:
time: 1130 us; the launch traced here: 1120 us
  waiting for transfers between devices  846 us (75%)
  other arithmetic  67.6 us (6%)
  matrix products  62.6 us (6%)
  blocking collectives  54.5 us (5%)
  Pallas kernels  52.8 us (5%)
  local copies, waits for them, and re-layouts  21.8 us (2%)
  between operations  16.1 us (1%)
    reduce_scatter x6, waiting for transfers between devices, scatter_rows(): return lax.psum_scatter(value, 'expert', scatter_dimension=0, tiled=True)  250 us
    reduce_scatter x3, waiting for transfers between devices, sum_over_groups(): part = lax.psum_scatter(value, 'group', scatter_dimension=axis, tiled=True)  226 us
    all_gather x5, waiting for transfers between devices, gather_rows(): return lax.all_gather(value, 'expert', axis=0, tiled=True)  194 us
    all_gather x3, waiting for transfers between devices, sum_over_groups(): return lax.all_gather(part, 'group', axis=axis, tiled=True).astype(F32)  136 us
    pallas_call x1, Pallas kernels, run_experts(): pl.pallas_call(functools.partial(expert_kernel, sizes), grid=(local,), ou...  52.8 us
    convert_element_type x3, other arithmetic, sum_over_groups(): return lax.all_gather(part, 'group', axis=axis, tiled=True).astype(F32)  36.4 us
    psum x1, waiting for transfers between devices, per_device(): share_qkv = lax.psum(scatter_rows(grad_qkv.astype(BF)), 'group').astype(F32)  36.1 us
    all_gather x2, blocking collectives, gather_rows(): return lax.all_gather(value, 'expert', axis=0, tiled=True)  31.2 us
  transfers between devices with their start and end apart: 18, of which 18 were waited for; matrix products, arithmetic and copies ran while one was open for 9% of the time, Pallas kernels for 0%

profile of v1, /device:TPU:0, one launch (start us, length us, event | category | flops | bytes accessed | tf_op | source)
XLA Modules:
  0.0 1123.1 jit_solution(10001577424445661086)
XLA Ops:
  11.7 15.0 %all_gather.30 = bf16[1024,34]{0,1:T(8,128)(2,1)S(1)} all-gather(bf16[256,34]{0,1:T(8,128)(2,1)S(1)} %pad_maximum_fusion.13), channel_id=1, replica_groups=mesh['group'=8,'expert'=4] {'expert'}, dimensions={0}, use_global_device_ids=true | all-gather | bytes 87040 | tf_op jit(solution)/shard_map/all_gather | solution.py:214
  28.8 65.0 %all-gather.9.cloned.1.call-done = bf16[1024,2048]{1,0:T(8,128)(2,1)} async-done(((bf16[256,2048]{1,0:T(8,128)(2,1)}), bf16[1024,2048]{1,0:T(8,128)(2,1)}) %all-gather.9.cloned.1.call-update) | async-done | bytes 4194320 | tf_op jit(solution)/shard_map/all_gather | solution.py:214
  104.8 39.8 %all-gather.11.cloned.1.call-done = bf16[1024,1024]{1,0:T(8,128)(2,1)} async-done(((bf16[256,1024]{1,0:T(8,128)(2,1)}), bf16[1024,1024]{1,0:T(8,128)(2,1)}) %all-gather.11.cloned.1.call-update) | async-done | bytes 2097168 | tf_op jit(solution)/shard_map/all_gather | solution.py:214
  174.9 15.7 %all-gather.13.cloned.1.call-done = bf16[1024,1024]{1,0:T(8,128)(2,1)} async-done(((bf16[256,1024]{1,0:T(8,128)(2,1)}), bf16[1024,1024]{1,0:T(8,128)(2,1)}) %all-gather.13.cloned.1.call-update) | async-done | bytes 2097168 | tf_op jit(solution)/shard_map/all_gather | solution.py:214
  194.5 16.2 %all_gather.36.rank_col_ref = bf16[1024,32]{1,0:T(8,128)(2,1)S(1)} all-gather(bf16[256,32]{1,0:T(8,128)(2,1)S(1)} %fusion.19), channel_id=1, replica_groups=mesh['group'=8,'expert'=4] {'expert'}, dimensions={0}, use_global_device_ids=true | all-gather | bytes 81920 | tf_op jit(solution)/shard_map/all_gather | solution.py:214
  212.2 27.2 %all-gather.17.cloned.1.call-done.ct_ref = bf16[1024,1024]{1,0:T(8,128)(2,1)} async-done(((bf16[256,1024]{1,0:T(8,128)(2,1)}), bf16[1024,1024]{1,0:T(8,128)(2,1)}) %all-gather.17.cloned.1.call-update) | async-done | bytes 2097168 | tf_op jit(solution)/shard_map/all_gather | solution.py:214
  239.5 46.5 %all-gather.15.cloned.1.call-done.x_ref = bf16[1024,1024]{1,0:T(8,128)(2,1)} async-done(((bf16[256,1024]{1,0:T(8,128)(2,1)}), bf16[1024,1024]{1,0:T(8,128)(2,1)}) %all-gather.15.cloned.1.call-update) | async-done | bytes 2097168 | tf_op jit(solution)/shard_map/all_gather | solution.py:214
  286.0 52.8 %experts.1 = (bf16[1024,1024]{1,0:T(8,128)(2,1)}, bf16[1024,1152]{1,0:T(8,128)(2,1)}, bf16[8,1024,512]{2,1,0:T(8,128)(2,1)}, bf16[8,1024,512]{2,1,0:T(8,128)(2,1)}, bf16[8,512,1024]{2,1,0:T(8,128)(2,1)}) custom-call(bf16[1024,1024]{1,0:T(8,128)(2,1)} %all-gather.15.cloned.1.call-done.x_ref, bf16[1024,1024]{1,0:T(8,128)(2,1)} %all-gather.17.cloned.1.call-done.ct_ref, ...), custom_call_target="tpu_custom_call" | custom-call | flops 30601641984 | bytes 58720256 | tf_op jit(solution)/shard_map/experts/pallas_call | solution.py:170
  342.1 43.4 %reduce-scatter.12.cloned.1.call-done = bf16[256,1152]{1,0:T(8,128)(2,1)} async-done(((bf16[1024,1152]{1,0:T(8,128)(2,1)}), bf16[256,1152]{1,0:T(8,128)(2,1)}) %reduce-scatter.12.cloned.1.call-update) | async-done | bytes 589840 | tf_op jit(solution)/shard_map/reduce_scatter | solution.py:218
  389.9 41.0 %reduce-scatter.10.cloned.1.call-done = bf16[256,1024]{1,0:T(8,128)(2,1)} async-done(((bf16[1024,1024]{1,0:T(8,128)(2,1)}), bf16[256,1024]{1,0:T(8,128)(2,1)}) %reduce-scatter.10.cloned.1.call-update) | async-done | bytes 524304 | tf_op jit(solution)/shard_map/reduce_scatter | solution.py:218
  469.9 34.2 %reduce-scatter.14.cloned.1.call-done = bf16[256,1024]{0,1:T(8,128)(2,1)} async-done(((bf16[1024,1024]{0,1:T(8,128)(2,1)}), bf16[256,1024]{0,1:T(8,128)(2,1)}) %reduce-scatter.14.cloned.1.call-update) | async-done | bytes 524304 | tf_op jit(solution)/shard_map/reduce_scatter | solution.py:218
  517.0 32.3 %reduce-scatter.20.cloned.1.call-done = bf16[256,1024]{1,0:T(8,128)(2,1)} async-done(((bf16[1024,1024]{1,0:T(8,128)(2,1)}), bf16[256,1024]{1,0:T(8,128)(2,1)}) %reduce-scatter.20.cloned.1.call-update) | async-done | bytes 524304 | tf_op jit(solution)/shard_map/reduce_scatter | solution.py:218
  549.3 78.7 %reduce-scatter.18.cloned.1.call-done = bf16[256,2048]{1,0:T(8,128)(2,1)} async-done(((bf16[1024,2048]{1,0:T(8,128)(2,1)}), bf16[256,2048]{1,0:T(8,128)(2,1)}) %reduce-scatter.18.cloned.1.call-update) | async-done | bytes 1048592 | tf_op jit(solution)/shard_map/reduce_scatter | solution.py:218
  628.1 75.9 %reduce-scatter.22.cloned.1.call-done = bf16[8,128,512]{2,1,0:T(8,128)(2,1)} async-done(((bf16[8,1024,512]{2,1,0:T(8,128)(2,1)}), bf16[8,128,512]{2,1,0:T(8,128)(2,1)}) %reduce-scatter.22.cloned.1.call-update) | async-done | bytes 1048592 | tf_op jit(solution)/shard_map/reduce_scatter | solution.py:385
  704.1 75.2 %reduce-scatter.24.cloned.1.call-done = bf16[8,128,512]{2,1,0:T(8,128)(2,1)} async-done(((bf16[8,1024,512]{2,1,0:T(8,128)(2,1)}), bf16[8,128,512]{2,1,0:T(8,128)(2,1)}) %reduce-scatter.24.cloned.1.call-update) | async-done | bytes 1048592 | tf_op jit(solution)/shard_map/reduce_scatter | solution.py:385
  779.4 74.8 %reduce-scatter.26.cloned.1.call-done = bf16[8,64,1024]{2,1,0:T(8,128)(2,1)} async-done(((bf16[8,512,1024]{2,1,0:T(8,128)(2,1)}), bf16[8,64,1024]{2,1,0:T(8,128)(2,1)}) %reduce-scatter.26.cloned.1.call-update) | async-done | bytes 1048592 | tf_op jit(solution)/shard_map/reduce_scatter | solution.py:385
  855.5 20.8 %reduce-scatter.16.cloned.1.call-done = bf16[256,34]{0,1:T(8,128)(2,1)} async-done(((bf16[1024,34]{0,1:T(8,128)(2,1)}), bf16[256,34]{0,1:T(8,128)(2,1)}) %reduce-scatter.16.cloned.1.call-update) | async-done | bytes 17424 | tf_op jit(solution)/shard_map/reduce_scatter | solution.py:218
  876.2 23.2 %psum.21 = bf16[256,34]{0,1:T(8,128)(2,1)S(1)} all-reduce(bf16[256,34]{0,1:T(8,128)(2,1)} %reduce-scatter.16.cloned.1.call-done), channel_id=1, replica_groups=mesh['group'=8,'expert'=4] {'group'}, use_global_device_ids=true, to_apply=%region_16.17 | all-reduce | flops 8704 | bytes 34816 | tf_op jit(solution)/shard_map/psum | solution.py:382
  900.7 36.1 %all-reduce.3.cloned.1.call-done = (bf16[256,2048]{1,0:T(8,128)(2,1)}, bf16[256,1024]{1,0:T(8,128)(2,1)}) async-done(((bf16[256,2048]{1,0:T(8,128)(2,1)}, bf16[256,1024]{1,0:T(8,128)(2,1)}), (bf16[256,2048]{1,0:T(8,128)(2,1)}, bf16[256,1024]{1,0:T(8,128)(2,1)})) %all-reduce.3.cloned.1.call-update) | async-done | bytes 1572880 | tf_op jit(solution)/shard_map/psum | solution.py:380
  943.1 48.9 %all-gather.19.cloned.1.call-done = bf16[8,1024,512]{2,1,0:T(8,128)(2,1)} async-done(((bf16[8,128,512]{2,1,0:T(8,128)(2,1)}), bf16[8,1024,512]{2,1,0:T(8,128)(2,1)}) %all-gather.19.cloned.1.call-update) | async-done | bytes 8388624 | tf_op jit(solution)/shard_map/all_gather | solution.py:386
  992.1 12.3 %convert_element_type.190 = f32[8,1024,512]{2,1,0:T(8,128)} convert(bf16[8,1024,512]{2,1,0:T(8,128)(2,1)} %all-gather.19.cloned.1.call-done) | non-fusion elementwise | flops 4194304 | bytes 25165824 | tf_op jit(solution)/shard_map/convert_element_type | solution.py:386
  1004.4 43.7 %all-gather.21.cloned.1.call-done = bf16[8,1024,512]{2,1,0:T(8,128)(2,1)} async-done(((bf16[8,128,512]{2,1,0:T(8,128)(2,1)}), bf16[8,1024,512]{2,1,0:T(8,128)(2,1)}) %all-gather.21.cloned.1.call-update) | async-done | bytes 8388624 | tf_op jit(solution)/shard_map/all_gather | solution.py:386
  1048.1 12.3 %convert_element_type.191 = f32[8,1024,512]{2,1,0:T(8,128)} convert(bf16[8,1024,512]{2,1,0:T(8,128)(2,1)} %all-gather.21.cloned.1.call-done) | non-fusion elementwise | flops 4194304 | bytes 25165824 | tf_op jit(solution)/shard_map/convert_element_type | solution.py:386
  1060.4 43.7 %all-gather.23.cloned.1.call-done = bf16[8,512,1024]{2,1,0:T(8,128)(2,1)} async-done(((bf16[8,64,1024]{2,1,0:T(8,128)(2,1)}), bf16[8,512,1024]{2,1,0:T(8,128)(2,1)}) %all-gather.23.cloned.1.call-update) | async-done | bytes 8388624 | tf_op jit(solution)/shard_map/all_gather | solution.py:386
  (181 shorter events, 132.1 us)
Async XLA Ops:
  7.2 94.5 %copy-start.10 = (bf16[256,1024]{1,0:T(8,128)(2,1)S(1)}, bf16[256,1024]{1,0:T(8,128)(2,1)}, u32[]{:S(2)}) copy-start(bf16[256,1024]{1,0:T(8,128)(2,1)} %param.27) | copy-start | bytes 1572868
  7.2 86.7 %all-gather.9.cloned.1.call-start = ((), (), s32[]{:S(2)}) async-start(), calls=%async_computation.9 | async-start | bytes 5242880 | tf_op jit(solution)/shard_map/all_gather | solution.py:214
  9.6 135.0 %all-gather.11.cloned.1.call-start = ((), (), s32[]{:S(2)}) async-start(), calls=%async_computation.10 | async-start | bytes 2621440 | tf_op jit(solution)/shard_map/all_gather | solution.py:214
  27.9 76.3 %copy-start.29 = (f32[256]{0:T(256)}, f32[256]{0:T(256)S(1)}, u32[]{:S(2)}) copy-start(f32[256]{0:T(256)S(1)} %add_rsqrt_fusion.1) | copy-start | bytes 3076
  28.0 76.3 %copy-start.23 = (f32[1024,1]{0,1:T(1,128)}, f32[1024,1]{0,1:T(1,128)S(1)}, u32[]{:S(2)}) copy-start(f32[1024,1]{0,1:T(1,128)S(1)} %get-tuple-element.43) | copy-start | bytes 12292
  28.0 165.1 %copy-start.20 = (f32[1024,1]{0,1:T(1,128)}, f32[1024,1]{0,1:T(1,128)S(1)}, u32[]{:S(2)}) copy-start(f32[1024,1]{0,1:T(1,128)S(1)} %get-tuple-element.42) | copy-start | bytes 12292
  100.3 90.4 %all-gather.13.cloned.1.call-start = ((), (), s32[]{:S(2)}) async-start(), calls=%async_computation.11 | async-start | bytes 2621440 | tf_op jit(solution)/shard_map/all_gather | solution.py:214
  101.0 138.5 %all-gather.17.cloned.1.call-start = ((), (), s32[]{:S(2)}) async-start(), calls=%async_computation.13 | async-start | bytes 2621440 | tf_op jit(solution)/shard_map/all_gather | solution.py:214
  102.7 183.3 %all-gather.15.cloned.1.call-start = ((), (), s32[]{:S(2)}) async-start(), calls=%async_computation.12 | async-start | bytes 2621440 | tf_op jit(solution)/shard_map/all_gather | solution.py:214
  194.1 191.4 %reduce-scatter.12.cloned.1.call-start = ((), (), s32[]{:S(2)}) async-start(), calls=%async_computation.15 | async-start | bytes 2949120 | tf_op jit(solution)/shard_map/reduce_scatter | solution.py:218
  194.3 192.3 %copy-start.15 = (pred[256,32]{1,0:T(32,128)(4,1)}, pred[256,32]{1,0:T(32,128)(4,1)S(1)}, u32[]{:S(2)}) copy-start(pred[256,32]{1,0:T(32,128)(4,1)S(1)} %copy.66) | copy-start | bytes 24580
  338.8 92.0 %copy-start.32 = (pred[256]{0:T(512)(128)(4,1)S(1)}, pred[256]{0:T(512)(128)(4,1)}, u32[]{:S(2)}) copy-start(pred[256]{0:T(512)(128)(4,1)} %copy-done.31) | copy-start | bytes 772
  338.8 92.0 %reduce-scatter.10.cloned.1.call-start = ((), (), s32[]{:S(2)}) async-start(), calls=%async_computation.14 | async-start | bytes 2621440 | tf_op jit(solution)/shard_map/reduce_scatter | solution.py:218
  339.6 164.5 %reduce-scatter.14.cloned.1.call-start = ((), (), s32[]{:S(2)}) async-start(), calls=%async_computation.16 | async-start | bytes 2621440 | tf_op jit(solution)/shard_map/reduce_scatter | solution.py:218
  461.2 88.1 %reduce-scatter.20.cloned.1.call-start = ((), (), s32[]{:S(2)}) async-start(), calls=%async_computation.19 | async-start | bytes 2621440 | tf_op jit(solution)/shard_map/reduce_scatter | solution.py:218
  464.3 163.7 %reduce-scatter.18.cloned.1.call-start = ((), (), s32[]{:S(2)}) async-start(), calls=%async_computation.18 | async-start | bytes 5242880 | tf_op jit(solution)/shard_map/reduce_scatter | solution.py:218
  509.7 194.3 %reduce-scatter.22.cloned.1.call-start = ((), (), s32[]{:S(2)}) async-start(), calls=%async_computation.20 | async-start | bytes 9437184 | tf_op jit(solution)/shard_map/reduce_scatter | solution.py:385
  510.5 268.8 %reduce-scatter.24.cloned.1.call-start = ((), (), s32[]{:S(2)}) async-start(), calls=%async_computation.22 | async-start | bytes 9437184 | tf_op jit(solution)/shard_map/reduce_scatter | solution.py:385
  511.1 343.1 %reduce-scatter.26.cloned.1.call-start = ((), (), s32[]{:S(2)}) async-start(), calls=%async_computation.24 | async-start | bytes 9437184 | tf_op jit(solution)/shard_map/reduce_scatter | solution.py:385
  511.8 364.4 %reduce-scatter.16.cloned.1.call-start = ((), (), s32[]{:S(2)}) async-start(), calls=%async_computation.17 | async-start | bytes 102400 | tf_op jit(solution)/shard_map/reduce_scatter | solution.py:218
  516.9 419.8 %all-reduce.3.cloned.1.call-start = ((), (), s32[]{:S(2)}) async-start(), calls=%async_computation.26 | async-start | bytes 3145728 | tf_op jit(solution)/shard_map/psum | solution.py:380
  628.0 364.0 %all-gather.19.cloned.1.call-start = ((), (), s32[]{:S(2)}) async-start(), calls=%async_computation.21 | async-start | bytes 9437184 | tf_op jit(solution)/shard_map/all_gather | solution.py:386
  704.0 344.1 %all-gather.21.cloned.1.call-start = ((), (), s32[]{:S(2)}) async-start(), calls=%async_computation.23 | async-start | bytes 9437184 | tf_op jit(solution)/shard_map/all_gather | solution.py:386
  779.3 324.8 %all-gather.23.cloned.1.call-start = ((), (), s32[]{:S(2)}) async-start(), calls=%async_computation.25 | async-start | bytes 9437184 | tf_op jit(solution)/shard_map/all_gather | solution.py:386
  (27 other events, 573.0 us)
Sparse Core Ops, SparseCore 0:
  10.1 83.6 all-gather.8
  100.4 44.1 all-gather.10
  146.1 44.4 all-gather.12
  192.6 46.7 all-gather.16
  241.4 44.4 all-gather.14
  339.0 46.4 reduce-scatter.11
  387.8 43.0 reduce-scatter.9
  461.3 42.8 reduce-scatter.13
  506.4 42.8 reduce-scatter.19
  552.0 75.9 reduce-scatter.17
  632.0 71.8 reduce-scatter.21
  707.9 71.3 reduce-scatter.23
  782.8 71.3 reduce-scatter.25
  856.8 19.3 reduce-scatter.15
  879.4 57.3 all-reduce.2
  938.5 53.4 all-gather.18
  993.8 54.2 all-gather.20
  1049.9 54.2 all-gather.22

commit v2 on v1

--- a/solution.py
+++ b/solution.py
@@ -210,6 +210,587 @@
     )(x_all, ct_all, router_t, rank_row, rank_col, w_gate, w_up, w_down)
 
 
+MESH = pl.DeviceIdType.MESH
+ANY = pl.BlockSpec(memory_space=pl.ANY)
+IN_VMEM = pl.BlockSpec(memory_space=pltpu.VMEM)
+
+
+def remote(source, target, send, receive, device):
+    return pltpu.make_async_remote_copy(
+        src_ref=source,
+        dst_ref=target,
+        send_sem=send,
+        recv_sem=receive,
+        device_id=device,
+        device_id_type=MESH,
+    )
+
+
+def greet(devices):
+    barrier = pltpu.get_barrier_semaphore()
+    count = 0
+    for condition, device in devices:
+        if condition is None:
+            pl.semaphore_signal(barrier, inc=1, device_id=device, device_id_type=MESH)
+            count = count + 1
+        else:
+
+            @pl.when(condition)
+            def _():
+                pl.semaphore_signal(barrier, inc=1, device_id=device, device_id_type=MESH)
+
+            count = count + jnp.where(condition, 1, 0)
+    pl.semaphore_wait(barrier, count)
+
+
+def line_gather_kernel(n, count, *refs):
+    ins, outs = refs[:count], refs[count : 2 * count]
+    local, send, receive = refs[2 * count :]
+    group, me = lax.axis_index("group"), lax.axis_index("expert")
+    left, right = (group, me - 1), (group, me + 1)
+    own = [
+        pltpu.make_async_copy(ins[i], outs[i].at[me], local.at[i]) for i in range(count)
+    ]
+    for copy in own:
+        copy.start()
+    greet([(me > 0, left), (me < n - 1, right)])
+
+    def hop(i, step, side):
+        block = me - step if side == 0 else me + step
+        source = ins[i] if step == 0 else outs[i].at[block]
+        index = (side, step, i)
+        return remote(
+            source, outs[i].at[block], send.at[index], receive.at[index], right if side == 0 else left
+        )
+
+    def arrival(i, step, side):
+        block = me - 1 - step if side == 0 else me + 1 + step
+        index = (side, step, i)
+        return remote(
+            outs[i].at[block], outs[i].at[block], send.at[index], receive.at[index], left if side == 0 else right
+        )
+
+    def sends(step, side):
+        return (me - step >= 0) & (me < n - 1) if side == 0 else (me + step < n) & (me > 0)
+
+    def arrives(step, side):
+        return me - 1 - step >= 0 if side == 0 else me + 1 + step < n
+
+    for step in range(n - 1):
+        for side in (0, 1):
+
+            @pl.when(sends(step, side))
+            def _():
+                for i in range(count):
+                    hop(i, step, side).start()
+
+        for side in (0, 1):
+
+            @pl.when(arrives(step, side))
+            def _():
+                for i in range(count):
+                    arrival(i, step, side).wait_recv()
+
+    for step in range(n - 1):
+        for side in (0, 1):
+
+            @pl.when(sends(step, side))
+            def _():
+                for i in range(count):
+                    hop(i, step, side).wait_send()
+
+    for copy in own:
+        copy.wait()
+
+
+def line_gather(values, n, collective_id, name):
+    count = len(values)
+    outs = pl.pallas_call(
+        functools.partial(line_gather_kernel, n, count),
+        out_shape=[jax.ShapeDtypeStruct((n,) + v.shape, v.dtype) for v in values],
+        in_specs=[IN_VMEM] * count,
+        out_specs=[ANY] * count,
+        scratch_shapes=[
+            pltpu.SemaphoreType.DMA((count,)),
+            pltpu.SemaphoreType.DMA((2, n - 1, count)),
+            pltpu.SemaphoreType.DMA((2, n - 1, count)),
+        ],
+        compiler_params=pltpu.CompilerParams(collective_id=collective_id, has_side_effects=True),
+        cost_estimate=pl.CostEstimate(flops=0, bytes_accessed=100000000, transcendentals=0),
+        name=name,
+    )(*values)
+    return [o.reshape((n * v.shape[0],) + v.shape[1:]) for o, v in zip(outs, values)]
+
+
+def line_scatter_kernel(n, part_ref, out_ref, landing, staging, send, receive):
+    group, me = lax.axis_index("group"), lax.axis_index("expert")
+    left, right = (group, me - 1), (group, me + 1)
+    rows = part_ref.shape[1]
+    tile = 32
+    greet([(me > 0, left), (me < n - 1, right)])
+
+    def add(target, first, second):
+        def body(t, carry):
+            span = pl.ds(pl.multiple_of(t * tile, tile), tile)
+            target[span, :] = (first[span, :].astype(F32) + second[span, :].astype(F32)).astype(
+                target.dtype
+            )
+            return carry
+
+        lax.fori_loop(0, rows // tile, body, 0)
+
+    def copy(source, step, side):
+        return remote(
+            source,
+            landing.at[side, step],
+            send.at[side, step],
+            receive.at[side, step],
+            right if side == 0 else left,
+        )
+
+    for step in range(n - 1):
+        for side in (0, 1):
+            owner = n - 1 - step if side == 0 else step
+            beyond = me < owner if side == 0 else me > owner
+            edge = me == 0 if side == 0 else me == n - 1
+
+            @pl.when(beyond & edge)
+            def _():
+                copy(part_ref.at[owner], step, side).start()
+
+            @pl.when(beyond & jnp.logical_not(edge))
+            def _():
+                copy(part_ref.at[owner], step, side).wait_recv()
+                add(staging.at[side, step], part_ref.at[owner], landing.at[side, step])
+                copy(staging.at[side, step], step, side).start()
+
+    @pl.when(me > 0)
+    def _():
+        step = n - 1 - me
+        copy(part_ref.at[me], step, 0).wait_recv()
+
+    @pl.when(me < n - 1)
+    def _():
+        copy(part_ref.at[me], me, 1).wait_recv()
+
+    def finish(t, carry):
+        span = pl.ds(pl.multiple_of(t * tile, tile), tile)
+        total = part_ref[me, span, :].astype(F32)
+        from_left = landing[0, jnp.minimum(n - 1 - me, n - 2), span, :].astype(F32)
+        from_right = landing[1, jnp.minimum(me, n - 2), span, :].astype(F32)
+        total = total + jnp.where(me > 0, from_left, 0.0)
+        total = total + jnp.where(me < n - 1, from_right, 0.0)
+        out_ref[span, :] = total.astype(out_ref.dtype)
+        return carry
+
+    lax.fori_loop(0, rows // tile, finish, 0)
+    for step in range(n - 1):
+        for side in (0, 1):
+            owner = n - 1 - step if side == 0 else step
+            beyond = me < owner if side == 0 else me > owner
+
+            @pl.when(beyond)
+            def _():
+                copy(part_ref.at[owner], step, side).wait_send()
+
+
+def line_scatter(value, n, dtype, collective_id, name):
+    total, width = value.shape
+    rows = total // n
+    return pl.pallas_call(
+        functools.partial(line_scatter_kernel, n),
+        out_shape=jax.ShapeDtypeStruct((rows, width), dtype),
+        in_specs=[IN_VMEM],
+        out_specs=IN_VMEM,
+        scratch_shapes=[
+            pltpu.VMEM((2, n - 1, rows, width), BF),
+            pltpu.VMEM((2, n - 1, rows, width), BF),
+            pltpu.SemaphoreType.DMA((2, n - 1)),
+            pltpu.SemaphoreType.DMA((2, n - 1)),
+        ],
+        compiler_params=pltpu.CompilerParams(collective_id=collective_id, has_side_effects=True),
+        cost_estimate=pl.CostEstimate(flops=0, bytes_accessed=100000000, transcendentals=0),
+        name=name,
+    )(value.reshape(n, rows, width))
+
+
+def plane_position():
+    group, me = lax.axis_index("group"), lax.axis_index("expert")
+    c, x, y = group % 2, (group // 2) % 2, (group // 4) % 2
+    by_c, by_x, by_y = (group + 1 - 2 * c, me), (group + 2 - 4 * x, me), (group + 4 - 8 * y, me)
+    return group, me, (y, x, c), (by_y, by_x, by_c)
+
+
+def weights_kernel(n, pieces, widths, *refs):
+    wq, wk, wv, wo, small = refs[:5]
+    outs, owns = refs[5:8], refs[8:11]
+    load, store, zsend, zrecv, psend, precv, csend, crecv = refs[11:]
+    group, me, (y, x, c), (by_y, by_x, by_c) = plane_position()
+    left, right = (group, me - 1), (group, me + 1)
+    eighth = owns[0].shape[0]
+    span = pl.ds(pl.multiple_of((y * 4 + x * 2 + c) * eighth, eighth), eighth)
+    query_width, key_width = wq.shape[1], wk.shape[1]
+    targets = (
+        owns[0].at[:, :query_width],
+        owns[0].at[:, query_width : query_width + key_width],
+        owns[0].at[:, query_width + key_width :],
+        owns[1],
+        owns[2],
+    )
+    loads = [
+        pltpu.make_async_copy(source.at[span, :], target, load.at[i])
+        for i, (source, target) in enumerate(zip((wq, wk, wv, wo, small), targets))
+    ]
+    for copy in loads:
+        copy.start()
+    for copy in loads:
+        copy.wait()
+    stores = [
+        pltpu.make_async_copy(owns[i], outs[i].at[me, y, x, c], store.at[i]) for i in range(3)
+    ]
+    for copy in stores:
+        copy.start()
+    greet(
+        [(me > 0, left), (me < n - 1, right), (None, by_c), (None, by_x), (None, by_y)]
+    )
+
+    def hop(i, step, side):
+        block = me - step if side == 0 else me + step
+        source = owns[i] if step == 0 else outs[i].at[block, y, x, c]
+        index = (side, step, i)
+        return remote(
+            source,
+            outs[i].at[block, y, x, c],
+            zsend.at[index],
+            zrecv.at[index],
+            right if side == 0 else left,
+        )
+
+    def sends(step, side):
+        return (me - step >= 0) & (me < n - 1) if side == 0 else (me + step < n) & (me > 0)
+
+    def first(slot, block, p):
+        i, start, width, along_x = pieces[p]
+        spot = outs[i].at[block, y, x, c, :, start : start + width]
+        source = owns[i].at[:, start : start + width] if slot == 0 else spot
+        index = (0, slot, p)
+        return remote(source, spot, psend.at[index], precv.at[index], by_x if along_x else by_y)
+
+    def second(slot, block, p):
+        i, start, width, along_x = pieces[p]
+        columns = slice(start, start + width)
+        if along_x:
+            spot = outs[i].at[block, y, :, c, :, columns]
+        else:
+            spot = outs[i].at[block, :, x, c, :, columns]
+        index = (1, slot, p)
+        return remote(spot, spot, psend.at[index], precv.at[index], by_y if along_x else by_x)
+
+    def third(slot, block, i):
+        spot = outs[i].at[block, :, :, c]
+        index = (slot, i)
+        return remote(spot, spot, csend.at[index], crecv.at[index], by_c)
+
+    def held(step):
+        if step == 0:
+            return [(0, me, me >= 0)]
+        return [(step, me - step, me - step >= 0), (n - 1 + step, me + step, me + step < n)]
+
+    count = len(pieces)
+    for step in range(n + 2):
+        if step < n:
+            for slot, block, there in held(step):
+
+                @pl.when(there)
+                def _():
+                    if step > 0:
+                        side = 0 if slot < n else 1
+                        for i in range(3):
+                            hop(i, step - 1, side).wait_recv()
+                    for p in range(count):
+                        first(slot, block, p).start()
+
+            if step < n - 1:
+                for side in (0, 1):
+
+                    @pl.when(sends(step, side))
+                    def _():
+                        for i in range(3):
+                            hop(i, step, side).start()
+
+        if 1 <= step < n + 1:
+            if step == 1:
+                for copy in stores:
+                    copy.wait()
+            for slot, block, there in held(step - 1):
+
+                @pl.when(there)
+                def _():
+                    for p in range(count):
+                        first(slot, block, p).wait_recv()
+                    for p in range(count):
+                        second(slot, block, p).start()
+
+        if step >= 2:
+            for slot, block, there in held(step - 2):
+
+                @pl.when(there)
+                def _():
+                    for p in range(count):
+                        second(slot, block, p).wait_recv()
+                    for i in range(3):
+                        third(slot, block, i).start()
+
+    for step in range(n):
+        for slot, block, there in held(step):
+
+            @pl.when(there)
+            def _():
+                for p in range(count):
+                    first(slot, block, p).wait_send()
+                    second(slot, block, p).wait_send()
+                for i in range(3):
+                    third(slot, block, i).wait()
+
+        if step < n - 1:
+            for side in (0, 1):
+
+                @pl.when(sends(step, side))
+                def _():
+                    for i in range(3):
+                        hop(i, step, side).wait_send()
+
+
+def path_pieces(query_width, key_width, out_width, small_width):
+    half = (query_width + 2 * key_width + out_width) // 2
+    return (
+        (0, 0, half, True),
+        (0, half, query_width + 2 * key_width - half, False),
+        (1, 0, out_width, False),
+        (2, 0, small_width, True),
+    )
+
+
+def gather_weights(wq, wk, wv, wo, small, n, collective_id):
+    rows = wq.shape[0]
+    eighth = rows // 8
+    widths = (wq.shape[1] + wk.shape[1] + wv.shape[1], wo.shape[1], small.shape[1])
+    pieces = path_pieces(wq.shape[1], wk.shape[1], wo.shape[1], small.shape[1])
+    outs = pl.pallas_call(
+        functools.partial(weights_kernel, n, pieces, widths),
+        out_shape=[jax.ShapeDtypeStruct((n, 2, 2, 2, eighth, w), BF) for w in widths],
+        in_specs=[ANY] * 5,
+        out_specs=[ANY] * 3,
+        scratch_shapes=[pltpu.VMEM((eighth, w), BF) for w in widths]
+        + [
+            pltpu.SemaphoreType.DMA((5,)),
+            pltpu.SemaphoreType.DMA((3,)),
+            pltpu.SemaphoreType.DMA((2, n - 1, 3)),
+            pltpu.SemaphoreType.DMA((2, n - 1, 3)),
+            pltpu.SemaphoreType.DMA((2, 2 * n - 1, 4)),
+            pltpu.SemaphoreType.DMA((2, 2 * n - 1, 4)),
+            pltpu.SemaphoreType.DMA((2 * n - 1, 3)),
+            pltpu.SemaphoreType.DMA((2 * n - 1, 3)),
+        ],
+        compiler_params=pltpu.CompilerParams(collective_id=collective_id, has_side_effects=True),
+        cost_estimate=pl.CostEstimate(flops=0, bytes_accessed=100000000, transcendentals=0),
+        name="gather_weights",
+    )(wq, wk, wv, wo, small)
+    return [o.reshape(n * rows, w) for o, w in zip(outs, widths)]
+
+
+def reduce_kernel(n, pieces, *refs):
+    ins, outs = refs[:3], refs[3:5]
+    pair, one, two, landing, staging = refs[5:7], refs[7:9], refs[9:11], refs[11:13], refs[13:15]
+    csend, crecv, psend, precv, zsend, zrecv, gsend, grecv = refs[15:]
+    group, me, (y, x, c), (by_y, by_x, by_c) = plane_position()
+    left, right = (group, me - 1), (group, me + 1)
+    eighth = pair[0].shape[3]
+    greet(
+        [(me > 0, left), (me < n - 1, right), (None, by_c), (None, by_x), (None, by_y)]
+    )
+
+    places, ends = [], [0, 0]
+    for array, start, width, along_x in pieces:
+        path = 0 if along_x else 1
+        places.append((array, start, width, path, ends[path]))
+        ends[path] += width
+
+    def swap(p):
+        array, start, width, path, at = places[p]
+        return remote(
+            ins[array].at[:, :, :, 1 - c, :, start : start + width],
+            pair[path].at[:, :, :, :, at : at + width],
+            csend.at[p],
+            crecv.at[p],
+            by_c,
+        )
+
+    for p in range(len(places)):
+        swap(p).start()
+    for p in range(len(places)):
+        swap(p).wait_recv()
+        array, start, width, path, at = places[p]
+
+        def pair_sum(t, carry):
+            z, a, b = t // 4, (t // 2) % 2, t % 2
+            mine = ins[array][z, a, b, c, :, start : start + width].astype(F32)
+            theirs = pair[path][z, a, b, :, at : at + width].astype(F32)
+            pair[path][z, a, b, :, at : at + width] = (mine + theirs).astype(BF)
+            return carry
+
+        lax.fori_loop(0, 4 * n, pair_sum, 0)
+
+    def first(path):
+        source = pair[0].at[:, :, 1 - x] if path == 0 else pair[1].at[:, 1 - y]
+        return remote(
+            source, one[path], psend.at[0, path], precv.at[0, path], by_x if path == 0 else by_y
+        )
+
+    def second(path):
+        source = one[path].at[:, 1 - y] if path == 0 else one[path].at[:, 1 - x]
+        return remote(
+            source, two[path], psend.at[1, path], precv.at[1, path], by_y if path == 0 else by_x
+        )
+
+    for path in (0, 1):
+        first(path).start()
+    for path in (0, 1):
+        first(path).wait_recv()
+
+        def first_sum(t, carry):
+            z, a = t // 2, t % 2
+            mine = pair[0][z, a, x] if path == 0 else pair[1][z, y, a]
+            one[path][z, a] = (mine.astype(F32) + one[path][z, a].astype(F32)).astype(BF)
+            return carry
+
+        lax.fori_loop(0, 2 * n, first_sum, 0)
+        second(path).start()
+    for path in (0, 1):
+        second(path).wait_recv()
+
+        def second_sum(z, carry):
+            mine = one[0][z, y] if path == 0 else one[1][z, x]
+            two[path][z] = (mine.astype(F32) + two[path][z].astype(F32)).astype(BF)
+            return carry
+
+        lax.fori_loop(0, n, second_sum, 0)
+
+    def hop(source, path, step, side):
+        index = (path, side, step)
+        return remote(
+            source,
+            landing[path].at[side, step],
+            zsend.at[index],
+            zrecv.at[index],
+            right if side == 0 else left,
+        )
+
+    for step in range(n - 1):
+        for side in (0, 1):
+            owner = n - 1 - step if side == 0 else step
+            beyond = me < owner if side == 0 else me > owner
+            edge = me == 0 if side == 0 else me == n - 1
+
+            @pl.when(beyond & edge)
+            def _():
+                for path in (0, 1):
+                    hop(two[path].at[owner], path, step, side).start()
+
+            @pl.when(beyond & jnp.logical_not(edge))
+            def _():
+                for path in (0, 1):
+                    hop(two[path].at[owner], path, step, side).wait_recv()
+                    staging[path][side, step] = (
+                        two[path][owner].astype(F32) + landing[path][side, step].astype(F32)
+                    ).astype(BF)
+                    hop(staging[path].at[side, step], path, step, side).start()
+
+    @pl.when(me > 0)
+    def _():
+        for path in (0, 1):
+            hop(two[path].at[me], path, n - 1 - me, 0).wait_recv()
+
+    @pl.when(me < n - 1)
+    def _():
+        for path in (0, 1):
+            hop(two[path].at[me], path, me, 1).wait_recv()
+
+    for path in (0, 1):
+        total = two[path][me].astype(F32)
+        from_left = landing[path][0, jnp.minimum(n - 1 - me, n - 2)].astype(F32)
+        from_right = landing[path][1, jnp.minimum(me, n - 2)].astype(F32)
+        total = total + jnp.where(me > 0, from_left, 0.0)
+        total = total + jnp.where(me < n - 1, from_right, 0.0)
+        outs[path][y, x, c] = total.astype(BF)
+
+    def spread(path, stage):
+        out = outs[path]
+        if stage == 2:
+            spot, device = out.at[:, :, c], by_c
+        elif stage == 0:
+            spot, device = out.at[y, x, c], by_x if path == 0 else by_y
+        elif path == 0:
+            spot, device = out.at[y, :, c], by_y
+        else:
+            spot, device = out.at[:, x, c], by_x
+        return remote(spot, spot, gsend.at[path, stage], grecv.at[path, stage], device)
+
+    for stage in range(3):
+        for path in (0, 1):
+            spread(path, stage).start()
+        for path in (0, 1):
+            spread(path, stage).wait_recv()
+
+    for path in (0, 1):
+        for stage in range(3):
+            spread(path, stage).wait_send()
+        first(path).wait_send()
+        second(path).wait_send()
+    for p in range(len(places)):
+        swap(p).wait_send()
+    for step in range(n - 1):
+        for side in (0, 1):
+            owner = n - 1 - step if side == 0 else step
+            beyond = me < owner if side == 0 else me > owner
+
+            @pl.when(beyond)
+            def _():
+                for path in (0, 1):
+                    hop(two[path].at[owner], path, step, side).wait_send()
+
+
+def reduce_weights(grad_qkv, grad_out, grad_small, query_width, n, collective_id):
+    values = (grad_qkv, grad_out, grad_small)
+    rows = grad_qkv.shape[0] // n
+    eighth = rows // 8
+    key_width = (grad_qkv.shape[1] - query_width) // 2
+    pieces = path_pieces(query_width, key_width, grad_out.shape[1], grad_small.shape[1])
+    widths = [sum(p[2] for p in pieces if p[3]), sum(p[2] for p in pieces if not p[3])]
+    scratch = [pltpu.VMEM((n, 2, 2, eighth, w), BF) for w in widths]
+    scratch += [pltpu.VMEM((n, 2, eighth, w), BF) for w in widths]
+    scratch += [pltpu.VMEM((n, eighth, w), BF) for w in widths]
+    scratch += [pltpu.VMEM((2, n - 1, eighth, w), BF) for w in widths] * 2
+    sems = [(4,), (4,), (2, 2), (2, 2), (2, 2, n - 1), (2, 2, n - 1), (2, 3), (2, 3)]
+    outs = pl.pallas_call(
+        functools.partial(reduce_kernel, n, pieces),
+        out_shape=[jax.ShapeDtypeStruct((2, 2, 2, eighth, w), BF) for w in widths],
+        in_specs=[IN_VMEM] * 3,
+        out_specs=[IN_VMEM] * 2,
+        scratch_shapes=scratch + [pltpu.SemaphoreType.DMA(s) for s in sems],
+        compiler_params=pltpu.CompilerParams(
+            collective_id=collective_id, has_side_effects=True, vmem_limit_bytes=48 * 1024 * 1024
+        ),
+        cost_estimate=pl.CostEstimate(flops=0, bytes_accessed=100000000, transcendentals=0),
+        name="reduce_weights",
+    )(*[v.reshape(n, 2, 2, 2, eighth, v.shape[1]) for v in values])
+    first, second = [o.reshape(rows, w) for o, w in zip(outs, widths)]
+    cut = pieces[0][2]
+    rest = pieces[1][2]
+    qkv = jnp.concatenate([first[:, :cut], second[:, :rest]], axis=1)
+    return qkv, second[:, rest:], first[:, cut:]
+
+
 def gather_rows(value):
     return lax.all_gather(value, "expert", axis=0, tiled=True)
 
@@ -235,6 +816,7 @@
     cotangent,
 ):
     rows = tokens.shape[0]
+    n, groups = lax.axis_size("expert"), lax.axis_size("group")
     my_index = lax.axis_index("expert")
     capacity = 3 * rows * TOP // (2 * EXPERTS)
     group_of_heads = QUERY_HEADS // KEY_VALUE_HEADS
@@ -245,21 +827,23 @@
     valid_rows = (positions < length)[:, None]
     grad_output = jnp.where(valid_rows, cotangent, jnp.zeros_like(cotangent))
 
-    qkv_weight = gather_rows(jnp.concatenate([w_query, key_projection, value_projection], axis=1))
-    small = jnp.concatenate([norm_gain1[:, None], norm_gain2[:, None], w_router], axis=1)
-    small = gather_rows(small)
-    gain_one = small[:, 0].astype(F32)
-    gain_two = small[:, 1].astype(F32)
-    router_weight = small[:, 2:]
-    out_weight = gather_rows(w_out)
+    small = jnp.concatenate(
+        [w_router, norm_gain1[:, None], norm_gain2[:, None]]
+        + [jnp.zeros((w_router.shape[0], LANES - EXPERTS - 2), BF)],
+        axis=1,
+    )
+    qkv_weight, out_weight, small = gather_weights(
+        w_query, key_projection, value_projection, w_out, small, n, 1
+    )
+    router_weight = small[:, :EXPERTS]
+    gain_one = small[:, EXPERTS].astype(F32)
+    gain_two = small[:, EXPERTS + 1].astype(F32)
 
     expert_ids = jnp.arange(EXPERTS, dtype=jnp.int32)
     hot = jnp.any(routes[:, :, None] == expert_ids, axis=1)
     row_id = jnp.arange(rows, dtype=jnp.int32)
-    earlier = (row_id[None, :] < row_id[:, None]).astype(BF)
-    rank = jnp.where(hot, dot(earlier, hot.astype(BF)), 255.0).astype(BF)
-    rank_all = gather_rows(rank)
-    rank_row = rank_all.T.astype(F32)
+    earlier = (row_id[:, None] < row_id[None, :]).astype(BF)
+    rank = jnp.where(hot.T, dot(hot.T.astype(BF), earlier), 255.0).astype(BF)
     ct_all = gather_rows(grad_output)
 
     cosine_lookup, sine_lookup = rotary_tables(positions, HEAD_DIMENSION)
@@ -279,7 +863,12 @@
         unrotated_key.reshape(rows, KEY_VALUE_HEADS, HEAD_DIMENSION), cosine_lookup, sine_lookup
     ).astype(BF)
     local_keys = local_keys.reshape(rows, key_width)
-    kv_all = gather_rows(jnp.concatenate([local_keys, value_pre.astype(BF)], axis=1))
+    kv_all, rank_all = line_gather(
+        [jnp.concatenate([local_keys, value_pre.astype(BF)], axis=1), rank], n, 2, "gather_kv"
+    )
+    rank_all = rank_all.reshape(n, EXPERTS, rows)
+    rank_row = jnp.transpose(rank_all, (1, 0, 2)).reshape(EXPERTS, n * rows).astype(F32)
+    rank_col = jnp.transpose(rank_all, (0, 2, 1)).reshape(n * rows, EXPERTS)
     key_portion = kv_all[:, :key_width].reshape(-1, KEY_VALUE_HEADS, HEAD_DIMENSION)
     value_portion = kv_all[:, key_width:].reshape(-1, KEY_VALUE_HEADS, HEAD_DIMENSION)
     key_count = kv_all.shape[0]
@@ -305,12 +894,12 @@
     inverse_two = lax.rsqrt(jnp.mean(residual * residual, axis=-1, keepdims=True) + EPSILON)
     unit_two = residual * inverse_two
     second_norm = (unit_two * gain_two).astype(BF)
-    x_all = gather_rows(second_norm)
+    (x_all,) = line_gather([second_norm], n, 3, "gather_rows")
 
     y_part, gs_part, grad_gate, grad_up, grad_down = run_experts(
-        x_all, ct_all, router_weight.T, rank_row, rank_all, w_gate, w_up, w_down, rows, capacity
-    )
-    gs = scatter_rows(gs_part).astype(F32)
+        x_all, ct_all, router_weight.T, rank_row, rank_col, w_gate, w_up, w_down, rows, capacity
+    )
+    gs = line_scatter(gs_part, n, F32, 4, "scatter_grads")
     expert_sum = scatter_rows(y_part).astype(F32)
     mixed = (residual + expert_sum).astype(BF)
 
@@ -349,8 +938,12 @@
     value_gradient = jnp.einsum(
         "hgqk,qhgd->khd", probability.astype(BF), head_gradient, preferred_element_type=F32
     ).reshape(key_count, key_width)
-    kv_gradient = scatter_rows(
-        jnp.concatenate([key_gradient.astype(BF), value_gradient.astype(BF)], axis=1)
+    kv_gradient = line_scatter(
+        jnp.concatenate([key_gradient.astype(BF), value_gradient.astype(BF)], axis=1),
+        n,
+        BF,
+        5,
+        "scatter_kv",
     )
     own_key_gradient = kv_gradient[:, :key_width].astype(F32)
     grad_query_rows = grad_query_acc.reshape(rows, QUERY_HEADS, HEAD_DIMENSION) * score_scale
@@ -375,11 +968,17 @@
     grad_tokens = grad_residual + inverse_one * (
         scaled_one - unit_one * jnp.mean(scaled_one * unit_one, axis=-1, keepdims=True)
     )
-    grad_small = jnp.concatenate([grad_gain1[:, None], grad_gain2[:, None], grad_router], axis=1)
-
-    share_qkv = lax.psum(scatter_rows(grad_qkv.astype(BF)), "group").astype(F32)
-    share_out = lax.psum(scatter_rows(grad_out.astype(BF)), "group").astype(F32)
-    share_small = lax.psum(scatter_rows(grad_small.astype(BF)), "group").astype(F32)
+    grad_small = jnp.concatenate(
+        [grad_router, grad_gain1[:, None], grad_gain2[:, None]]
+        + [jnp.zeros((D, LANES - EXPERTS - 2), F32)],
+        axis=1,
+    )
+    shares = (grad_qkv.astype(BF), grad_out.astype(BF), grad_small.astype(BF))
+    if groups == 8:
+        shares = reduce_weights(*shares, query_width, n, 6)
+    else:
+        shares = [lax.psum(scatter_rows(share), "group") for share in shares]
+    share_qkv, share_out, share_small = [share.astype(F32) for share in shares]
 
     def sum_over_groups(value, axis):
         part = lax.psum_scatter(value, "group", scatter_dimension=axis, tiled=True)
@@ -388,13 +987,13 @@
     return (
         mixed,
         grad_tokens,
-        share_small[:, 0],
+        share_small[:, EXPERTS],
         share_qkv[:, :query_width],
         share_qkv[:, query_width : query_width + key_width],
         share_qkv[:, query_width + key_width :],
         share_out,
-        share_small[:, 1],
-        share_small[:, 2:],
+        share_small[:, EXPERTS + 1],
+        share_small[:, :EXPERTS],
         sum_over_groups(grad_gate, 1),
         sum_over_groups(grad_up, 1),
         sum_over_groups(grad_down, 1),

time: 1130 us -> 824 us (0.73)
  waiting for transfers between devices: 846 us -> 220 us
  Pallas kernels: 52.8 us -> 420 us
  blocking collectives: 54.5 us -> 0 us
    pallas_call x0 -> x6, Pallas kernels: none -> 367 us  [the longest x2 130 us: line_scatter(): pl.pallas_call(functools.partial(line_scatter_kernel, n), out_shape=jax.S...]
    reduce_scatter x6 -> x1, waiting for transfers between devices: 250 us -> 0.01 us  [scatter_rows(): return lax.psum_scatter(value, 'expert', scatter_dimension=0, tiled=True)]
    all_gather x5 -> x1, waiting for transfers between devices: 194 us -> 0.01 us  [gather_rows(): return lax.all_gather(value, 'expert', axis=0, tiled=True)]
    all_gather x3, waiting for transfers between devices: 136 us -> 0.01 us  [sum_over_groups(): return lax.all_gather(part, 'group', axis=axis, tiled=True).astype(F32)]
    psum x1 -> x0, waiting for transfers between devices: 36.1 us -> none  [per_device(): share_qkv = lax.psum(scatter_rows(grad_qkv.astype(BF)), 'group').astype(F32)]
    all_gather x2 -> x0, blocking collectives: 31.2 us -> none  [gather_rows(): return lax.all_gather(value, 'expert', axis=0, tiled=True)]
    psum x1 -> x0, blocking collectives: 23.2 us -> none  [per_device(): lax.psum(scatter_rows(grad_small.astype(BF)), 'group').astype(F32)]
  transfers between devices with their start and end apart: 18 -> 8, of which waited for: 18 -> 3; matrix products, arithmetic and copies ran while one was open for 9% -> 18% of each run, Pallas kernels for 0% -> 45%
where the time goes in v2:
time: 824 us; the launch traced here: 818 us
  Pallas kernels  420 us (51%)
  waiting for transfers between devices  220 us (27%)
  other arithmetic  68.2 us (8%)
  matrix products  61.4 us (7%)
  local copies, waits for them, and re-layouts  31.8 us (4%)
  between operations  15.7 us (2%)
    reduce_scatter x3, waiting for transfers between devices, sum_over_groups(): part = lax.psum_scatter(value, 'group', scatter_dimension=axis, tiled=True)  218 us
    pallas_call x2, Pallas kernels, line_scatter(): pl.pallas_call(functools.partial(line_scatter_kernel, n), out_shape=jax.S...  130 us
    pallas_call x1, Pallas kernels, reduce_weights(): pl.pallas_call(functools.partial(reduce_kernel, n, pieces), out_shape=[ja...  90 us
    pallas_call x2, Pallas kernels, line_gather(): pl.pallas_call(functools.partial(line_gather_kernel, n, count), out_shape...  78.5 us
    pallas_call x1, Pallas kernels, gather_weights(): pl.pallas_call(functools.partial(weights_kernel, n, pieces, widths), out_...  68.7 us
    pallas_call x1, Pallas kernels, run_experts(): pl.pallas_call(functools.partial(expert_kernel, sizes), grid=(local,), ou...  52.8 us
    convert_element_type x3, other arithmetic, sum_over_groups(): return lax.all_gather(part, 'group', axis=axis, tiled=True).astype(F32)  35.5 us
  transfers between devices with their start and end apart: 8, of which 3 were waited for; matrix products, arithmetic and copies ran while one was open for 18% of the time, Pallas kernels for 45%

profile of v2, /device:TPU:0, one launch (start us, length us, event | category | flops | bytes accessed | tf_op | source)
XLA Modules:
  0.0 818.2 jit_solution(4500463659932403065)
XLA Ops:
  13.1 68.7 %gather_weights.1 = (bf16[4,2,2,2,32,2048]{5,4,3,2,1,0:T(8,128)(2,1)}, bf16[4,2,2,2,32,1024]{5,4,3,2,1,0:T(8,128)(2,1)}, bf16[4,2,2,2,32,128]{5,4,3,2,1,0:T(8,128)(2,1)}) custom-call(bf16[256,1024]{1,0:T(8,128)(2,1)} %refs_0_.1, bf16[256,512]{1,0:T(8,128)(2,1)} %refs_1_.1, bf16[256,512]{1,0:T(8,128)(2,1)} %refs_2_.1, bf16[256,1024]{1,0:T(8,128)(2,1)} %refs_3_.1, ...), custom_call_target="tpu_custom_call" | custom-call | bytes 100000000 | tf_op jit(solution)/shard_map/gather_weights/pallas_call | solution.py:579
  84.5 3.7 fusion.39
  90.7 42.4 %gather_kv.1 = (bf16[4,256,1024]{2,1,0:T(8,128)(2,1)}, bf16[4,32,256]{2,1,0:T(8,128)(2,1)}) custom-call(bf16[256,1024]{1,0:T(8,128)(2,1)} %pad_maximum_fusion.2.refs_0_, bf16[32,256]{1,0:T(8,128)(2,1)} %fusion.23.refs_1_), custom_call_target="tpu_custom_call" | custom-call | bytes 100000000 | tf_op jit(solution)/shard_map/gather_kv/pallas_call | solution.py:308
  138.7 7.7 fusion.56
  146.5 8.6 %fusion.2 = f32[8,2,256]{2,1,0:T(2,128)S(1)} fusion(f32[8,2,256,1024]{2,3,1,0:T(8,128)} %get-tuple-element.62, f32[8,2,256]{2,1,0:T(2,128)S(1)} %get-tuple-element.61, pred[256,1024]{0,1:T(8,128)(4,1)S(1)} %fusion.33), kind=kLoop, calls=%fused_computation.6 | loop fusion | flops 12578816 | bytes 17072128 | tf_op jit(solution)/shard_map/reduce_sum | solution.py:884
  155.1 8.4 %fusion.32 = (bf16[256,8,2,64]{0,3,2,1:T(8,128)(2,1)S(1)}, f32[8,2,256,64]{2,3,1,0:T(8,128)}) fusion(f32[256,8,2]{0,2,1:T(2,128)S(1)} %bitcast.146, bf16[1024,8,64,1]{0,2,3,1:T(8,128)(2,1)S(1)} %bitcast.136, f32[8,2,256,1024]{2,3,1,0:T(8,128)} %get-tuple-element.62, f32[8,2,256]{2,1,0:T(2,128)S(1)} %get-tuple-element.61, pred[256,1024]{0,1:T(8,128)(4,1)S(1)} %fusion.33), kind=kOutput, calls=%fused_computation.48 | convolution fusion | flops 549978112 | bytes 19693568 | tf_op jit(solution)/shard_map/hgqk,khd->hgqd/dot_general | solution.py:886
  165.3 36.1 %gather_rows.1 = bf16[4,256,1024]{2,1,0:T(8,128)(2,1)} custom-call(bf16[256,1024]{1,0:T(8,128)(2,1)} %multiply_convert_fusion.refs_0_), custom_call_target="tpu_custom_call" | custom-call | bytes 100000000 | tf_op jit(solution)/shard_map/gather_rows/pallas_call | solution.py:308
  203.8 52.8 %experts.1 = (bf16[1024,1024]{1,0:T(8,128)(2,1)}, bf16[1024,1152]{1,0:T(8,128)(2,1)}, bf16[8,1024,512]{2,1,0:T(8,128)(2,1)}, bf16[8,1024,512]{2,1,0:T(8,128)(2,1)}, bf16[8,512,1024]{2,1,0:T(8,128)(2,1)}) custom-call(bf16[1024,1024]{1,0:T(8,128)(2,1)} %bitcast.130, bf16[1024,1024]{1,0:T(8,128)(2,1)} %all-gather.5.cloned.1.call-done.ct_ref, ...), custom_call_target="tpu_custom_call" | custom-call | flops 30601641984 | bytes 58720256 | tf_op jit(solution)/shard_map/experts/pallas_call | solution.py:170
  258.6 68.6 %reduce-scatter.7.cloned.1.call-done = bf16[8,128,512]{2,1,0:T(8,128)(2,1)} async-done(((bf16[8,1024,512]{2,1,0:T(8,128)(2,1)}), bf16[8,128,512]{2,1,0:T(8,128)(2,1)}) %reduce-scatter.7.cloned.1.call-update) | async-done | bytes 1048592 | tf_op jit(solution)/shard_map/reduce_scatter | solution.py:984
  327.7 74.9 %reduce-scatter.9.cloned.1.call-done = bf16[8,128,512]{2,1,0:T(8,128)(2,1)} async-done(((bf16[8,1024,512]{2,1,0:T(8,128)(2,1)}), bf16[8,128,512]{2,1,0:T(8,128)(2,1)}) %reduce-scatter.9.cloned.1.call-update) | async-done | bytes 1048592 | tf_op jit(solution)/shard_map/reduce_scatter | solution.py:984
  402.7 74.7 %reduce-scatter.11.cloned.1.call-done = bf16[8,64,1024]{2,1,0:T(8,128)(2,1)} async-done(((bf16[8,512,1024]{2,1,0:T(8,128)(2,1)}), bf16[8,64,1024]{2,1,0:T(8,128)(2,1)}) %reduce-scatter.11.cloned.1.call-update) | async-done | bytes 1048592 | tf_op jit(solution)/shard_map/reduce_scatter | solution.py:984
  478.1 83.6 %scatter_grads.1 = f32[256,1152]{1,0:T(8,128)} custom-call(bf16[4,256,1152]{2,1,0:T(8,128)(2,1)} %bitcast.127), custom_call_target="tpu_custom_call" | custom-call | bytes 100000000 | tf_op jit(solution)/shard_map/scatter_grads/pallas_call | solution.py:400
  575.7 8.3 %fusion.20 = bf16[1024,8,64]{0,2,1:T(8,128)(2,1)} fusion(bf16[256,8,2,64]{0,3,2,1:T(8,128)(2,1)S(1)} %bitcast.131, f32[8,2,256,1024]{2,3,1,0:T(8,128)} %get-tuple-element.62, f32[8,2,256]{2,1,0:T(2,128)S(1)} %bitcast.151, pred[256,1024]{0,1:T(8,128)(4,1)S(1)} %copy-done.10), kind=kOutput, calls=%fused_computation.28 | convolution fusion | flops 549978112 | bytes 18628608 | tf_op jit(solution)/shard_map/hgqk,qhgd->khd/dot_general | solution.py:938
  589.3 9.1 %fusion.1 = bf16[8,2,256,1024]{2,3,1,0:T(8,128)(2,1)S(1)} fusion(f32[8,2,256,1024]{2,3,1,0:T(8,128)} %get-tuple-element.62, bf16[1024,8,64,1]{0,2,3,1:T(8,128)(2,1)} %bitcast.137, bf16[256,8,2,64]{0,3,2,1:T(8,128)(2,1)} %bitcast.132, f32[8,2,256]{2,1,0:T(2,128)S(1)} %fusion.31, f32[8,2,256]{2,1,0:T(2,128)S(1)} %bitcast.152, pred[256,1024]{0,1:T(8,128)(4,1)S(1)} %copy-done.10), kind=kOutput, calls=%fused_computation.2 | convolution fusion | flops 557842432 | bytes 27033600 | tf_op jit(solution)/shard_map/qhgd,khd->hgqk/dot_general | solution.py:928
  598.4 3.4 copy-done
  601.8 3.6 fusion.19
  610.6 3.1 pad_maximum_fusion.part_ref
  613.7 46.7 %scatter_kv.1 = bf16[256,1024]{1,0:T(8,128)(2,1)} custom-call(bf16[4,256,1024]{2,1,0:T(8,128)(2,1)} %pad_maximum_fusion.part_ref), custom_call_target="tpu_custom_call" | custom-call | bytes 100000000 | tf_op jit(solution)/shard_map/scatter_kv/pallas_call | solution.py:400
  665.4 5.1 convolution_multiply_fusion
  674.7 4.8 convolution_convert_fusion
  679.4 90.0 %reduce_weights.1 = (bf16[2,2,2,32,1664]{4,3,2,1,0:T(8,128)(2,1)S(1)}, bf16[2,2,2,32,1536]{4,3,2,1,0:T(8,128)(2,1)S(1)}) custom-call(bf16[4,2,2,2,32,2048]{5,4,3,2,1,0:T(8,128)(2,1)} %bitcast.121, bf16[4,2,2,2,32,1024]{5,4,3,2,1,0:T(8,128)(2,1)S(1)} %bitcast.107, bf16[4,2,2,2,32,128]{5,4,3,2,1,0:T(8,128)(2,1)S(1)} %maximum_maximum_fusion.refs_2_), custom_call_target="tpu_custom_call" | custom-call | bytes 100000000 | tf_op jit(solution)/shard_map/reduce_weights/pallas_call | solution.py:775
  775.7 11.9 %convert_element_type.193 = f32[8,1024,512]{2,1,0:T(8,128)} convert(bf16[8,1024,512]{2,1,0:T(8,128)(2,1)} %all-gather.7.cloned.1.call-done) | non-fusion elementwise | flops 4194304 | bytes 25165824 | tf_op jit(solution)/shard_map/convert_element_type | solution.py:985
  787.6 11.9 %convert_element_type.194 = f32[8,1024,512]{2,1,0:T(8,128)} convert(bf16[8,1024,512]{2,1,0:T(8,128)(2,1)} %all-gather.9.cloned.1.call-done) | non-fusion elementwise | flops 4194304 | bytes 25165824 | tf_op jit(solution)/shard_map/convert_element_type | solution.py:985
  799.5 11.7 %convert_element_type.195 = f32[8,512,1024]{2,1,0:T(8,128)} convert(bf16[8,512,1024]{2,1,0:T(8,128)(2,1)} %all-gather.11.cloned.1.call-done) | non-fusion elementwise | flops 4194304 | bytes 25165824 | tf_op jit(solution)/shard_map/convert_element_type | solution.py:985
  (157 shorter events, 62.7 us)
Async XLA Ops:
  7.2 196.6 %all-gather.5.cloned.1.call-start = ((), (), s32[]{:S(2)}) async-start(), calls=%async_computation.4 | async-start | bytes 2621440 | tf_op jit(solution)/shard_map/all_gather | solution.py:795
  9.9 317.3 %reduce-scatter.7.cloned.1.call-start = ((), (), s32[]{:S(2)}) async-start(), calls=%async_computation.6 | async-start | bytes 9437184 | tf_op jit(solution)/shard_map/reduce_scatter | solution.py:984
  11.4 77.6 %copy-start.26 = (s32[256,8]{0,1:T(8,128)S(1)}, s32[256,8]{0,1:T(8,128)}, u32[]{:S(2)}) copy-start(s32[256,8]{0,1:T(8,128)} %param.16) | copy-start | bytes 24580
  136.3 10.2 %copy-start.3 = (bf16[1024,512]{0,1:T(8,128)(2,1)}, bf16[1024,512]{0,1:T(8,128)(2,1)S(1)}, u32[]{:S(2)}) copy-start(bf16[1024,512]{0,1:T(8,128)(2,1)S(1)} %copy.111) | copy-start | bytes 3145732
  136.8 9.7 %copy-start.11 = (bf16[256,16,32]{0,2,1:T(8,128)(2,1)}, bf16[256,16,32]{0,2,1:T(8,128)(2,1)S(1)}, u32[]{:S(2)}) copy-start(bf16[256,16,32]{0,2,1:T(8,128)(2,1)S(1)} %get-tuple-element.46) | copy-start | bytes 786436
  136.8 9.7 %copy-start.13 = (bf16[256,16,32]{0,2,1:T(8,128)(2,1)}, bf16[256,16,32]{0,2,1:T(8,128)(2,1)S(1)}, u32[]{:S(2)}) copy-start(bf16[256,16,32]{0,2,1:T(8,128)(2,1)S(1)} %get-tuple-element.47) | copy-start | bytes 786436
  138.5 16.6 %copy-start.18 = (bf16[1024,512]{0,1:T(8,128)(2,1)}, bf16[1024,512]{0,1:T(8,128)(2,1)S(1)}, u32[]{:S(2)}) copy-start(bf16[1024,512]{0,1:T(8,128)(2,1)S(1)} %copy.113) | copy-start | bytes 3145732
  138.7 16.4 %copy-start.9 = (pred[256,1024]{0,1:T(8,128)(4,1)}, pred[256,1024]{0,1:T(8,128)(4,1)S(1)}, u32[]{:S(2)}) copy-start(pred[256,1024]{0,1:T(8,128)(4,1)S(1)} %fusion.33) | copy-start | bytes 786436
  155.1 8.4 %copy-start.5 = (bf16[4,2,2,2,32,1024]{5,4,3,2,1,0:T(8,128)(2,1)S(1)}, bf16[4,2,2,2,32,1024]{5,4,3,2,1,0:T(8,128)(2,1)}, u32[]{:S(2)}) copy-start(bf16[4,2,2,2,32,1024]{5,4,3,2,1,0:T(8,128)(2,1)} %get-tuple-element.27) | copy-start | bytes 6291460
  163.5 38.0 %copy-start.7 = (bf16[4,2,2,2,32,128]{5,4,3,2,1,0:T(8,128)(2,1)S(1)}, bf16[4,2,2,2,32,128]{5,4,3,2,1,0:T(8,128)(2,1)}, u32[]{:S(2)}) copy-start(bf16[4,2,2,2,32,128]{5,4,3,2,1,0:T(8,128)(2,1)} %get-tuple-element.24) | copy-start | bytes 786436
  163.5 38.7 %copy-start.23 = (bf16[4,32,256]{2,1,0:T(8,128)(2,1)S(1)}, bf16[4,32,256]{2,1,0:T(8,128)(2,1)}, u32[]{:S(2)}) copy-start(bf16[4,32,256]{2,1,0:T(8,128)(2,1)} %get-tuple-element.28) | copy-start | bytes 196612
  256.6 146.0 %reduce-scatter.9.cloned.1.call-start = ((), (), s32[]{:S(2)}) async-start(), calls=%async_computation.8 | async-start | bytes 9437184 | tf_op jit(solution)/shard_map/reduce_scatter | solution.py:984
  257.3 220.2 %copy-start.6 = (bf16[256,1024]{1,0:T(8,128)(2,1)S(1)}, bf16[256,1024]{1,0:T(8,128)(2,1)}, u32[]{:S(2)}) copy-start(bf16[256,1024]{1,0:T(8,128)(2,1)} %multiply_convert_fusion.refs_0_) | copy-start | bytes 1572868
  257.3 220.0 %reduce-scatter.11.cloned.1.call-start = ((), (), s32[]{:S(2)}) async-start(), calls=%async_computation.10 | async-start | bytes 9437184 | tf_op jit(solution)/shard_map/reduce_scatter | solution.py:984
  257.9 311.4 %reduce-scatter.5.cloned.1.call-start = ((), (), s32[]{:S(2)}) async-start(), calls=%async_computation.5 | async-start | bytes 2621440 | tf_op jit(solution)/shard_map/reduce_scatter | solution.py:799
  258.5 517.2 %all-gather.7.cloned.1.call-start = ((), (), s32[]{:S(2)}) async-start(), calls=%async_computation.7 | async-start | bytes 9437184 | tf_op jit(solution)/shard_map/all_gather | solution.py:985
  327.2 460.4 %all-gather.9.cloned.1.call-start = ((), (), s32[]{:S(2)}) async-start(), calls=%async_computation.9 | async-start | bytes 9437184 | tf_op jit(solution)/shard_map/all_gather | solution.py:985
  402.7 396.8 %all-gather.11.cloned.1.call-start = ((), (), s32[]{:S(2)}) async-start(), calls=%async_computation.11 | async-start | bytes 9437184 | tf_op jit(solution)/shard_map/all_gather | solution.py:985
  561.7 14.0 %copy-start.10 = (pred[256,1024]{0,1:T(8,128)(4,1)S(1)}, pred[256,1024]{0,1:T(8,128)(4,1)}, u32[]{:S(2)}) copy-start(pred[256,1024]{0,1:T(8,128)(4,1)} %copy-done.9) | copy-start | bytes 786436
  572.0 101.9 %copy-start.1 = (f32[256,1024]{1,0:T(8,128)}, f32[256,1024]{1,0:T(8,128)S(1)}, u32[]{:S(2)}) copy-start(f32[256,1024]{1,0:T(8,128)S(1)} %get-tuple-element.50) | copy-start | bytes 3145732
  589.3 12.5 %copy-start.12 = (bf16[256,16,32]{0,2,1:T(8,128)(2,1)S(1)}, bf16[256,16,32]{0,2,1:T(8,128)(2,1)}, u32[]{:S(2)}) copy-start(bf16[256,16,32]{0,2,1:T(8,128)(2,1)} %copy-done.11) | copy-start | bytes 786436
  589.3 12.5 %copy-start.14 = (bf16[256,16,32]{0,2,1:T(8,128)(2,1)S(1)}, bf16[256,16,32]{0,2,1:T(8,128)(2,1)}, u32[]{:S(2)}) copy-start(bf16[256,16,32]{0,2,1:T(8,128)(2,1)} %copy-done.13) | copy-start | bytes 786436
  605.4 59.9 %copy-start.4 = (bf16[1024,512]{0,1:T(8,128)(2,1)S(1)}, bf16[1024,512]{0,1:T(8,128)(2,1)}, u32[]{:S(2)}) copy-start(bf16[1024,512]{0,1:T(8,128)(2,1)} %copy-done.3) | copy-start | bytes 3145732
  679.4 95.0 %copy-start.2 = (f32[256,1024]{1,0:T(8,128)S(1)}, f32[256,1024]{1,0:T(8,128)}, u32[]{:S(2)}) copy-start(f32[256,1024]{1,0:T(8,128)} %copy-done.1) | copy-start | bytes 3145732
  (12 other events, 49.2 us)
Sparse Core Ops, SparseCore 0:
  10.1 56.1 all-gather.4
  256.7 70.3 reduce-scatter.6
  331.2 71.3 reduce-scatter.8
  405.9 71.3 reduce-scatter.10
  479.5 75.0 reduce-scatter.4
  556.4 54.3 all-gather.6
  612.7 54.2 all-gather.8
  668.9 73.1 all-gather.10

commit v3 on v2

--- a/solution.py
+++ b/solution.py
@@ -52,162 +52,6 @@
 
 def dot_tn(a, b):
     return lax.dot_general(a, b, (((0,), (0,)), ((), ())), preferred_element_type=F32)
-
-
-def expert_kernel(
-    sizes,
-    x_ref,
-    ct_ref,
-    router_t_ref,
-    rank_row_ref,
-    rank_col_ref,
-    w_gate_ref,
-    w_up_ref,
-    w_down_ref,
-    y_ref,
-    gs_ref,
-    grad_gate_ref,
-    grad_up_ref,
-    grad_down_ref,
-    xs_ref,
-    g_ref,
-    gate_slot_ref,
-    dots_ref,
-):
-    blocks, rows, local, capacity = sizes
-    slots = local * capacity
-    step = pl.program_id(0)
-    base = lax.axis_index("expert") * local
-
-    @pl.when(step == 0)
-    def _():
-        logits = dot_nt(router_t_ref[...], x_ref[...])
-        hot = rank_row_ref[...] < 200.0
-        top = jnp.max(jnp.where(hot, logits, NEGATIVE_LARGE), axis=0, keepdims=True)
-        weight = jnp.where(hot, jnp.exp(jnp.minimum(logits - top, 0.0)), 0.0)
-        gates = weight / jnp.sum(weight, axis=0, keepdims=True)
-        expert_id = lax.broadcasted_iota(jnp.int32, gates.shape, 0)
-        slot_id = lax.broadcasted_iota(jnp.int32, (capacity, rows), 0).astype(F32)
-        rank_rows, gate_rows = [], []
-        for e in range(local):
-            mine = expert_id == base + e
-            rank_rows.append(jnp.sum(jnp.where(mine, rank_row_ref[...], 0.0), 0, keepdims=True))
-            gate_rows.append(jnp.sum(jnp.where(mine, gates, 0.0), 0, keepdims=True))
-        for b in range(blocks):
-            here = slice(b * rows, (b + 1) * rows)
-            pieces = []
-            for e in range(local):
-                taken = jnp.broadcast_to(rank_rows[e][:, here], (capacity, rows)) == slot_id
-                gate = jnp.sum(jnp.where(taken, gate_rows[e][:, here], 0.0), 1, keepdims=True)
-                gate_slot_ref[b, e * capacity : (e + 1) * capacity, :] = gate
-                pieces.append(jnp.where(taken, 1.0, 0.0).astype(BF))
-            pick = jnp.concatenate(pieces, axis=0)
-            xs_ref[b] = dot(pick, x_ref[here, :]).astype(BF)
-            g_ref[b] = dot(pick, ct_ref[here, :]).astype(BF)
-
-    here = pl.ds(pl.multiple_of(step * capacity, capacity), capacity)
-    xs = jnp.concatenate([xs_ref[b, here, :] for b in range(blocks)], axis=0)
-    g = jnp.concatenate([g_ref[b, here, :] for b in range(blocks)], axis=0).astype(F32)
-    gate_slot = jnp.concatenate([gate_slot_ref[b, here, :] for b in range(blocks)], axis=0)
-    w_gate, w_up, w_down = w_gate_ref[0], w_up_ref[0], w_down_ref[0]
-    gate_pre = dot(xs, w_gate)
-    up_pre = dot(xs, w_up)
-    sigmoid = jax.nn.sigmoid(gate_pre)
-    silu = gate_pre * sigmoid
-    activation = (silu * up_pre).astype(BF)
-    expert_out = dot(activation, w_down).astype(BF).astype(F32)
-    slot_dot = jnp.sum(g * expert_out, axis=1, keepdims=True)
-    grad_out = (gate_slot * g).astype(BF)
-    scaled_out = (gate_slot * expert_out).astype(BF)
-    grad_down_ref[0] = dot_tn(activation, grad_out).astype(BF)
-    grad_activation = dot_nt(grad_out, w_down)
-    grad_gate_pre = (
-        grad_activation * up_pre * sigmoid * (1.0 + gate_pre * (1.0 - sigmoid))
-    ).astype(BF)
-    grad_up_pre = (grad_activation * silu).astype(BF)
-    grad_gate_ref[0] = dot_tn(xs, grad_gate_pre).astype(BF)
-    grad_up_ref[0] = dot_tn(xs, grad_up_pre).astype(BF)
-    grad_in = (dot_nt(grad_gate_pre, w_gate) + dot_nt(grad_up_pre, w_up)).astype(BF)
-    lane = lax.broadcasted_iota(jnp.int32, (blocks * capacity, LANES), 1)
-    high = slot_dot.astype(BF).astype(F32)
-    middle = (slot_dot - high).astype(BF).astype(F32)
-    low = slot_dot - high - middle
-    mine = base + step
-    dots = jnp.where(lane == mine, high, 0.0)
-    dots = jnp.where(lane == mine + EXPERTS, middle, dots)
-    dots = jnp.where(lane == mine + 2 * EXPERTS, low, dots).astype(BF)
-    for b in range(blocks):
-        part = slice(b * capacity, (b + 1) * capacity)
-        xs_ref[b, here, :] = grad_in[part]
-        g_ref[b, here, :] = scaled_out[part]
-        dots_ref[b, here, :] = dots[part]
-
-    @pl.when(step == local - 1)
-    def _():
-        slot_expert = lax.broadcasted_iota(jnp.int32, (EXPERTS, slots), 1) // capacity
-        spread_row = lax.broadcasted_iota(jnp.int32, (EXPERTS, slots), 0)
-        spread = jnp.where(spread_row == slot_expert + base, 1.0, 0.0).astype(BF)
-        slot_rank = (lax.broadcasted_iota(jnp.int32, (rows, slots), 1) % capacity).astype(F32)
-        for b in range(blocks):
-            there = slice(b * rows, (b + 1) * rows)
-            ranks = dot(rank_col_ref[there, :], spread)
-            put = jnp.where(ranks == slot_rank, 1.0, 0.0).astype(BF)
-            y_ref[there, :] = dot(put, g_ref[b]).astype(BF)
-            gs_ref[there, :D] = dot(put, xs_ref[b]).astype(BF)
-            gs_ref[there, D:] = dot(put, dots_ref[b]).astype(BF)
-
-
-def run_experts(x_all, ct_all, router_t, rank_row, rank_col, w_gate, w_up, w_down, rows, capacity):
-    total = x_all.shape[0]
-    blocks, local = total // rows, w_gate.shape[0]
-    slots = local * capacity
-    sizes = (blocks, rows, local, capacity)
-    whole = lambda shape: pl.BlockSpec(
-        shape, lambda e: (0,) * len(shape), pipeline_mode=pl.Buffered(1)
-    )
-    per = lambda shape: pl.BlockSpec((1,) + shape, lambda e: (e, 0, 0))
-    flops = 2 * total * D * slots * 4 // blocks + 18 * blocks * slots * D * FF
-    return pl.pallas_call(
-        functools.partial(expert_kernel, sizes),
-        grid=(local,),
-        out_shape=(
-            jax.ShapeDtypeStruct((total, D), BF),
-            jax.ShapeDtypeStruct((total, D + LANES), BF),
-            jax.ShapeDtypeStruct((local, D, FF), BF),
-            jax.ShapeDtypeStruct((local, D, FF), BF),
-            jax.ShapeDtypeStruct((local, FF, D), BF),
-        ),
-        in_specs=[
-            whole((total, D)),
-            whole((total, D)),
-            whole((EXPERTS, D)),
-            whole((EXPERTS, total)),
-            whole((total, EXPERTS)),
-            per((D, FF)),
-            per((D, FF)),
-            per((FF, D)),
-        ],
-        out_specs=(
-            whole((total, D)),
-            whole((total, D + LANES)),
-            per((D, FF)),
-            per((D, FF)),
-            per((FF, D)),
-        ),
-        scratch_shapes=[
-            pltpu.VMEM((blocks, slots, D), BF),
-            pltpu.VMEM((blocks, slots, D), BF),
-            pltpu.VMEM((blocks, slots, 1), F32),
-            pltpu.VMEM((blocks, slots, LANES), BF),
-        ],
-        compiler_params=pltpu.CompilerParams(
-            dimension_semantics=("arbitrary",), vmem_limit_bytes=62 * 1024 * 1024
-        ),
-        cost_estimate=pl.CostEstimate(
-            flops=flops, bytes_accessed=2 * (6 * local * D * FF + 4 * total * D), transcendentals=0
-        ),
-        name="experts",
-    )(x_all, ct_all, router_t, rank_row, rank_col, w_gate, w_up, w_down)
 
 
 MESH = pl.DeviceIdType.MESH
@@ -791,6 +635,263 @@
     return qkv, second[:, rest:], first[:, cut:]
 
 
+def expert_kernel(sizes, plane, *refs):
+    blocks, rows, local, capacity = sizes
+    x_ref, ct_ref, router_t_ref, rank_row_ref, rank_col_ref = refs[:5]
+    w_gate_ref, w_up_ref, w_down_ref = refs[5:8]
+    y_ref, gs_ref, out_gate_ref, out_up_ref, out_down_ref = refs[8:13]
+    xs_ref, g_ref, gate_slot_ref, dots_ref = refs[13:17]
+    slots = local * capacity
+    step = pl.program_id(0)
+    base = lax.axis_index("expert") * local
+    if plane:
+        stage_refs, pair_refs, one_refs, two_refs = refs[17:20], refs[20:23], refs[23:27], refs[27:31]
+        csend, crecv, psend, precv, qsend, qrecv = refs[31:]
+        _, _, (y, x, c), (by_y, by_x, by_c) = plane_position()
+        half = stage_refs[2].shape[4] // 2
+
+        @pl.when(step == 0)
+        def _():
+            greet([(None, by_c), (None, by_x), (None, by_y)])
+
+    @pl.when(step == 0)
+    def _():
+        logits = dot_nt(router_t_ref[...], x_ref[...])
+        hot = rank_row_ref[...] < 200.0
+        top = jnp.max(jnp.where(hot, logits, NEGATIVE_LARGE), axis=0, keepdims=True)
+        weight = jnp.where(hot, jnp.exp(jnp.minimum(logits - top, 0.0)), 0.0)
+        gates = weight / jnp.sum(weight, axis=0, keepdims=True)
+        expert_id = lax.broadcasted_iota(jnp.int32, gates.shape, 0)
+        slot_id = lax.broadcasted_iota(jnp.int32, (capacity, rows), 0).astype(F32)
+        rank_rows, gate_rows = [], []
+        for e in range(local):
+            mine = expert_id == base + e
+            rank_rows.append(jnp.sum(jnp.where(mine, rank_row_ref[...], 0.0), 0, keepdims=True))
+            gate_rows.append(jnp.sum(jnp.where(mine, gates, 0.0), 0, keepdims=True))
+        for b in range(blocks):
+            here = slice(b * rows, (b + 1) * rows)
+            pieces = []
+            for e in range(local):
+                taken = jnp.broadcast_to(rank_rows[e][:, here], (capacity, rows)) == slot_id
+                gate = jnp.sum(jnp.where(taken, gate_rows[e][:, here], 0.0), 1, keepdims=True)
+                gate_slot_ref[b, e * capacity : (e + 1) * capacity, :] = gate
+                pieces.append(jnp.where(taken, 1.0, 0.0).astype(BF))
+            pick = jnp.concatenate(pieces, axis=0)
+            xs_ref[b] = dot(pick, x_ref[here, :]).astype(BF)
+            g_ref[b] = dot(pick, ct_ref[here, :]).astype(BF)
+
+    @pl.when(step < local)
+    def _():
+        here = pl.ds(pl.multiple_of(step * capacity, capacity), capacity)
+        xs = jnp.concatenate([xs_ref[b, here, :] for b in range(blocks)], axis=0)
+        g = jnp.concatenate([g_ref[b, here, :] for b in range(blocks)], axis=0).astype(F32)
+        gate_slot = jnp.concatenate([gate_slot_ref[b, here, :] for b in range(blocks)], axis=0)
+        w_gate, w_up, w_down = w_gate_ref[0], w_up_ref[0], w_down_ref[0]
+        gate_pre = dot(xs, w_gate)
+        up_pre = dot(xs, w_up)
+        sigmoid = jax.nn.sigmoid(gate_pre)
+        silu = gate_pre * sigmoid
+        activation = (silu * up_pre).astype(BF)
+        expert_out = dot(activation, w_down).astype(BF).astype(F32)
+        slot_dot = jnp.sum(g * expert_out, axis=1, keepdims=True)
+        grad_out = (gate_slot * g).astype(BF)
+        scaled_out = (gate_slot * expert_out).astype(BF)
+        grad_down = dot_tn(activation, grad_out).astype(BF)
+        grad_activation = dot_nt(grad_out, w_down)
+        grad_gate_pre = (
+            grad_activation * up_pre * sigmoid * (1.0 + gate_pre * (1.0 - sigmoid))
+        ).astype(BF)
+        grad_up_pre = (grad_activation * silu).astype(BF)
+        grad_gate = dot_tn(xs, grad_gate_pre).astype(BF)
+        grad_up = dot_tn(xs, grad_up_pre).astype(BF)
+        if plane:
+            for ref, value in zip(stage_refs, (grad_gate, grad_up, grad_down)):
+                ref[step % 2] = value.reshape(ref.shape[1:])
+        else:
+            out_gate_ref[0], out_up_ref[0], out_down_ref[0] = grad_gate, grad_up, grad_down
+        grad_in = (dot_nt(grad_gate_pre, w_gate) + dot_nt(grad_up_pre, w_up)).astype(BF)
+        lane = lax.broadcasted_iota(jnp.int32, (blocks * capacity, LANES), 1)
+        high = slot_dot.astype(BF).astype(F32)
+        middle = (slot_dot - high).astype(BF).astype(F32)
+        low = slot_dot - high - middle
+        mine = base + step
+        dots = jnp.where(lane == mine, high, 0.0)
+        dots = jnp.where(lane == mine + EXPERTS, middle, dots)
+        dots = jnp.where(lane == mine + 2 * EXPERTS, low, dots).astype(BF)
+        for b in range(blocks):
+            part = slice(b * capacity, (b + 1) * capacity)
+            xs_ref[b, here, :] = grad_in[part]
+            g_ref[b, here, :] = scaled_out[part]
+            dots_ref[b, here, :] = dots[part]
+
+    @pl.when(step == (local if plane else local - 1))
+    def _():
+        slot_expert = lax.broadcasted_iota(jnp.int32, (EXPERTS, slots), 1) // capacity
+        spread_row = lax.broadcasted_iota(jnp.int32, (EXPERTS, slots), 0)
+        spread = jnp.where(spread_row == slot_expert + base, 1.0, 0.0).astype(BF)
+        slot_rank = (lax.broadcasted_iota(jnp.int32, (rows, slots), 1) % capacity).astype(F32)
+        for b in range(blocks):
+            there = slice(b * rows, (b + 1) * rows)
+            ranks = dot(rank_col_ref[there, :], spread)
+            put = jnp.where(ranks == slot_rank, 1.0, 0.0).astype(BF)
+            y_ref[there, :] = dot(put, g_ref[b]).astype(BF)
+            gs_ref[there, :D] = dot(put, xs_ref[b]).astype(BF)
+            gs_ref[there, D:] = dot(put, dots_ref[b]).astype(BF)
+
+    if not plane:
+        return
+
+    gate, up, low_down, high_down = range(4)
+    low_rows, high_rows = slice(0, half), slice(half, 2 * half)
+
+    def swap(e, i):
+        slot = e % 2
+        return remote(
+            stage_refs[i].at[slot, :, :, 1 - c],
+            pair_refs[i].at[e % 3],
+            csend.at[slot, i],
+            crecv.at[e % 3, i],
+            by_c,
+        )
+
+    def first(e, k):
+        slot = e % 3
+        source = {
+            gate: lambda: pair_refs[0].at[slot, :, 1 - x],
+            up: lambda: pair_refs[1].at[slot, 1 - y],
+            low_down: lambda: pair_refs[2].at[slot, :, 1 - x, low_rows],
+            high_down: lambda: pair_refs[2].at[slot, 1 - y, :, high_rows],
+        }[k]()
+        device = by_x if k in (gate, low_down) else by_y
+        return remote(source, one_refs[k].at[slot], psend.at[slot, k], precv.at[slot, k], device)
+
+    def second(e, k):
+        along_x = k in (gate, low_down)
+        source = one_refs[k].at[e % 3, 1 - y] if along_x else one_refs[k].at[e % 3, 1 - x]
+        slot = e % 2
+        return remote(
+            source,
+            two_refs[k].at[slot],
+            qsend.at[slot, k],
+            qrecv.at[slot, k],
+            by_y if along_x else by_x,
+        )
+
+    def add(first_value, second_value):
+        return (first_value.astype(F32) + second_value.astype(F32)).astype(BF)
+
+    @pl.when(step >= 3)
+    def _():
+        e = step - 3
+        for k in range(4):
+            second(e, k).wait()
+        own = [one_refs[k][e % 3, y if k in (gate, low_down) else x] for k in range(4)]
+        out_gate_ref[0] = add(own[gate], two_refs[gate][e % 2])
+        out_up_ref[0] = add(own[up], two_refs[up][e % 2])
+        out_down_ref[0, low_rows] = add(own[low_down], two_refs[low_down][e % 2])
+        out_down_ref[0, high_rows] = add(own[high_down], two_refs[high_down][e % 2])
+
+    @pl.when((step >= 2) & (step < local + 2))
+    def _():
+        e = step - 2
+        slot = e % 3
+        for k in range(4):
+            first(e, k).wait()
+            for t in (0, 1):
+                mine = {
+                    gate: lambda: pair_refs[0][slot, t, x],
+                    up: lambda: pair_refs[1][slot, y, t],
+                    low_down: lambda: pair_refs[2][slot, t, x, low_rows],
+                    high_down: lambda: pair_refs[2][slot, y, t, high_rows],
+                }[k]()
+                one_refs[k][slot, t] = add(mine, one_refs[k][slot, t])
+            second(e, k).start()
+
+    @pl.when((step >= 1) & (step < local + 1))
+    def _():
+        e = step - 1
+        slot = e % 3
+        for i in range(3):
+            swap(e, i).wait()
+
+            def pair_sum(t, carry):
+                a, b = t // 2, t % 2
+                pair_refs[i][slot, a, b] = add(
+                    stage_refs[i][e % 2, a, b, c], pair_refs[i][slot, a, b]
+                )
+                return carry
+
+            lax.fori_loop(0, 4, pair_sum, 0)
+        for k in range(4):
+            first(e, k).start()
+
+    @pl.when(step < local)
+    def _():
+        for i in range(3):
+            swap(step, i).start()
+
+
+def run_experts(
+    x_all, ct_all, router_t, rank_row, rank_col, w_gate, w_up, w_down, rows, capacity, plane, collective_id
+):
+    total = x_all.shape[0]
+    blocks, local = total // rows, w_gate.shape[0]
+    slots = local * capacity
+    sizes = (blocks, rows, local, capacity)
+    whole = lambda shape: pl.BlockSpec(
+        shape, lambda e: (0,) * len(shape), pipeline_mode=pl.Buffered(1)
+    )
+    per = lambda shape: pl.BlockSpec((1,) + shape, lambda e: (jnp.minimum(e, local - 1), 0, 0))
+    shapes = ((D, FF), (D, FF), (FF, D))
+    scratch = [
+        pltpu.VMEM((blocks, slots, D), BF),
+        pltpu.VMEM((blocks, slots, D), BF),
+        pltpu.VMEM((blocks, slots, 1), F32),
+        pltpu.VMEM((blocks, slots, LANES), BF),
+    ]
+    params = dict(dimension_semantics=("arbitrary",), vmem_limit_bytes=62 * 1024 * 1024)
+    if plane:
+        eighths = [(a // 8, b) for a, b in shapes]
+        out = lambda shape: pl.BlockSpec((1,) + shape, lambda e: (jnp.maximum(e - 3, 0), 0, 0))
+        grad_shapes, grad_specs = eighths, [out(shape) for shape in eighths]
+        low = (eighths[2][0] // 2, eighths[2][1])
+        passed = (eighths[0], eighths[1], low, low)
+        scratch += [pltpu.VMEM((2, 2, 2, 2) + shape, BF) for shape in eighths]
+        scratch += [pltpu.VMEM((3, 2, 2) + shape, BF) for shape in eighths]
+        scratch += [pltpu.VMEM((3, 2) + shape, BF) for shape in passed]
+        scratch += [pltpu.VMEM((2,) + shape, BF) for shape in passed]
+        sems = [(2, 3), (3, 3), (3, 4), (3, 4), (2, 4), (2, 4)]
+        scratch += [pltpu.SemaphoreType.DMA(shape) for shape in sems]
+        params |= dict(collective_id=collective_id, has_side_effects=True)
+    else:
+        grad_shapes, grad_specs = shapes, [per(shape) for shape in shapes]
+    flops = 2 * total * D * slots * 4 // blocks + 18 * blocks * slots * D * FF
+    return pl.pallas_call(
+        functools.partial(expert_kernel, sizes, plane),
+        grid=(local + 3 if plane else local,),
+        out_shape=[
+            jax.ShapeDtypeStruct((total, D), BF),
+            jax.ShapeDtypeStruct((total, D + LANES), BF),
+        ]
+        + [jax.ShapeDtypeStruct((local,) + shape, BF) for shape in grad_shapes],
+        in_specs=[
+            whole((total, D)),
+            whole((total, D)),
+            whole((EXPERTS, D)),
+            whole((EXPERTS, total)),
+            whole((total, EXPERTS)),
+        ]
+        + [per(shape) for shape in shapes],
+        out_specs=[whole((total, D)), whole((total, D + LANES))] + grad_specs,
+        scratch_shapes=scratch,
+        compiler_params=pltpu.CompilerParams(**params),
+        cost_estimate=pl.CostEstimate(
+            flops=flops, bytes_accessed=2 * (6 * local * D * FF + 4 * total * D), transcendentals=0
+        ),
+        name="experts",
+    )(x_all, ct_all, router_t, rank_row, rank_col, w_gate, w_up, w_down)
+
+
 def gather_rows(value):
     return lax.all_gather(value, "expert", axis=0, tiled=True)
 
@@ -897,7 +998,7 @@
     (x_all,) = line_gather([second_norm], n, 3, "gather_rows")
 
     y_part, gs_part, grad_gate, grad_up, grad_down = run_experts(
-        x_all, ct_all, router_weight.T, rank_row, rank_col, w_gate, w_up, w_down, rows, capacity
+        x_all, ct_all, router_weight.T, rank_row, rank_col, w_gate, w_up, w_down, rows, capacity, groups == 8, 7
     )
     gs = line_scatter(gs_part, n, F32, 4, "scatter_grads")
     expert_sum = scatter_rows(y_part).astype(F32)
@@ -980,9 +1081,10 @@
         shares = [lax.psum(scatter_rows(share), "group") for share in shares]
     share_qkv, share_out, share_small = [share.astype(F32) for share in shares]
 
-    def sum_over_groups(value, axis):
-        part = lax.psum_scatter(value, "group", scatter_dimension=axis, tiled=True)
-        return lax.all_gather(part, "group", axis=axis, tiled=True).astype(F32)
+    def sum_over_groups(value):
+        if groups != 8:
+            value = lax.psum_scatter(value, "group", scatter_dimension=1, tiled=True)
+        return lax.all_gather(value, "group", axis=1, tiled=True).astype(F32)
 
     return (
         mixed,
@@ -994,9 +1096,9 @@
         share_out,
         share_small[:, EXPERTS + 1],
         share_small[:, :EXPERTS],
-        sum_over_groups(grad_gate, 1),
-        sum_over_groups(grad_up, 1),
-        sum_over_groups(grad_down, 1),
+        sum_over_groups(grad_gate),
+        sum_over_groups(grad_up),
+        sum_over_groups(grad_down),
     )
 
 

time: 824 us -> 670 us (0.81)
  waiting for transfers between devices: 220 us -> 1.8 us
  Pallas kernels: 420 us -> 485 us
    reduce_scatter x3 -> x0, waiting for transfers between devices: 218 us -> none  [sum_over_groups(): part = lax.psum_scatter(value, 'group', scatter_dimension=axis, tiled=True)]
    pallas_call x1, Pallas kernels: 52.8 us -> 125 us  [run_experts(): pl.pallas_call(functools.partial(expert_kernel, sizes, plane), grid=(loca...]
  transfers between devices with their start and end apart: 8 -> 5, of which waited for: 3 -> 0; matrix products, arithmetic and copies ran while one was open for 18% -> 22% of each run, Pallas kernels for 45% -> 54%
where the time goes in v3:
time: 670 us; the launch traced here: 664 us
  Pallas kernels  485 us (72%)
  other arithmetic  69.5 us (10%)
  matrix products  60.6 us (9%)
  local copies, waits for them, and re-layouts  31.5 us (5%)
  between operations  15.4 us (2%)
    pallas_call x2, Pallas kernels, line_scatter(): pl.pallas_call(functools.partial(line_scatter_kernel, n), out_shape=jax.S...  129 us
    pallas_call x1, Pallas kernels, run_experts(): pl.pallas_call(functools.partial(expert_kernel, sizes, plane), grid=(loca...  125 us
    pallas_call x1, Pallas kernels, reduce_weights(): pl.pallas_call(functools.partial(reduce_kernel, n, pieces), out_shape=[ja...  84.3 us
    pallas_call x2, Pallas kernels, line_gather(): pl.pallas_call(functools.partial(line_gather_kernel, n, count), out_shape...  79.7 us
    pallas_call x1, Pallas kernels, gather_weights(): pl.pallas_call(functools.partial(weights_kernel, n, pieces, widths), out_...  67.1 us
    convert_element_type x3, other arithmetic, sum_over_groups(): return lax.all_gather(value, 'group', axis=1, tiled=True).astype(F32)  35.5 us
  transfers between devices with their start and end apart: 5, of which 0 were waited for; matrix products, arithmetic and copies ran while one was open for 22% of the time, Pallas kernels for 54%

profile of v3, /device:TPU:0, one launch (start us, length us, event | category | flops | bytes accessed | tf_op | source)
XLA Modules:
  0.0 664.4 jit_solution(5938858713233179081)
XLA Ops:
  14.4 67.1 %gather_weights.1 = (bf16[4,2,2,2,32,2048]{5,4,3,2,1,0:T(8,128)(2,1)}, bf16[4,2,2,2,32,1024]{5,4,3,2,1,0:T(8,128)(2,1)}, bf16[4,2,2,2,32,128]{5,4,3,2,1,0:T(8,128)(2,1)}) custom-call(bf16[256,1024]{1,0:T(8,128)(2,1)} %refs_0_.1, bf16[256,512]{1,0:T(8,128)(2,1)} %refs_1_.1, bf16[256,512]{1,0:T(8,128)(2,1)} %refs_2_.1, bf16[256,1024]{1,0:T(8,128)(2,1)} %refs_3_.1, ...), custom_call_target="tpu_custom_call" | custom-call | bytes 100000000 | tf_op jit(solution)/shard_map/gather_weights/pallas_call | solution.py:423
  83.0 3.6 fusion.39
  93.0 43.4 %gather_kv.1 = (bf16[4,256,1024]{2,1,0:T(8,128)(2,1)}, bf16[4,32,256]{2,1,0:T(8,128)(2,1)}) custom-call(bf16[256,1024]{1,0:T(8,128)(2,1)} %pad_maximum_fusion.2.refs_0_, bf16[32,256]{1,0:T(8,128)(2,1)} %fusion.23.refs_1_), custom_call_target="tpu_custom_call" | custom-call | bytes 100000000 | tf_op jit(solution)/shard_map/gather_kv/pallas_call | solution.py:152
  136.4 2.6 fusion.54
  140.8 8.8 %fusion.56 = (f32[8,2,256]{2,1,0:T(2,128)S(1)}, f32[8,2,256,1024]{2,3,1,0:T(8,128)}) fusion(bf16[1024,8,64,1]{0,2,3,1:T(8,128)(2,1)S(1)} %bitcast.112, bf16[256,8,2,32]{0,3,2,1:T(8,128)(2,1)} %bitcast.125, bf16[256,8,2,32]{0,3,2,1:T(8,128)(2,1)} %bitcast.123, pred[256,1024]{0,1:T(8,128)(4,1)S(1)} %fusion.33), kind=kOutput, calls=%fused_computation.117 | convolution fusion | flops 550498304 | bytes 18628608 | tf_op jit(solution)/shard_map/qhgd,khd->hgqk/dot_general | solution.py:977
  151.7 9.0 %fusion.2 = f32[8,2,256]{2,1,0:T(2,128)S(1)} fusion(f32[8,2,256,1024]{2,3,1,0:T(8,128)} %get-tuple-element.62, f32[8,2,256]{2,1,0:T(2,128)S(1)} %get-tuple-element.61, pred[256,1024]{0,1:T(8,128)(4,1)S(1)} %fusion.33), kind=kLoop, calls=%fused_computation.6 | loop fusion | flops 12578816 | bytes 17072128 | tf_op jit(solution)/shard_map/reduce_sum | solution.py:985
  160.7 8.4 %fusion.32 = (bf16[256,8,2,64]{0,3,2,1:T(8,128)(2,1)S(1)}, f32[8,2,256,64]{2,3,1,0:T(8,128)}) fusion(f32[256,8,2]{0,2,1:T(2,128)S(1)} %bitcast.146, bf16[1024,8,64,1]{0,2,3,1:T(8,128)(2,1)S(1)} %bitcast.136, f32[8,2,256,1024]{2,3,1,0:T(8,128)} %get-tuple-element.62, f32[8,2,256]{2,1,0:T(2,128)S(1)} %get-tuple-element.61, pred[256,1024]{0,1:T(8,128)(4,1)S(1)} %fusion.33), kind=kOutput, calls=%fused_computation.48 | convolution fusion | flops 549978112 | bytes 19693568 | tf_op jit(solution)/shard_map/hgqk,khd->hgqd/dot_general | solution.py:987
  170.9 36.2 %gather_rows.1 = bf16[4,256,1024]{2,1,0:T(8,128)(2,1)} custom-call(bf16[256,1024]{1,0:T(8,128)(2,1)} %multiply_convert_fusion.refs_0_), custom_call_target="tpu_custom_call" | custom-call | bytes 100000000 | tf_op jit(solution)/shard_map/gather_rows/pallas_call | solution.py:152
  207.2 125.0 %experts.1 = (bf16[1024,1024]{1,0:T(8,128)(2,1)}, bf16[1024,1152]{1,0:T(8,128)(2,1)}, bf16[8,128,512]{2,1,0:T(8,128)(2,1)}, bf16[8,128,512]{2,1,0:T(8,128)(2,1)}, bf16[8,64,1024]{2,1,0:T(8,128)(2,1)}) custom-call(bf16[1024,1024]{1,0:T(8,128)(2,1)} %bitcast.130, bf16[1024,1024]{1,0:T(8,128)(2,1)} %all-gather.5.cloned.1.call-done.refs_1_, ...), custom_call_target="tpu_custom_call" | custom-call | flops 30601641984 | bytes 58720256 | tf_op jit(solution)/shard_map/experts/pallas_call | solution.py:869
  334.8 81.9 %scatter_grads.1 = f32[256,1152]{1,0:T(8,128)} custom-call(bf16[4,256,1152]{2,1,0:T(8,128)(2,1)} %bitcast.127), custom_call_target="tpu_custom_call" | custom-call | bytes 100000000 | tf_op jit(solution)/shard_map/scatter_grads/pallas_call | solution.py:244
  420.6 2.6 multiply_reduce_fusion
  424.4 2.6 multiply_add_fusion
  431.3 8.6 %fusion.1 = bf16[8,2,256,1024]{2,3,1,0:T(8,128)(2,1)S(1)} fusion(f32[8,2,256,1024]{2,3,1,0:T(8,128)} %get-tuple-element.62, bf16[1024,8,64,1]{0,2,3,1:T(8,128)(2,1)} %bitcast.137, bf16[256,8,2,64]{0,3,2,1:T(8,128)(2,1)S(1)} %bitcast.131, f32[8,2,256]{2,1,0:T(2,128)S(1)} %fusion.31, f32[8,2,256]{2,1,0:T(2,128)S(1)} %bitcast.151, ...), kind=kOutput, calls=%fused_computation.2 | convolution fusion | flops 557842432 | bytes 27033600 | tf_op jit(solution)/shard_map/qhgd,khd->hgqk/dot_general | solution.py:1029
  439.9 3.4 copy-done
  443.3 2.6 fusion.19
  449.9 9.9 %fusion.20 = bf16[1024,8,64]{0,2,1:T(8,128)(2,1)} fusion(bf16[256,8,2,64]{0,3,2,1:T(8,128)(2,1)} %bitcast.132, f32[8,2,256,1024]{2,3,1,0:T(8,128)} %get-tuple-element.62, f32[8,2,256]{2,1,0:T(2,128)S(1)} %bitcast.152, pred[256,1024]{0,1:T(8,128)(4,1)S(1)} %copy-done.8), kind=kOutput, calls=%fused_computation.28 | convolution fusion | flops 549978112 | bytes 18628608 | tf_op jit(solution)/shard_map/hgqk,qhgd->khd/dot_general | solution.py:1039
  463.4 3.1 pad_maximum_fusion.part_ref
  466.5 47.3 %scatter_kv.1 = bf16[256,1024]{1,0:T(8,128)(2,1)} custom-call(bf16[4,256,1024]{2,1,0:T(8,128)(2,1)} %pad_maximum_fusion.part_ref), custom_call_target="tpu_custom_call" | custom-call | bytes 100000000 | tf_op jit(solution)/shard_map/scatter_kv/pallas_call | solution.py:244
  518.8 5.0 convolution_multiply_fusion
  528.2 3.5 convolution_convert_fusion
  531.7 84.3 %reduce_weights.1 = (bf16[2,2,2,32,1664]{4,3,2,1,0:T(8,128)(2,1)S(1)}, bf16[2,2,2,32,1536]{4,3,2,1,0:T(8,128)(2,1)S(1)}) custom-call(bf16[4,2,2,2,32,2048]{5,4,3,2,1,0:T(8,128)(2,1)} %bitcast.121, bf16[4,2,2,2,32,1024]{5,4,3,2,1,0:T(8,128)(2,1)S(1)} %bitcast.107, bf16[4,2,2,2,32,128]{5,4,3,2,1,0:T(8,128)(2,1)S(1)} %maximum_maximum_fusion.refs_2_), custom_call_target="tpu_custom_call" | custom-call | bytes 100000000 | tf_op jit(solution)/shard_map/reduce_weights/pallas_call | solution.py:619
  622.2 11.7 %convert_element_type.195 = f32[8,512,1024]{2,1,0:T(8,128)} convert(bf16[8,512,1024]{2,1,0:T(8,128)(2,1)} %all-gather.11.cloned.1.call-done) | non-fusion elementwise | flops 4194304 | bytes 25165824 | tf_op jit(solution)/shard_map/convert_element_type | solution.py:1087
  633.9 11.9 %convert_element_type.194 = f32[8,1024,512]{2,1,0:T(8,128)} convert(bf16[8,1024,512]{2,1,0:T(8,128)(2,1)} %all-gather.9.cloned.1.call-done) | non-fusion elementwise | flops 4194304 | bytes 25165824 | tf_op jit(solution)/shard_map/convert_element_type | solution.py:1087
  645.8 11.9 %convert_element_type.193 = f32[8,1024,512]{2,1,0:T(8,128)} convert(bf16[8,1024,512]{2,1,0:T(8,128)(2,1)} %all-gather.7.cloned.1.call-done) | non-fusion elementwise | flops 4194304 | bytes 25165824 | tf_op jit(solution)/shard_map/convert_element_type | solution.py:1087
  (146 shorter events, 54.5 us)
Async XLA Ops:
  7.2 75.8 %copy-start.6 = (bf16[256,1024]{1,0:T(8,128)(2,1)S(1)}, bf16[256,1024]{1,0:T(8,128)(2,1)}, u32[]{:S(2)}) copy-start(bf16[256,1024]{1,0:T(8,128)(2,1)} %param.14) | copy-start | bytes 1572868
  7.2 200.0 %all-gather.5.cloned.1.call-start = ((), (), s32[]{:S(2)}) async-start(), calls=%async_computation.1 | async-start | bytes 2621440 | tf_op jit(solution)/shard_map/all_gather | solution.py:896
  9.9 414.4 %reduce-scatter.2.cloned.1.call-start = ((), (), s32[]{:S(2)}) async-start(), calls=%async_computation.2 | async-start | bytes 2621440 | tf_op jit(solution)/shard_map/reduce_scatter | solution.py:900
  83.0 4.6 copy-start.25
  83.0 5.4 copy-start.5
  140.6 9.1 %copy-start.1 = (bf16[1024,512]{0,1:T(8,128)(2,1)}, bf16[1024,512]{0,1:T(8,128)(2,1)S(1)}, u32[]{:S(2)}) copy-start(bf16[1024,512]{0,1:T(8,128)(2,1)S(1)} %copy.111) | copy-start | bytes 3145732
  140.8 19.9 %copy-start.7 = (pred[256,1024]{0,1:T(8,128)(4,1)}, pred[256,1024]{0,1:T(8,128)(4,1)S(1)}, u32[]{:S(2)}) copy-start(pred[256,1024]{0,1:T(8,128)(4,1)S(1)} %fusion.33) | copy-start | bytes 786436
  140.8 8.8 %copy-start.20 = (bf16[4,32,256]{2,1,0:T(8,128)(2,1)S(1)}, bf16[4,32,256]{2,1,0:T(8,128)(2,1)}, u32[]{:S(2)}) copy-start(bf16[4,32,256]{2,1,0:T(8,128)(2,1)} %get-tuple-element.28) | copy-start | bytes 196612
  151.7 9.0 %copy-start.14 = (bf16[1024,512]{0,1:T(8,128)(2,1)}, bf16[1024,512]{0,1:T(8,128)(2,1)S(1)}, u32[]{:S(2)}) copy-start(bf16[1024,512]{0,1:T(8,128)(2,1)S(1)} %copy.113) | copy-start | bytes 3145732
  160.7 8.4 %copy-start.3 = (bf16[4,2,2,2,32,1024]{5,4,3,2,1,0:T(8,128)(2,1)S(1)}, bf16[4,2,2,2,32,1024]{5,4,3,2,1,0:T(8,128)(2,1)}, u32[]{:S(2)}) copy-start(bf16[4,2,2,2,32,1024]{5,4,3,2,1,0:T(8,128)(2,1)} %get-tuple-element.27) | copy-start | bytes 6291460
  332.2 290.1 %all-gather.11.cloned.1.call-start = ((), (), s32[]{:S(2)}) async-start(), calls=%async_computation.5 | async-start | bytes 9437184 | tf_op jit(solution)/shard_map/all_gather | solution.py:1087
  332.9 301.0 %all-gather.9.cloned.1.call-start = ((), (), s32[]{:S(2)}) async-start(), calls=%async_computation.4 | async-start | bytes 9437184 | tf_op jit(solution)/shard_map/all_gather | solution.py:1087
  333.5 312.3 %all-gather.7.cloned.1.call-start = ((), (), s32[]{:S(2)}) async-start(), calls=%async_computation.3 | async-start | bytes 9437184 | tf_op jit(solution)/shard_map/all_gather | solution.py:1087
  427.0 4.2 copy-start.8
  431.2 12.1 %copy-start.9 = (bf16[256,16,32]{0,2,1:T(8,128)(2,1)S(1)}, bf16[256,16,32]{0,2,1:T(8,128)(2,1)}, u32[]{:S(2)}) copy-start(bf16[256,16,32]{0,2,1:T(8,128)(2,1)} %get-tuple-element.46) | copy-start | bytes 786436
  431.2 12.0 %copy-start.10 = (bf16[256,16,32]{0,2,1:T(8,128)(2,1)S(1)}, bf16[256,16,32]{0,2,1:T(8,128)(2,1)}, u32[]{:S(2)}) copy-start(bf16[256,16,32]{0,2,1:T(8,128)(2,1)} %get-tuple-element.47) | copy-start | bytes 786436
  439.9 3.4 copy-start
  466.5 52.3 %copy-start.2 = (bf16[1024,512]{0,1:T(8,128)(2,1)S(1)}, bf16[1024,512]{0,1:T(8,128)(2,1)}, u32[]{:S(2)}) copy-start(bf16[1024,512]{0,1:T(8,128)(2,1)} %copy-done.1) | copy-start | bytes 3145732
  518.8 5.3 copy-start.23
  518.8 5.3 copy-start.21
  518.8 5.3 copy-start.26
  524.1 2.9 copy-start.15
  524.1 3.2 copy-start.12
  616.8 4.1 copy-start.17
  (8 other events, 13.7 us)
Sparse Core Ops, SparseCore 0:
  10.1 57.1 all-gather.4
  332.3 74.3 reduce-scatter.1
  408.6 55.0 all-gather.10
  465.4 54.2 all-gather.8
  521.4 72.6 all-gather.6

commit v4 on v3

--- a/solution.py
+++ b/solution.py
@@ -892,6 +892,147 @@
     )(x_all, ct_all, router_t, rank_row, rank_col, w_gate, w_up, w_down)
 
 
+def mask_bias(bias_ref, length_ref, rows):
+    base = lax.axis_index("expert") * rows
+    key = lax.broadcasted_iota(jnp.int32, bias_ref.shape, 0)
+    query = lax.broadcasted_iota(jnp.int32, bias_ref.shape, 1) + base
+    allowed = (key <= query) & (key < length_ref[0])
+    bias_ref[...] = jnp.where(allowed, 0.0, NEGATIVE_LARGE)
+
+
+def head_columns(ref, head):
+    start = 2 * HEAD_DIMENSION * head
+    middle = start + HEAD_DIMENSION
+    return jnp.concatenate([ref[:, start:middle], ref[:, middle : middle + HEAD_DIMENSION]], 0)
+
+
+def put_heads(ref, head, transposed):
+    rows = ref.shape[0]
+    value = transposed.T
+    start = 2 * HEAD_DIMENSION * head
+    middle = start + HEAD_DIMENSION
+    ref[:, start:middle] = value[:rows].astype(ref.dtype)
+    ref[:, middle : middle + HEAD_DIMENSION] = value[rows:].astype(ref.dtype)
+
+
+def attention_kernel(length_ref, q_ref, kv_ref, mixed_ref, log_total_ref, bias_ref):
+    @pl.when(pl.program_id(0) == 0)
+    def _():
+        mask_bias(bias_ref, length_ref, q_ref.shape[0])
+
+    bias = jnp.concatenate([bias_ref[...]] * 2, axis=1)
+    for head in (0, 1):
+        columns = slice(head * HEAD_DIMENSION, (head + 1) * HEAD_DIMENSION)
+        key, value = kv_ref[:, :LANES][:, columns], kv_ref[:, LANES:][:, columns]
+        query = head_columns(q_ref, head) * jnp.asarray(HEAD_DIMENSION**-0.5, BF)
+        scores = dot_nt(key, query) + bias
+        top = jnp.max(scores, axis=0, keepdims=True)
+        weights = jnp.exp(scores - top)
+        total = jnp.sum(weights, axis=0, keepdims=True)
+        put_heads(mixed_ref, head, dot_tn(value, weights.astype(BF)) / total)
+        log_total_ref[0, head : head + 1, :] = top + jnp.log(total)
+
+
+def attention(length, query, kv_all):
+    rows, keys = query.shape[0], kv_all.shape[0]
+    pairs = KEY_VALUE_HEADS // 2
+    return pl.pallas_call(
+        attention_kernel,
+        grid=(pairs,),
+        out_shape=(
+            jax.ShapeDtypeStruct(query.shape, BF),
+            jax.ShapeDtypeStruct((pairs, 2, 2 * rows), F32),
+        ),
+        in_specs=[
+            pl.BlockSpec(memory_space=pltpu.SMEM),
+            pl.BlockSpec((rows, 2 * LANES), lambda j: (0, j)),
+            pl.BlockSpec((keys, 2 * LANES), lambda j: (0, j)),
+        ],
+        out_specs=(
+            pl.BlockSpec((rows, 2 * LANES), lambda j: (0, j)),
+            pl.BlockSpec((1, 2, 2 * rows), lambda j: (j, 0, 0)),
+        ),
+        scratch_shapes=[pltpu.VMEM((keys, rows), F32)],
+        compiler_params=pltpu.CompilerParams(
+            dimension_semantics=("arbitrary",), vmem_limit_bytes=48 * 1024 * 1024
+        ),
+        cost_estimate=pl.CostEstimate(
+            flops=16 * rows * keys * D, bytes_accessed=4 * keys * D, transcendentals=0
+        ),
+        name="attention",
+    )(length, query, kv_all)
+
+
+def attention_back_kernel(
+    length_ref, q_ref, kv_ref, grad_ref, log_total_ref, grad_q_ref, grad_kv_ref, bias_ref
+):
+    @pl.when(pl.program_id(0) == 0)
+    def _():
+        mask_bias(bias_ref, length_ref, q_ref.shape[0])
+
+    scale = HEAD_DIMENSION**-0.5
+    bias = jnp.concatenate([bias_ref[...]] * 2, axis=1)
+    for head in (0, 1):
+        columns = slice(head * HEAD_DIMENSION, (head + 1) * HEAD_DIMENSION)
+        key, value = kv_ref[:, :LANES][:, columns], kv_ref[:, LANES:][:, columns]
+        query = head_columns(q_ref, head) * jnp.asarray(scale, BF)
+        grad = head_columns(grad_ref, head)
+        scores = dot_nt(key, query) + bias
+        probs = jnp.exp(scores - log_total_ref[0, head : head + 1, :])
+        grad_probs = dot_nt(value, grad)
+        delta = jnp.sum(probs * grad_probs, axis=0, keepdims=True)
+        grad_scores = (probs * (grad_probs - delta)).astype(BF)
+        grad_kv_ref[:, head * HEAD_DIMENSION : (head + 1) * HEAD_DIMENSION] = dot(
+            grad_scores, query
+        ).astype(BF)
+        start = LANES + head * HEAD_DIMENSION
+        grad_kv_ref[:, start : start + HEAD_DIMENSION] = dot(probs.astype(BF), grad).astype(BF)
+        put_heads(grad_q_ref, head, dot_tn(key, grad_scores) * scale)
+
+
+def attention_back(length, query, kv_all, grad_mixed, log_total):
+    rows, keys = query.shape[0], kv_all.shape[0]
+    pairs = KEY_VALUE_HEADS // 2
+    row_spec = pl.BlockSpec((rows, 2 * LANES), lambda j: (0, j))
+    key_spec = pl.BlockSpec((keys, 2 * LANES), lambda j: (0, j))
+    return pl.pallas_call(
+        attention_back_kernel,
+        grid=(pairs,),
+        out_shape=(
+            jax.ShapeDtypeStruct(query.shape, F32),
+            jax.ShapeDtypeStruct(kv_all.shape, BF),
+        ),
+        in_specs=[
+            pl.BlockSpec(memory_space=pltpu.SMEM),
+            row_spec,
+            key_spec,
+            row_spec,
+            pl.BlockSpec((1, 2, 2 * rows), lambda j: (j, 0, 0)),
+        ],
+        out_specs=(row_spec, key_spec),
+        scratch_shapes=[pltpu.VMEM((keys, rows), F32)],
+        compiler_params=pltpu.CompilerParams(
+            dimension_semantics=("arbitrary",), vmem_limit_bytes=48 * 1024 * 1024
+        ),
+        cost_estimate=pl.CostEstimate(
+            flops=40 * rows * keys * D, bytes_accessed=6 * keys * D, transcendentals=0
+        ),
+        name="attention_back",
+    )(length, query, kv_all, grad_mixed, log_total)
+
+
+def pair_columns(first, second):
+    rows = first.shape[0]
+    both = [value.reshape(rows, -1, 1, LANES) for value in (first, second)]
+    return jnp.concatenate(both, axis=2).reshape(rows, -1)
+
+
+def unpair_columns(value):
+    rows = value.shape[0]
+    value = value.reshape(rows, -1, 2, LANES)
+    return value[:, :, 0].reshape(rows, -1), value[:, :, 1].reshape(rows, -1)
+
+
 def gather_rows(value):
     return lax.all_gather(value, "expert", axis=0, tiled=True)
 
@@ -920,8 +1061,6 @@
     n, groups = lax.axis_size("expert"), lax.axis_size("group")
     my_index = lax.axis_index("expert")
     capacity = 3 * rows * TOP // (2 * EXPERTS)
-    group_of_heads = QUERY_HEADS // KEY_VALUE_HEADS
-    score_scale = HEAD_DIMENSION ** (-0.5)
     query_width, key_width = w_query.shape[1], key_projection.shape[1]
     length = lengths[0]
     positions = my_index * rows + jnp.arange(rows, dtype=jnp.int32)
@@ -945,7 +1084,6 @@
     row_id = jnp.arange(rows, dtype=jnp.int32)
     earlier = (row_id[:, None] < row_id[None, :]).astype(BF)
     rank = jnp.where(hot.T, dot(hot.T.astype(BF), earlier), 255.0).astype(BF)
-    ct_all = gather_rows(grad_output)
 
     cosine_lookup, sine_lookup = rotary_tables(positions, HEAD_DIMENSION)
     token_f32 = tokens.astype(F32)
@@ -959,38 +1097,20 @@
     query_rows = apply_rotation(
         query_pre.reshape(rows, QUERY_HEADS, HEAD_DIMENSION), cosine_lookup, sine_lookup
     ).astype(BF)
-    query_rows = query_rows.reshape(rows, KEY_VALUE_HEADS, group_of_heads, HEAD_DIMENSION)
+    query_rows = query_rows.reshape(rows, query_width)
     local_keys = apply_rotation(
         unrotated_key.reshape(rows, KEY_VALUE_HEADS, HEAD_DIMENSION), cosine_lookup, sine_lookup
     ).astype(BF)
     local_keys = local_keys.reshape(rows, key_width)
     kv_all, rank_all = line_gather(
-        [jnp.concatenate([local_keys, value_pre.astype(BF)], axis=1), rank], n, 2, "gather_kv"
+        [pair_columns(local_keys, value_pre.astype(BF)), rank], n, 2, "gather_kv"
     )
     rank_all = rank_all.reshape(n, EXPERTS, rows)
     rank_row = jnp.transpose(rank_all, (1, 0, 2)).reshape(EXPERTS, n * rows).astype(F32)
     rank_col = jnp.transpose(rank_all, (0, 2, 1)).reshape(n * rows, EXPERTS)
-    key_portion = kv_all[:, :key_width].reshape(-1, KEY_VALUE_HEADS, HEAD_DIMENSION)
-    value_portion = kv_all[:, key_width:].reshape(-1, KEY_VALUE_HEADS, HEAD_DIMENSION)
-    key_count = kv_all.shape[0]
-    scores = (
-        jnp.einsum("qhgd,khd->hgqk", query_rows, key_portion, preferred_element_type=F32)
-        * score_scale
-    )
-    columns = jnp.arange(key_count, dtype=jnp.int32)
-    allowed = (columns[None, :] <= positions[:, None]) & (columns[None, :] < length)
-    masked = jnp.where(allowed, scores, NEGATIVE_LARGE)
-    maximum = jnp.max(masked, axis=-1)
-    weights = jnp.where(allowed, jnp.exp(masked - maximum[..., None]), 0.0)
-    total = jnp.sum(weights, axis=-1)
-    mixed_f32 = (
-        jnp.einsum(
-            "hgqk,khd->hgqd", weights.astype(BF), value_portion, preferred_element_type=F32
-        )
-        / total[..., None]
-    )
-    log_total = maximum + jnp.log(total)
-    mixed_low = jnp.transpose(mixed_f32, (2, 0, 1, 3)).reshape(rows, query_width).astype(BF)
+    grad_output_late, kv_all = lax.optimization_barrier((grad_output, kv_all))
+    ct_all = gather_rows(grad_output_late)
+    mixed_low, log_total = attention(lengths, query_rows, kv_all)
     residual = token_f32 + dot(mixed_low, out_weight)
     inverse_two = lax.rsqrt(jnp.mean(residual * residual, axis=-1, keepdims=True) + EPSILON)
     unit_two = residual * inverse_two
@@ -1001,8 +1121,6 @@
         x_all, ct_all, router_weight.T, rank_row, rank_col, w_gate, w_up, w_down, rows, capacity, groups == 8, 7
     )
     gs = line_scatter(gs_part, n, F32, 4, "scatter_grads")
-    expert_sum = scatter_rows(y_part).astype(F32)
-    mixed = (residual + expert_sum).astype(BF)
 
     logits = dot(second_norm, router_weight)
     chosen = jnp.where(hot, logits, NEGATIVE_LARGE)
@@ -1023,44 +1141,29 @@
     grad_attn = grad_residual.astype(BF)
     grad_out = dot_tn(mixed_low, grad_attn)
     mixed_gradient = dot_nt(grad_attn, out_weight).astype(BF)
-    head_gradient = mixed_gradient.reshape(rows, KEY_VALUE_HEADS, group_of_heads, HEAD_DIMENSION)
-    delta = jnp.einsum("qhgd,hgqd->hgq", head_gradient, mixed_f32, preferred_element_type=F32)
-    probability = jnp.where(allowed, jnp.exp(masked - log_total[..., None]), 0.0)
-    grad_prob = jnp.einsum(
-        "qhgd,khd->hgqk", head_gradient, value_portion, preferred_element_type=F32
-    )
-    grad_scores = (probability * (grad_prob - delta[..., None])).astype(BF)
-    grad_query_acc = jnp.einsum(
-        "hgqk,khd->qhgd", grad_scores, key_portion, preferred_element_type=F32
-    )
-    key_gradient = jnp.einsum(
-        "hgqk,qhgd->khd", grad_scores, query_rows, preferred_element_type=F32
-    ).reshape(key_count, key_width)
-    value_gradient = jnp.einsum(
-        "hgqk,qhgd->khd", probability.astype(BF), head_gradient, preferred_element_type=F32
-    ).reshape(key_count, key_width)
-    kv_gradient = line_scatter(
-        jnp.concatenate([key_gradient.astype(BF), value_gradient.astype(BF)], axis=1),
-        n,
-        BF,
-        5,
-        "scatter_kv",
-    )
-    own_key_gradient = kv_gradient[:, :key_width].astype(F32)
-    grad_query_rows = grad_query_acc.reshape(rows, QUERY_HEADS, HEAD_DIMENSION) * score_scale
+    grad_query_acc, kv_terms = attention_back(
+        lengths, query_rows, kv_all, mixed_gradient, log_total
+    )
+    kv_gradient = line_scatter(kv_terms, n, BF, 5, "scatter_kv")
+    kv_gradient, y_part = lax.optimization_barrier((kv_gradient, y_part))
+    expert_sum = scatter_rows(y_part).astype(F32)
+    mixed = (residual + expert_sum).astype(BF)
+    own_key_gradient, own_value_gradient = unpair_columns(kv_gradient)
     grad_query_pre = (
-        apply_rotation(grad_query_rows, cosine_lookup, -sine_lookup)
+        apply_rotation(
+            grad_query_acc.reshape(rows, QUERY_HEADS, HEAD_DIMENSION), cosine_lookup, -sine_lookup
+        )
         .reshape(rows, query_width)
         .astype(BF)
     )
     grad_key_pre = apply_rotation(
-        own_key_gradient.reshape(rows, KEY_VALUE_HEADS, HEAD_DIMENSION) * score_scale,
+        own_key_gradient.astype(F32).reshape(rows, KEY_VALUE_HEADS, HEAD_DIMENSION),
         cosine_lookup,
         -sine_lookup,
     )
     grad_key_pre = grad_key_pre.reshape(rows, key_width).astype(BF)
     grad_qkv_pre = jnp.concatenate(
-        [grad_query_pre, grad_key_pre, kv_gradient[:, key_width:]], axis=1
+        [grad_query_pre, grad_key_pre, own_value_gradient], axis=1
     )
     grad_qkv = dot_tn(first_norm, grad_qkv_pre)
     grad_first = dot_nt(grad_qkv_pre, qkv_weight)

time: 670 us -> 685 us (1.022)
  waiting for transfers between devices: 1.8 us -> 82.2 us
  matrix products: 60.6 us -> 17.2 us
  other arithmetic: 69.5 us -> 54.6 us
  Pallas kernels: 485 us -> 478 us
    all_gather x3, waiting for transfers between devices: 0.01 us -> 80.5 us  [sum_over_groups(): return lax.all_gather(value, 'group', axis=1, tiled=True).astype(F32)]
    dot_general x6 -> x0, matrix products: 43.4 us -> none  [the longest x1 9.9 us: per_device(): jnp.einsum('hgqk,qhgd->khd', probability.astype(BF), head_gradient, prefe...]
    pallas_call x2, Pallas kernels: 129 us -> 98.7 us  [line_scatter(): pl.pallas_call(functools.partial(line_scatter_kernel, n), out_shape=jax.S...]
    pallas_call x1, Pallas kernels: 67.1 us -> 40.8 us  [gather_weights(): pl.pallas_call(functools.partial(weights_kernel, n, pieces, widths), out_...]
    pallas_call x0 -> x2, Pallas kernels: none -> 24.2 us  [the longest x1 15.3 us: attention_back(): pl.pallas_call(attention_back_kernel, grid=(pairs,), out_shape=(jax.Shape...]
    pallas_call x2, Pallas kernels: 79.7 us -> 101 us  [line_gather(): pl.pallas_call(functools.partial(line_gather_kernel, n, count), out_shape...]
    reduce_sum x1 -> x0, other arithmetic: 8.95 us -> none  [per_device(): total = jnp.sum(weights, axis=-1)]
    convert_element_type x6 -> x1, local copies, waits for them, and re-layouts: 7.92 us -> 0.21 us  [per_device(): query_rows = apply_rotation(query_pre.reshape(rows, QUERY_HEADS, HEAD_DIM...]
  transfers between devices with their start and end apart: 5 -> 5, of which waited for: 0 -> 2; matrix products, arithmetic and copies ran while one was open for 22% -> 9% of each run, Pallas kernels for 54% -> 23%
where the time goes in v4:
time: 685 us; the launch traced here: 676 us
  Pallas kernels  478 us (70%)
  waiting for transfers between devices  82.2 us (12%)
  other arithmetic  54.6 us (8%)
  local copies, waits for them, and re-layouts  28.4 us (4%)
  matrix products  17.2 us (3%)
  between operations  15.6 us (2%)
    pallas_call x1, Pallas kernels, run_experts(): pl.pallas_call(functools.partial(expert_kernel, sizes, plane), grid=(loca...  126 us
    pallas_call x2, Pallas kernels, line_gather(): pl.pallas_call(functools.partial(line_gather_kernel, n, count), out_shape...  101 us
    pallas_call x2, Pallas kernels, line_scatter(): pl.pallas_call(functools.partial(line_scatter_kernel, n), out_shape=jax.S...  98.7 us
    pallas_call x1, Pallas kernels, reduce_weights(): pl.pallas_call(functools.partial(reduce_kernel, n, pieces), out_shape=[ja...  87.5 us
    all_gather x3, waiting for transfers between devices, sum_over_groups(): return lax.all_gather(value, 'group', axis=1, tiled=True).astype(F32)  80.5 us
    pallas_call x1, Pallas kernels, gather_weights(): pl.pallas_call(functools.partial(weights_kernel, n, pieces, widths), out_...  40.8 us
    convert_element_type x3, other arithmetic, sum_over_groups(): return lax.all_gather(value, 'group', axis=1, tiled=True).astype(F32)  36.7 us
    pallas_call x1, Pallas kernels, attention_back(): pl.pallas_call(attention_back_kernel, grid=(pairs,), out_shape=(jax.Shape...  15.3 us
  transfers between devices with their start and end apart: 5, of which 2 were waited for; matrix products, arithmetic and copies ran while one was open for 9% of the time, Pallas kernels for 23%

profile of v4, /device:TPU:0, one launch (start us, length us, event | category | flops | bytes accessed | tf_op | source)
XLA Modules:
  0.0 676.4 jit_solution(12705386014483603225)
XLA Ops:
  11.7 40.8 %gather_weights.1 = (bf16[4,2,2,2,32,2048]{5,4,3,2,1,0:T(8,128)(2,1)}, bf16[4,2,2,2,32,1024]{5,4,3,2,1,0:T(8,128)(2,1)}, bf16[4,2,2,2,32,128]{5,4,3,2,1,0:T(8,128)(2,1)}) custom-call(bf16[256,1024]{1,0:T(8,128)(2,1)} %refs_0_.1, bf16[256,512]{1,0:T(8,128)(2,1)} %refs_1_.1, bf16[256,512]{1,0:T(8,128)(2,1)} %refs_2_.1, bf16[256,1024]{1,0:T(8,128)(2,1)} %refs_3_.1, ...), custom_call_target="tpu_custom_call" | custom-call | bytes 100000000 | tf_op jit(solution)/shard_map/gather_weights/pallas_call | solution.py:423
  53.9 3.5 fusion.17
  64.2 41.9 %gather_kv.1 = (bf16[4,256,1024]{2,1,0:T(8,128)(2,1)}, bf16[4,32,256]{2,1,0:T(8,128)(2,1)}) custom-call(bf16[256,1024]{1,0:T(8,128)(2,1)} %reshape.245.refs_0_, bf16[32,256]{1,0:T(8,128)(2,1)} %fusion.4.refs_1_), custom_call_target="tpu_custom_call" | custom-call | bytes 100000000 | tf_op jit(solution)/shard_map/gather_kv/pallas_call | solution.py:152
  106.3 2.3 slice.122
  109.4 1.6 copy.86
  113.3 1.8 copy-done.1
  115.1 8.9 %attention.1 = (bf16[256,1024]{1,0:T(8,128)(2,1)S(1)}, f32[4,2,512]{2,1,0:T(2,128)S(1)}) custom-call(s32[1]{0:T(128)} %copy.116.length_ref, bf16[256,1024]{1,0:T(8,128)(2,1)S(1)} %copy.90.q_ref, bf16[1024,1024]{1,0:T(8,128)(2,1)S(1)} %bitcast.55), custom_call_target="tpu_custom_call" | custom-call | flops 4294967296 | bytes 4194304 | tf_op jit(solution)/shard_map/attention/pallas_call | solution.py:939
  126.7 59.4 %gather_rows.1 = bf16[4,256,1024]{2,1,0:T(8,128)(2,1)} custom-call(bf16[256,1024]{1,0:T(8,128)(2,1)} %multiply_convert_fusion.refs_0_), custom_call_target="tpu_custom_call" | custom-call | bytes 100000000 | tf_op jit(solution)/shard_map/gather_rows/pallas_call | solution.py:152
  187.3 125.7 %experts.1 = (bf16[1024,1024]{1,0:T(8,128)(2,1)}, bf16[1024,1152]{1,0:T(8,128)(2,1)}, bf16[8,128,512]{2,1,0:T(8,128)(2,1)}, bf16[8,128,512]{2,1,0:T(8,128)(2,1)}, bf16[8,64,1024]{2,1,0:T(8,128)(2,1)}) custom-call(bf16[1024,1024]{1,0:T(8,128)(2,1)} %bitcast.66, bf16[1024,1024]{1,0:T(8,128)(2,1)} %all-gather.5.cloned.1.call-done.refs_1_, ...), custom_call_target="tpu_custom_call" | custom-call | flops 30601641984 | bytes 58720256 | tf_op jit(solution)/shard_map/experts/pallas_call | solution.py:869
  313.0 53.4 %scatter_grads.1 = f32[256,1152]{1,0:T(8,128)} custom-call(bf16[4,256,1152]{2,1,0:T(8,128)(2,1)} %bitcast.65), custom_call_target="tpu_custom_call" | custom-call | bytes 100000000 | tf_op jit(solution)/shard_map/scatter_grads/pallas_call | solution.py:244
  369.2 1.7 multiply_reduce_fusion
  373.3 15.3 %attention_back.1 = (f32[256,1024]{1,0:T(8,128)S(1)}, bf16[1024,1024]{1,0:T(8,128)(2,1)S(1)}) custom-call(s32[1]{0:T(128)} %copy.116.length_ref, bf16[256,1024]{1,0:T(8,128)(2,1)S(1)} %copy.90.q_ref, bf16[1024,1024]{1,0:T(8,128)(2,1)} %bitcast.54, bf16[256,1024]{1,0:T(8,128)(2,1)S(1)} %convolution_convert_fusion.2.grad_ref, ...), custom_call_target="tpu_custom_call" | custom-call | flops 10737418240 | bytes 6291456 | tf_op jit(solution)/shard_map/attention_back/pallas_call | solution.py:998
  389.9 45.3 %scatter_kv.1 = bf16[256,1024]{1,0:T(8,128)(2,1)} custom-call(bf16[4,256,1024]{2,1,0:T(8,128)(2,1)} %bitcast.49), custom_call_target="tpu_custom_call" | custom-call | bytes 100000000 | tf_op jit(solution)/shard_map/scatter_kv/pallas_call | solution.py:244
  439.1 1.5 fusion.28
  444.7 1.5 subtract_convert_fusion
  446.3 4.8 fusion.10
  453.1 3.5 convolution_convert_fusion
  456.6 87.5 %reduce_weights.1 = (bf16[2,2,2,32,1664]{4,3,2,1,0:T(8,128)(2,1)S(1)}, bf16[2,2,2,32,1536]{4,3,2,1,0:T(8,128)(2,1)S(1)}) custom-call(bf16[4,2,2,2,32,2048]{5,4,3,2,1,0:T(8,128)(2,1)} %bitcast.62, bf16[4,2,2,2,32,1024]{5,4,3,2,1,0:T(8,128)(2,1)S(1)} %bitcast.48, bf16[4,2,2,2,32,128]{5,4,3,2,1,0:T(8,128)(2,1)S(1)} %maximum_maximum_fusion.refs_2_), custom_call_target="tpu_custom_call" | custom-call | bytes 100000000 | tf_op jit(solution)/shard_map/reduce_weights/pallas_call | solution.py:619
  550.3 2.0 add_convert_fusion
  552.3 12.5 %convert_element_type.163 = f32[8,512,1024]{2,1,0:T(8,128)} convert(bf16[8,512,1024]{2,1,0:T(8,128)(2,1)} %all-gather.11.cloned.1.call-done) | non-fusion elementwise | flops 4194304 | bytes 25165824 | tf_op jit(solution)/shard_map/convert_element_type | solution.py:1190
  564.8 36.8 %all-gather.9.cloned.1.call-done = bf16[8,1024,512]{2,1,0:T(8,128)(2,1)} async-done(((bf16[8,128,512]{2,1,0:T(8,128)(2,1)}), bf16[8,1024,512]{2,1,0:T(8,128)(2,1)}) %all-gather.9.cloned.1.call-update) | async-done | bytes 8388624 | tf_op jit(solution)/shard_map/all_gather | solution.py:1190
  601.5 12.3 %convert_element_type.162 = f32[8,1024,512]{2,1,0:T(8,128)} convert(bf16[8,1024,512]{2,1,0:T(8,128)(2,1)} %all-gather.9.cloned.1.call-done) | non-fusion elementwise | flops 4194304 | bytes 25165824 | tf_op jit(solution)/shard_map/convert_element_type | solution.py:1190
  613.9 43.7 %all-gather.7.cloned.1.call-done = bf16[8,1024,512]{2,1,0:T(8,128)(2,1)} async-done(((bf16[8,128,512]{2,1,0:T(8,128)(2,1)}), bf16[8,1024,512]{2,1,0:T(8,128)(2,1)}) %all-gather.7.cloned.1.call-update) | async-done | bytes 8388624 | tf_op jit(solution)/shard_map/all_gather | solution.py:1190
  657.6 11.9 %convert_element_type.161 = f32[8,1024,512]{2,1,0:T(8,128)} convert(bf16[8,1024,512]{2,1,0:T(8,128)(2,1)} %all-gather.7.cloned.1.call-done) | non-fusion elementwise | flops 4194304 | bytes 25165824 | tf_op jit(solution)/shard_map/convert_element_type | solution.py:1190
  (155 shorter events, 41.3 us)
Async XLA Ops:
  7.2 46.7 %copy-start.11 = (bf16[256,1024]{1,0:T(8,128)(2,1)S(1)}, bf16[256,1024]{1,0:T(8,128)(2,1)}, u32[]{:S(2)}) copy-start(bf16[256,1024]{1,0:T(8,128)(2,1)} %param.14) | copy-start | bytes 1572868
  7.2 180.1 %all-gather.5.cloned.1.call-start = ((), (), s32[]{:S(2)}) async-start(), calls=%async_computation.1 | async-start | bytes 2621440 | tf_op jit(solution)/shard_map/all_gather | solution.py:1037
  8.5 48.9 %copy-start.31 = (f32[256]{0:T(256)}, f32[256]{0:T(256)S(1)}, u32[]{:S(2)}) copy-start(f32[256]{0:T(256)S(1)} %add_rsqrt_fusion.1) | copy-start | bytes 3076
  11.0 46.5 %copy-start.33 = (bf16[128]{0:T(256)(128)(2,1)}, bf16[128]{0:T(256)(128)(2,1)S(1)}, u32[]{:S(2)}) copy-start(bf16[128]{0:T(256)(128)(2,1)S(1)} %pad.22.clone) | copy-start | bytes 772
  53.9 5.6 copy-start.30
  59.5 3.8 copy-start.35
  61.5 49.5 %copy-start.19 = (f32[256,32]{0,1:T(8,128)}, f32[256,32]{0,1:T(8,128)S(1)}, u32[]{:S(2)}) copy-start(f32[256,32]{0,1:T(8,128)S(1)} %get-tuple-element.74) | copy-start | bytes 98308
  63.3 45.3 %copy-start.10 = (bf16[4,2,2,2,32,128]{5,4,3,2,1,0:T(8,128)(2,1)S(1)}, bf16[4,2,2,2,32,128]{5,4,3,2,1,0:T(8,128)(2,1)}, u32[]{:S(2)}) copy-start(bf16[4,2,2,2,32,128]{5,4,3,2,1,0:T(8,128)(2,1)} %get-tuple-element.32) | copy-start | bytes 786436
  106.2 444.2 %reduce-scatter.2.cloned.1.call-start = ((), (), s32[]{:S(2)}) async-start(), calls=%async_computation.2 | async-start | bytes 2621440 | tf_op jit(solution)/shard_map/reduce_scatter | solution.py:1041
  115.1 8.9 %copy-start.7 = (bf16[4,2,2,2,32,1024]{5,4,3,2,1,0:T(8,128)(2,1)S(1)}, bf16[4,2,2,2,32,1024]{5,4,3,2,1,0:T(8,128)(2,1)}, u32[]{:S(2)}) copy-start(bf16[4,2,2,2,32,1024]{5,4,3,2,1,0:T(8,128)(2,1)} %get-tuple-element.37) | copy-start | bytes 6291460
  126.7 59.4 %copy-start.9 = (bf16[256,1024]{1,0:T(8,128)(2,1)S(1)}, bf16[256,1024]{1,0:T(8,128)(2,1)}, u32[]{:S(2)}) copy-start(bf16[256,1024]{1,0:T(8,128)(2,1)} %multiply_convert_fusion.refs_0_) | copy-start | bytes 1572868
  313.0 53.5 %copy-start.29 = (f32[256]{0:T(256)S(1)}, f32[256]{0:T(256)}, u32[]{:S(2)}) copy-start(f32[256]{0:T(256)} %fusion.20) | copy-start | bytes 3076
  313.0 56.1 %copy-start.3 = (f32[256,1024]{1,0:T(8,128)S(1)}, f32[256,1024]{1,0:T(8,128)}, u32[]{:S(2)}) copy-start(f32[256,1024]{1,0:T(8,128)} %copy-done.2) | copy-start | bytes 3145732
  372.5 16.1 %copy-start.5 = (f32[256,1024]{1,0:T(8,128)}, f32[256,1024]{1,0:T(8,128)S(1)}, u32[]{:S(2)}) copy-start(f32[256,1024]{1,0:T(8,128)S(1)} %multiply_add_fusion) | copy-start | bytes 3145732
  435.2 117.1 %all-gather.11.cloned.1.call-start = ((), (), s32[]{:S(2)}) async-start(), calls=%async_computation.5 | async-start | bytes 9437184 | tf_op jit(solution)/shard_map/all_gather | solution.py:1190
  436.0 165.6 %all-gather.9.cloned.1.call-start = ((), (), s32[]{:S(2)}) async-start(), calls=%async_computation.4 | async-start | bytes 9437184 | tf_op jit(solution)/shard_map/all_gather | solution.py:1190
  436.6 221.0 %all-gather.7.cloned.1.call-start = ((), (), s32[]{:S(2)}) async-start(), calls=%async_computation.3 | async-start | bytes 9437184 | tf_op jit(solution)/shard_map/all_gather | solution.py:1190
  440.6 4.0 copy-start.20
  440.6 4.0 copy-start.23
  444.7 6.5 copy-start.27
  446.3 4.9 copy-start.21
  446.3 5.3 copy-start.17
  446.3 5.3 copy-start.34
  446.3 5.6 copy-start.6
  (18 other events, 31.9 us)
Sparse Core Ops, SparseCore 0:
  106.3 53.4 all-gather.4
  435.4 42.5 reduce-scatter.1
  479.9 65.5 all-gather.10
  547.3 54.2 all-gather.8
  603.3 54.2 all-gather.6

commit v5 on v4

--- a/solution.py
+++ b/solution.py
@@ -166,76 +166,108 @@
     return [o.reshape((n * v.shape[0],) + v.shape[1:]) for o, v in zip(outs, values)]
 
 
-def line_scatter_kernel(n, part_ref, out_ref, landing, staging, send, receive):
-    group, me = lax.axis_index("group"), lax.axis_index("expert")
-    left, right = (group, me - 1), (group, me + 1)
-    rows = part_ref.shape[1]
-    tile = 32
-    greet([(me > 0, left), (me < n - 1, right)])
-
-    def add(target, first, second):
-        def body(t, carry):
-            span = pl.ds(pl.multiple_of(t * tile, tile), tile)
-            target[span, :] = (first[span, :].astype(F32) + second[span, :].astype(F32)).astype(
-                target.dtype
-            )
-            return carry
-
-        lax.fori_loop(0, rows // tile, body, 0)
-
-    def copy(source, step, side):
+class LineSum:
+    def __init__(self, n, part, landing, staging, send, receive):
+        self.n, self.part, self.landing, self.staging = n, part, landing, staging
+        self.send, self.receive = send, receive
+        self.group, self.me = lax.axis_index("group"), lax.axis_index("expert")
+        self.rows = part.shape[1]
+        self.tile = min(32, self.rows)
+
+    def neighbours(self):
+        left, right = (self.group, self.me - 1), (self.group, self.me + 1)
+        return [(self.me > 0, left), (self.me < self.n - 1, right)]
+
+    def copy(self, source, step, side):
+        index = (side, step)
+        device = (self.group, self.me + 1 if side == 0 else self.me - 1)
         return remote(
-            source,
-            landing.at[side, step],
-            send.at[side, step],
-            receive.at[side, step],
-            right if side == 0 else left,
+            source, self.landing.at[index], self.send.at[index], self.receive.at[index], device
         )
 
-    for step in range(n - 1):
-        for side in (0, 1):
-            owner = n - 1 - step if side == 0 else step
-            beyond = me < owner if side == 0 else me > owner
-            edge = me == 0 if side == 0 else me == n - 1
+    def places(self):
+        me, n = self.me, self.n
+        for step in range(n - 1):
+            for side in (0, 1):
+                owner = n - 1 - step if side == 0 else step
+                beyond = me < owner if side == 0 else me > owner
+                edge = me == 0 if side == 0 else me == n - 1
+                yield step, side, owner, beyond, edge
+
+    def start(self):
+        for step, side, owner, beyond, edge in self.places():
 
             @pl.when(beyond & edge)
             def _():
-                copy(part_ref.at[owner], step, side).start()
+                self.copy(self.part.at[owner], step, side).start()
+
+    def spans(self, body):
+        def tile_body(t, carry):
+            body(pl.ds(pl.multiple_of(t * self.tile, self.tile), self.tile))
+            return carry
+
+        lax.fori_loop(0, self.rows // self.tile, tile_body, 0)
+
+    def forward(self, only):
+        for step, side, owner, beyond, edge in self.places():
+            if step != only:
+                continue
 
             @pl.when(beyond & jnp.logical_not(edge))
             def _():
-                copy(part_ref.at[owner], step, side).wait_recv()
-                add(staging.at[side, step], part_ref.at[owner], landing.at[side, step])
-                copy(staging.at[side, step], step, side).start()
-
-    @pl.when(me > 0)
-    def _():
-        step = n - 1 - me
-        copy(part_ref.at[me], step, 0).wait_recv()
-
-    @pl.when(me < n - 1)
-    def _():
-        copy(part_ref.at[me], me, 1).wait_recv()
-
-    def finish(t, carry):
-        span = pl.ds(pl.multiple_of(t * tile, tile), tile)
-        total = part_ref[me, span, :].astype(F32)
-        from_left = landing[0, jnp.minimum(n - 1 - me, n - 2), span, :].astype(F32)
-        from_right = landing[1, jnp.minimum(me, n - 2), span, :].astype(F32)
-        total = total + jnp.where(me > 0, from_left, 0.0)
-        total = total + jnp.where(me < n - 1, from_right, 0.0)
-        out_ref[span, :] = total.astype(out_ref.dtype)
-        return carry
-
-    lax.fori_loop(0, rows // tile, finish, 0)
-    for step in range(n - 1):
-        for side in (0, 1):
-            owner = n - 1 - step if side == 0 else step
-            beyond = me < owner if side == 0 else me > owner
+                self.copy(self.part.at[owner], step, side).wait_recv()
+
+                def add(span):
+                    total = self.part[owner, span, :].astype(F32)
+                    total = total + self.landing[side, step, span, :].astype(F32)
+                    self.staging[side, step, span, :] = total.astype(BF)
+
+                self.spans(add)
+                self.copy(self.staging.at[side, step], step, side).start()
+
+    def finish(self, out_ref):
+        me, n = self.me, self.n
+
+        @pl.when(me > 0)
+        def _():
+            self.copy(self.part.at[me], n - 1 - me, 0).wait_recv()
+
+        @pl.when(me < n - 1)
+        def _():
+            self.copy(self.part.at[me], me, 1).wait_recv()
+
+        def total(span):
+            value = self.part[me, span, :].astype(F32)
+            from_left = self.landing[0, jnp.minimum(n - 1 - me, n - 2), span, :].astype(F32)
+            from_right = self.landing[1, jnp.minimum(me, n - 2), span, :].astype(F32)
+            value = value + jnp.where(me > 0, from_left, 0.0)
+            value = value + jnp.where(me < n - 1, from_right, 0.0)
+            out_ref[span, :] = value.astype(out_ref.dtype)
+
+        self.spans(total)
+        for step, side, owner, beyond, edge in self.places():
 
             @pl.when(beyond)
             def _():
-                copy(part_ref.at[owner], step, side).wait_send()
+                self.copy(self.part.at[owner], step, side).wait_send()
+
+
+def line_sum_scratch(n, rows, width):
+    return [
+        pltpu.VMEM((2, n - 1, rows, width), BF),
+        pltpu.VMEM((2, n - 1, rows, width), BF),
+        pltpu.SemaphoreType.DMA((2, n - 1)),
+        pltpu.SemaphoreType.DMA((2, n - 1)),
+    ]
+
+
+def line_scatter_kernel(n, part_ref, out_ref, *scratch):
+    line = LineSum(n, part_ref, *scratch)
+    greet(line.neighbours())
+    line.start()
+    for step in range(n - 1):
+        line.forward(step)
+    line.finish(out_ref)
 
 
 def line_scatter(value, n, dtype, collective_id, name):
@@ -246,12 +278,7 @@
         out_shape=jax.ShapeDtypeStruct((rows, width), dtype),
         in_specs=[IN_VMEM],
         out_specs=IN_VMEM,
-        scratch_shapes=[
-            pltpu.VMEM((2, n - 1, rows, width), BF),
-            pltpu.VMEM((2, n - 1, rows, width), BF),
-            pltpu.SemaphoreType.DMA((2, n - 1)),
-            pltpu.SemaphoreType.DMA((2, n - 1)),
-        ],
+        scratch_shapes=line_sum_scratch(n, rows, width),
         compiler_params=pltpu.CompilerParams(collective_id=collective_id, has_side_effects=True),
         cost_estimate=pl.CostEstimate(flops=0, bytes_accessed=100000000, transcendentals=0),
         name=name,
@@ -266,9 +293,9 @@
 
 
 def weights_kernel(n, pieces, widths, *refs):
-    wq, wk, wv, wo, small = refs[:5]
-    outs, owns = refs[5:8], refs[8:11]
-    load, store, zsend, zrecv, psend, precv, csend, crecv = refs[11:]
+    wq, wk, wv, wo, small, extra = refs[:6]
+    outs, extra_out, owns = refs[6:9], refs[9], refs[10:13]
+    load, store, zsend, zrecv, psend, precv, csend, crecv, xsend, xrecv = refs[13:]
     group, me, (y, x, c), (by_y, by_x, by_c) = plane_position()
     left, right = (group, me - 1), (group, me + 1)
     eighth = owns[0].shape[0]
@@ -292,6 +319,7 @@
     stores = [
         pltpu.make_async_copy(owns[i], outs[i].at[me, y, x, c], store.at[i]) for i in range(3)
     ]
+    stores.append(pltpu.make_async_copy(extra, extra_out.at[me], store.at[3]))
     for copy in stores:
         copy.start()
     greet(
@@ -313,6 +341,17 @@
     def sends(step, side):
         return (me - step >= 0) & (me < n - 1) if side == 0 else (me + step < n) & (me > 0)
 
+    def extra_hop(step, side):
+        block = me - step if side == 0 else me + step
+        source = extra if step == 0 else extra_out.at[block]
+        return remote(
+            source,
+            extra_out.at[block],
+            xsend.at[side, step],
+            xrecv.at[side, step],
+            right if side == 0 else left,
+        )
+
     def first(slot, block, p):
         i, start, width, along_x = pieces[p]
         spot = outs[i].at[block, y, x, c, :, start : start + width]
@@ -385,6 +424,19 @@
                     for i in range(3):
                         third(slot, block, i).start()
 
+            for side in (0, 1):
+                if step > 2:
+
+                    @pl.when(me - step + 2 >= 0 if side == 0 else me + step - 2 < n)
+                    def _():
+                        extra_hop(step - 3, side).wait_recv()
+
+                if step < n + 1:
+
+                    @pl.when(sends(step - 2, side))
+                    def _():
+                        extra_hop(step - 2, side).start()
+
     for step in range(n):
         for slot, block, there in held(step):
 
@@ -403,6 +455,7 @@
                 def _():
                     for i in range(3):
                         hop(i, step, side).wait_send()
+                    extra_hop(step, side).wait_send()
 
 
 def path_pieces(query_width, key_width, out_width, small_width):
@@ -415,38 +468,44 @@
     )
 
 
-def gather_weights(wq, wk, wv, wo, small, n, collective_id):
+def gather_weights(wq, wk, wv, wo, small, extra, n, collective_id):
     rows = wq.shape[0]
     eighth = rows // 8
     widths = (wq.shape[1] + wk.shape[1] + wv.shape[1], wo.shape[1], small.shape[1])
     pieces = path_pieces(wq.shape[1], wk.shape[1], wo.shape[1], small.shape[1])
     outs = pl.pallas_call(
         functools.partial(weights_kernel, n, pieces, widths),
-        out_shape=[jax.ShapeDtypeStruct((n, 2, 2, 2, eighth, w), BF) for w in widths],
-        in_specs=[ANY] * 5,
-        out_specs=[ANY] * 3,
+        out_shape=[jax.ShapeDtypeStruct((n, 2, 2, 2, eighth, w), BF) for w in widths]
+        + [jax.ShapeDtypeStruct((n,) + extra.shape, BF)],
+        in_specs=[ANY] * 5 + [IN_VMEM],
+        out_specs=[ANY] * 4,
         scratch_shapes=[pltpu.VMEM((eighth, w), BF) for w in widths]
         + [
             pltpu.SemaphoreType.DMA((5,)),
-            pltpu.SemaphoreType.DMA((3,)),
+            pltpu.SemaphoreType.DMA((4,)),
             pltpu.SemaphoreType.DMA((2, n - 1, 3)),
             pltpu.SemaphoreType.DMA((2, n - 1, 3)),
             pltpu.SemaphoreType.DMA((2, 2 * n - 1, 4)),
             pltpu.SemaphoreType.DMA((2, 2 * n - 1, 4)),
             pltpu.SemaphoreType.DMA((2 * n - 1, 3)),
             pltpu.SemaphoreType.DMA((2 * n - 1, 3)),
+            pltpu.SemaphoreType.DMA((2, n - 1)),
+            pltpu.SemaphoreType.DMA((2, n - 1)),
         ],
         compiler_params=pltpu.CompilerParams(collective_id=collective_id, has_side_effects=True),
         cost_estimate=pl.CostEstimate(flops=0, bytes_accessed=100000000, transcendentals=0),
         name="gather_weights",
-    )(wq, wk, wv, wo, small)
-    return [o.reshape(n * rows, w) for o, w in zip(outs, widths)]
+    )(wq, wk, wv, wo, small, extra)
+    weights = [o.reshape(n * rows, w) for o, w in zip(outs, widths)]
+    return weights + [outs[3].reshape(-1, extra.shape[1])]
 
 
 def reduce_kernel(n, pieces, *refs):
-    ins, outs = refs[:3], refs[3:5]
-    pair, one, two, landing, staging = refs[5:7], refs[7:9], refs[9:11], refs[11:13], refs[13:15]
-    csend, crecv, psend, precv, zsend, zrecv, gsend, grecv = refs[15:]
+    ins, y_part, outs, y_out = refs[:3], refs[3], refs[4:6], refs[6]
+    refs = refs[7:]
+    pair, one, two, landing, staging = refs[:2], refs[2:4], refs[4:6], refs[6:8], refs[8:10]
+    csend, crecv, psend, precv, zsend, zrecv, gsend, grecv = refs[10:18]
+    line = LineSum(n, y_part, *refs[18:])
     group, me, (y, x, c), (by_y, by_x, by_c) = plane_position()
     left, right = (group, me - 1), (group, me + 1)
     eighth = pair[0].shape[3]
@@ -472,6 +531,7 @@
 
     for p in range(len(places)):
         swap(p).start()
+    line.start()
     for p in range(len(places)):
         swap(p).wait_recv()
         array, start, width, path, at = places[p]
@@ -499,6 +559,7 @@
 
     for path in (0, 1):
         first(path).start()
+    line.forward(0)
     for path in (0, 1):
         first(path).wait_recv()
 
@@ -510,6 +571,8 @@
 
         lax.fori_loop(0, 2 * n, first_sum, 0)
         second(path).start()
+    for step in range(1, n - 1):
+        line.forward(step)
     for path in (0, 1):
         second(path).wait_recv()
 
@@ -583,6 +646,8 @@
     for stage in range(3):
         for path in (0, 1):
             spread(path, stage).start()
+        if stage == 0:
+            line.finish(y_out)
         for path in (0, 1):
             spread(path, stage).wait_recv()
 
@@ -604,7 +669,7 @@
                     hop(two[path].at[owner], path, step, side).wait_send()
 
 
-def reduce_weights(grad_qkv, grad_out, grad_small, query_width, n, collective_id):
+def reduce_weights(grad_qkv, grad_out, grad_small, y_part, query_width, n, collective_id):
     values = (grad_qkv, grad_out, grad_small)
     rows = grad_qkv.shape[0] // n
     eighth = rows // 8
@@ -616,43 +681,53 @@
     scratch += [pltpu.VMEM((n, eighth, w), BF) for w in widths]
     scratch += [pltpu.VMEM((2, n - 1, eighth, w), BF) for w in widths] * 2
     sems = [(4,), (4,), (2, 2), (2, 2), (2, 2, n - 1), (2, 2, n - 1), (2, 3), (2, 3)]
+    y_rows = y_part.shape[0] // n
     outs = pl.pallas_call(
         functools.partial(reduce_kernel, n, pieces),
-        out_shape=[jax.ShapeDtypeStruct((2, 2, 2, eighth, w), BF) for w in widths],
-        in_specs=[IN_VMEM] * 3,
-        out_specs=[IN_VMEM] * 2,
-        scratch_shapes=scratch + [pltpu.SemaphoreType.DMA(s) for s in sems],
+        out_shape=[jax.ShapeDtypeStruct((2, 2, 2, eighth, w), BF) for w in widths]
+        + [jax.ShapeDtypeStruct((y_rows, y_part.shape[1]), F32)],
+        in_specs=[IN_VMEM] * 4,
+        out_specs=[IN_VMEM] * 3,
+        scratch_shapes=scratch
+        + [pltpu.SemaphoreType.DMA(s) for s in sems]
+        + line_sum_scratch(n, y_rows, y_part.shape[1]),
         compiler_params=pltpu.CompilerParams(
             collective_id=collective_id, has_side_effects=True, vmem_limit_bytes=48 * 1024 * 1024
         ),
         cost_estimate=pl.CostEstimate(flops=0, bytes_accessed=100000000, transcendentals=0),
         name="reduce_weights",
-    )(*[v.reshape(n, 2, 2, 2, eighth, v.shape[1]) for v in values])
+    )(
+        *[v.reshape(n, 2, 2, 2, eighth, v.shape[1]) for v in values],
+        y_part.reshape(n, y_rows, y_part.shape[1]),
+    )
     first, second = [o.reshape(rows, w) for o, w in zip(outs, widths)]
     cut = pieces[0][2]
     rest = pieces[1][2]
     qkv = jnp.concatenate([first[:, :cut], second[:, :rest]], axis=1)
-    return qkv, second[:, rest:], first[:, cut:]
+    return qkv, second[:, rest:], first[:, cut:], outs[2]
 
 
 def expert_kernel(sizes, plane, *refs):
     blocks, rows, local, capacity = sizes
-    x_ref, ct_ref, router_t_ref, rank_row_ref, rank_col_ref = refs[:5]
-    w_gate_ref, w_up_ref, w_down_ref = refs[5:8]
-    y_ref, gs_ref, out_gate_ref, out_up_ref, out_down_ref = refs[8:13]
-    xs_ref, g_ref, gate_slot_ref, dots_ref = refs[13:17]
+    x_ref, ct_low_ref, ct_high_ref, router_t_ref, rank_row_ref, rank_col_ref = refs[:6]
+    w_gate_ref, w_up_ref, w_down_ref = refs[6:9]
+    y_ref, gs_ref, out_gate_ref, out_up_ref, out_down_ref = refs[9:14]
+    xs_ref, g_ref, gate_slot_ref, dots_ref = refs[14:18]
+    refs = refs[18:]
     slots = local * capacity
     step = pl.program_id(0)
     base = lax.axis_index("expert") * local
     if plane:
-        stage_refs, pair_refs, one_refs, two_refs = refs[17:20], refs[20:23], refs[23:27], refs[27:31]
-        csend, crecv, psend, precv, qsend, qrecv = refs[31:]
+        stage_refs, pair_refs, one_refs, two_refs = refs[:3], refs[3:6], refs[6:10], refs[10:14]
+        csend, crecv, psend, precv, qsend, qrecv = refs[14:20]
+        gs_part = refs[20]
+        line = LineSum(blocks, gs_part, *refs[21:])
         _, _, (y, x, c), (by_y, by_x, by_c) = plane_position()
         half = stage_refs[2].shape[4] // 2
 
         @pl.when(step == 0)
         def _():
-            greet([(None, by_c), (None, by_x), (None, by_y)])
+            greet([(None, by_c), (None, by_x), (None, by_y)] + line.neighbours())
 
     @pl.when(step == 0)
     def _():
@@ -678,7 +753,9 @@
                 pieces.append(jnp.where(taken, 1.0, 0.0).astype(BF))
             pick = jnp.concatenate(pieces, axis=0)
             xs_ref[b] = dot(pick, x_ref[here, :]).astype(BF)
-            g_ref[b] = dot(pick, ct_ref[here, :]).astype(BF)
+            middle = ct_low_ref.shape[1]
+            g_ref[b, :, :middle] = dot(pick, ct_low_ref[here, :]).astype(BF)
+            g_ref[b, :, middle:] = dot(pick, ct_high_ref[here, :]).astype(BF)
 
     @pl.when(step < local)
     def _():
@@ -735,8 +812,13 @@
             ranks = dot(rank_col_ref[there, :], spread)
             put = jnp.where(ranks == slot_rank, 1.0, 0.0).astype(BF)
             y_ref[there, :] = dot(put, g_ref[b]).astype(BF)
-            gs_ref[there, :D] = dot(put, xs_ref[b]).astype(BF)
-            gs_ref[there, D:] = dot(put, dots_ref[b]).astype(BF)
+            back = dot(put, xs_ref[b]).astype(BF), dot(put, dots_ref[b]).astype(BF)
+            if plane:
+                gs_part[b, :, :D], gs_part[b, :, D:] = back
+            else:
+                gs_ref[there, :D], gs_ref[there, D:] = back
+        if plane:
+            line.start()
 
     if not plane:
         return
@@ -830,9 +912,31 @@
         for i in range(3):
             swap(step, i).start()
 
+    @pl.when(step == local + 1)
+    def _():
+        line.forward(0)
+
+    @pl.when(step == local + 2)
+    def _():
+        for k in range(1, blocks - 1):
+            line.forward(k)
+        line.finish(gs_ref)
+
 
 def run_experts(
-    x_all, ct_all, router_t, rank_row, rank_col, w_gate, w_up, w_down, rows, capacity, plane, collective_id
+    x_all,
+    ct_low,
+    ct_high,
+    router_t,
+    rank_row,
+    rank_col,
+    w_gate,
+    w_up,
+    w_down,
+    rows,
+    capacity,
+    plane,
+    collective_id,
 ):
     total = x_all.shape[0]
     blocks, local = total // rows, w_gate.shape[0]
@@ -862,34 +966,39 @@
         scratch += [pltpu.VMEM((2,) + shape, BF) for shape in passed]
         sems = [(2, 3), (3, 3), (3, 4), (3, 4), (2, 4), (2, 4)]
         scratch += [pltpu.SemaphoreType.DMA(shape) for shape in sems]
+        scratch += [pltpu.VMEM((blocks, rows, D + LANES), BF)]
+        scratch += line_sum_scratch(blocks, rows, D + LANES)
+        gs_shape, gs_type = (rows, D + LANES), F32
         params |= dict(collective_id=collective_id, has_side_effects=True)
     else:
         grad_shapes, grad_specs = shapes, [per(shape) for shape in shapes]
+        gs_shape, gs_type = (total, D + LANES), BF
     flops = 2 * total * D * slots * 4 // blocks + 18 * blocks * slots * D * FF
     return pl.pallas_call(
         functools.partial(expert_kernel, sizes, plane),
         grid=(local + 3 if plane else local,),
         out_shape=[
             jax.ShapeDtypeStruct((total, D), BF),
-            jax.ShapeDtypeStruct((total, D + LANES), BF),
+            jax.ShapeDtypeStruct(gs_shape, gs_type),
         ]
         + [jax.ShapeDtypeStruct((local,) + shape, BF) for shape in grad_shapes],
         in_specs=[
             whole((total, D)),
-            whole((total, D)),
+            whole(ct_low.shape),
+            whole(ct_high.shape),
             whole((EXPERTS, D)),
             whole((EXPERTS, total)),
             whole((total, EXPERTS)),
         ]
         + [per(shape) for shape in shapes],
-        out_specs=[whole((total, D)), whole((total, D + LANES))] + grad_specs,
+        out_specs=[whole((total, D)), whole(gs_shape)] + grad_specs,
         scratch_shapes=scratch,
         compiler_params=pltpu.CompilerParams(**params),
         cost_estimate=pl.CostEstimate(
             flops=flops, bytes_accessed=2 * (6 * local * D * FF + 4 * total * D), transcendentals=0
         ),
         name="experts",
-    )(x_all, ct_all, router_t, rank_row, rank_col, w_gate, w_up, w_down)
+    )(x_all, ct_low, ct_high, router_t, rank_row, rank_col, w_gate, w_up, w_down)
 
 
 def mask_bias(bias_ref, length_ref, rows):
@@ -915,15 +1024,114 @@
     ref[:, middle : middle + HEAD_DIMENSION] = value[rows:].astype(ref.dtype)
 
 
-def attention_kernel(length_ref, q_ref, kv_ref, mixed_ref, log_total_ref, bias_ref):
-    @pl.when(pl.program_id(0) == 0)
-    def _():
-        mask_bias(bias_ref, length_ref, q_ref.shape[0])
-
+def attention_kernel(
+    n, length_ref, q_ref, kv_ref, rank_ref, mixed_ref, log_total_ref, kv_all_ref, rank_all_ref, *scratch
+):
+    bias_ref, chunk_ref, rank_buffer, send, recv, rank_send, rank_recv = scratch
+    pair, pairs = pl.program_id(0), pl.num_programs(0)
+    group, me = lax.axis_index("group"), lax.axis_index("expert")
+    left, right = (group, me - 1), (group, me + 1)
+    rows, width = kv_ref.shape[1:]
+
+    def hop(j, step, side):
+        block = me - step if side == 0 else me + step
+        source = kv_ref.at[j] if step == 0 else chunk_ref.at[j, block]
+        index = (j, side, step)
+        return remote(
+            source,
+            chunk_ref.at[j, block],
+            send.at[index],
+            recv.at[index],
+            right if side == 0 else left,
+        )
+
+    def rank_hop(step, side):
+        block = me - step if side == 0 else me + step
+        source = rank_ref if step == 0 else rank_buffer.at[block]
+        index = (side, step)
+        return remote(
+            source,
+            rank_buffer.at[block],
+            rank_send.at[index],
+            rank_recv.at[index],
+            right if side == 0 else left,
+        )
+
+    def sends(step, side):
+        return (me - step >= 0) & (me < n - 1) if side == 0 else (me + step < n) & (me > 0)
+
+    def arrives(step, side):
+        return me - 1 - step >= 0 if side == 0 else me + 1 + step < n
+
+    def launch(make, step):
+        for side in (0, 1):
+
+            @pl.when(sends(step, side))
+            def _():
+                make(step, side).start()
+
+    def await_hop(make, step):
+        for side in (0, 1):
+
+            @pl.when(arrives(step, side))
+            def _():
+                make(step, side).wait_recv()
+
+    def drain(make):
+        for step in range(n - 1):
+            for side in (0, 1):
+
+                @pl.when(sends(step, side))
+                def _():
+                    make(step, side).wait_send()
+
+    def chunk(j):
+        return lambda step, side: hop(j, step, side)
+
+    @pl.when(pair == 0)
+    def _():
+        greet([(me > 0, left), (me < n - 1, right)])
+        launch(chunk(0), 0)
+        rank_buffer[me] = rank_ref[...]
+        launch(chunk(1), 0)
+        mask_bias(bias_ref, length_ref, rows)
+        await_hop(chunk(0), 0)
+        launch(chunk(0), 1)
+
+    for step in range(1, n - 1):
+        await_hop(chunk(pair), step)
+        if step < n - 2:
+            launch(chunk(pair), step + 1)
+
+    @pl.when(pair + 1 < pairs)
+    def _():
+        await_hop(chunk(pair + 1), 0)
+        launch(chunk(pair + 1), 1)
+
+    @pl.when(pair + 2 < pairs)
+    def _():
+        launch(chunk(pair + 2), 0)
+
+    @pl.when(pair == 1)
+    def _():
+        launch(rank_hop, 0)
+
+    for step in range(n - 1):
+
+        @pl.when(pair == jnp.minimum(2 + step, pairs - 1))
+        def _():
+            await_hop(rank_hop, step)
+            if step < n - 2:
+                launch(rank_hop, step + 1)
+
+    chunk_ref[pair, me] = kv_ref[pair]
+    kv = chunk_ref[pair].reshape(n * rows, width)
+    kv_all_ref[...] = kv
     bias = jnp.concatenate([bias_ref[...]] * 2, axis=1)
     for head in (0, 1):
-        columns = slice(head * HEAD_DIMENSION, (head + 1) * HEAD_DIMENSION)
-        key, value = kv_ref[:, :LANES][:, columns], kv_ref[:, LANES:][:, columns]
+        start = head * HEAD_DIMENSION
+        key = kv[:, start : start + HEAD_DIMENSION]
+        value = kv[:, LANES + start : LANES + start + HEAD_DIMENSION]
         query = head_columns(q_ref, head) * jnp.asarray(HEAD_DIMENSION**-0.5, BF)
         scores = dot_nt(key, query) + bias
         top = jnp.max(scores, axis=0, keepdims=True)
@@ -932,45 +1140,106 @@
         put_heads(mixed_ref, head, dot_tn(value, weights.astype(BF)) / total)
         log_total_ref[0, head : head + 1, :] = top + jnp.log(total)
 
-
-def attention(length, query, kv_all):
-    rows, keys = query.shape[0], kv_all.shape[0]
+    @pl.when(pair == pairs - 1)
+    def _():
+        drain(rank_hop)
+        rank_all_ref[...] = rank_buffer[...]
+        for j in range(KEY_VALUE_HEADS // 2):
+            drain(chunk(j))
+
+
+def attention(length, query, kv, rank, n, collective_id):
+    rows = query.shape[0]
+    keys, width = n * rows, 2 * LANES
     pairs = KEY_VALUE_HEADS // 2
     return pl.pallas_call(
-        attention_kernel,
+        functools.partial(attention_kernel, n),
         grid=(pairs,),
         out_shape=(
             jax.ShapeDtypeStruct(query.shape, BF),
             jax.ShapeDtypeStruct((pairs, 2, 2 * rows), F32),
+            jax.ShapeDtypeStruct((keys, pairs * width), BF),
+            jax.ShapeDtypeStruct((n,) + rank.shape, rank.dtype),
         ),
         in_specs=[
             pl.BlockSpec(memory_space=pltpu.SMEM),
-            pl.BlockSpec((rows, 2 * LANES), lambda j: (0, j)),
-            pl.BlockSpec((keys, 2 * LANES), lambda j: (0, j)),
+            pl.BlockSpec((rows, width), lambda j: (0, j)),
+            IN_VMEM,
+            IN_VMEM,
         ],
         out_specs=(
-            pl.BlockSpec((rows, 2 * LANES), lambda j: (0, j)),
+            pl.BlockSpec((rows, width), lambda j: (0, j)),
             pl.BlockSpec((1, 2, 2 * rows), lambda j: (j, 0, 0)),
+            pl.BlockSpec((keys, width), lambda j: (0, j)),
+            IN_VMEM,
         ),
-        scratch_shapes=[pltpu.VMEM((keys, rows), F32)],
+        scratch_shapes=[
+            pltpu.VMEM((keys, rows), F32),
+            pltpu.VMEM((pairs, n, rows, width), BF),
+            pltpu.VMEM((n,) + rank.shape, rank.dtype),
+            pltpu.SemaphoreType.DMA((pairs, 2, n - 1)),
+            pltpu.SemaphoreType.DMA((pairs, 2, n - 1)),
+            pltpu.SemaphoreType.DMA((2, n - 1)),
+            pltpu.SemaphoreType.DMA((2, n - 1)),
+        ],
         compiler_params=pltpu.CompilerParams(
-            dimension_semantics=("arbitrary",), vmem_limit_bytes=48 * 1024 * 1024
+            dimension_semantics=("arbitrary",),
+            vmem_limit_bytes=56 * 1024 * 1024,
+            collective_id=collective_id,
+            has_side_effects=True,
         ),
         cost_estimate=pl.CostEstimate(
-            flops=16 * rows * keys * D, bytes_accessed=4 * keys * D, transcendentals=0
+            flops=16 * rows * keys * D, bytes_accessed=100000000, transcendentals=0
         ),
         name="attention",
-    )(length, query, kv_all)
+    )(length, query, kv, rank)
 
 
 def attention_back_kernel(
-    length_ref, q_ref, kv_ref, grad_ref, log_total_ref, grad_q_ref, grad_kv_ref, bias_ref
+    n,
+    length_ref,
+    q_ref,
+    kv_ref,
+    grad_ref,
+    log_total_ref,
+    grad_q_ref,
+    grad_kv_ref,
+    bias_ref,
+    terms_ref,
+    landing,
+    staging,
+    send,
+    recv,
 ):
-    @pl.when(pl.program_id(0) == 0)
-    def _():
+    step, pairs = pl.program_id(0), pl.num_programs(0) - 1
+
+    def line(j):
+        return LineSum(
+            n, terms_ref.at[j], landing.at[j], staging.at[j], send.at[j], recv.at[j]
+        )
+
+    @pl.when(step == 0)
+    def _():
+        greet(line(0).neighbours())
         mask_bias(bias_ref, length_ref, q_ref.shape[0])
 
+    @pl.when(step < pairs)
+    def _():
+        attention_back_pair(
+            q_ref, kv_ref, grad_ref, log_total_ref, grad_q_ref, terms_ref.at[step], bias_ref
+        )
+        line(step).start()
+
+    @pl.when(step > 0)
+    def _():
+        for k in range(n - 1):
+            line(step - 1).forward(k)
+        line(step - 1).finish(grad_kv_ref)
+
+
+def attention_back_pair(q_ref, kv_ref, grad_ref, log_total_ref, grad_q_ref, grad_kv_ref, bias_ref):
     scale = HEAD_DIMENSION**-0.5
+    blocks, rows, _ = grad_kv_ref.shape
     bias = jnp.concatenate([bias_ref[...]] * 2, axis=1)
     for head in (0, 1):
         columns = slice(head * HEAD_DIMENSION, (head + 1) * HEAD_DIMENSION)
@@ -982,49 +1251,75 @@
         grad_probs = dot_nt(value, grad)
         delta = jnp.sum(probs * grad_probs, axis=0, keepdims=True)
         grad_scores = (probs * (grad_probs - delta)).astype(BF)
-        grad_kv_ref[:, head * HEAD_DIMENSION : (head + 1) * HEAD_DIMENSION] = dot(
-            grad_scores, query
-        ).astype(BF)
+        grad_key = dot(grad_scores, query).astype(BF).reshape(blocks, rows, HEAD_DIMENSION)
+        grad_kv_ref[:, :, columns] = grad_key
+        grad_value = dot(probs.astype(BF), grad).astype(BF).reshape(blocks, rows, HEAD_DIMENSION)
         start = LANES + head * HEAD_DIMENSION
-        grad_kv_ref[:, start : start + HEAD_DIMENSION] = dot(probs.astype(BF), grad).astype(BF)
+        grad_kv_ref[:, :, start : start + HEAD_DIMENSION] = grad_value
         put_heads(grad_q_ref, head, dot_tn(key, grad_scores) * scale)
 
 
-def attention_back(length, query, kv_all, grad_mixed, log_total):
+def attention_back(length, query, kv_all, grad_mixed, log_total, n, collective_id):
     rows, keys = query.shape[0], kv_all.shape[0]
-    pairs = KEY_VALUE_HEADS // 2
-    row_spec = pl.BlockSpec((rows, 2 * LANES), lambda j: (0, j))
-    key_spec = pl.BlockSpec((keys, 2 * LANES), lambda j: (0, j))
+    pairs, width = KEY_VALUE_HEADS // 2, 2 * LANES
+    now = lambda j: jnp.minimum(j, pairs - 1)
+    row_spec = pl.BlockSpec((rows, width), lambda j: (0, now(j)))
     return pl.pallas_call(
-        attention_back_kernel,
-        grid=(pairs,),
+        functools.partial(attention_back_kernel, n),
+        grid=(pairs + 1,),
         out_shape=(
             jax.ShapeDtypeStruct(query.shape, F32),
-            jax.ShapeDtypeStruct(kv_all.shape, BF),
+            jax.ShapeDtypeStruct((rows, pairs * width), BF),
         ),
         in_specs=[
             pl.BlockSpec(memory_space=pltpu.SMEM),
             row_spec,
-            key_spec,
+            pl.BlockSpec((keys, width), lambda j: (0, now(j))),
             row_spec,
-            pl.BlockSpec((1, 2, 2 * rows), lambda j: (j, 0, 0)),
+            pl.BlockSpec((1, 2, 2 * rows), lambda j: (now(j), 0, 0)),
         ],
-        out_specs=(row_spec, key_spec),
-        scratch_shapes=[pltpu.VMEM((keys, rows), F32)],
+        out_specs=(
+            row_spec,
+            pl.BlockSpec((rows, width), lambda j: (0, jnp.maximum(j - 1, 0))),
+        ),
+        scratch_shapes=[
+            pltpu.VMEM((keys, rows), F32),
+            pltpu.VMEM((pairs, n, rows, width), BF),
+            pltpu.VMEM((pairs, 2, n - 1, rows, width), BF),
+            pltpu.VMEM((pairs, 2, n - 1, rows, width), BF),
+            pltpu.SemaphoreType.DMA((pairs, 2, n - 1)),
+            pltpu.SemaphoreType.DMA((pairs, 2, n - 1)),
+        ],
         compiler_params=pltpu.CompilerParams(
-            dimension_semantics=("arbitrary",), vmem_limit_bytes=48 * 1024 * 1024
+            dimension_semantics=("arbitrary",),
+            vmem_limit_bytes=60 * 1024 * 1024,
+            collective_id=collective_id,
+            has_side_effects=True,
         ),
         cost_estimate=pl.CostEstimate(
-            flops=40 * rows * keys * D, bytes_accessed=6 * keys * D, transcendentals=0
+            flops=40 * rows * keys * D, bytes_accessed=100000000, transcendentals=0
         ),
         name="attention_back",
     )(length, query, kv_all, grad_mixed, log_total)
 
 
-def pair_columns(first, second):
-    rows = first.shape[0]
-    both = [value.reshape(rows, -1, 1, LANES) for value in (first, second)]
-    return jnp.concatenate(both, axis=2).reshape(rows, -1)
+def widen_kernel(value_ref, out_ref):
+    out_ref[...] = value_ref[...].astype(F32)
+
+
+def widen(value):
+    block = (1,) + value.shape[1:]
+    spec = pl.BlockSpec(block, lambda e: (e, 0, 0))
+    return pl.pallas_call(
+        widen_kernel,
+        grid=(value.shape[0],),
+        out_shape=jax.ShapeDtypeStruct(value.shape, F32),
+        in_specs=[spec],
+        out_specs=spec,
+        compiler_params=pltpu.CompilerParams(dimension_semantics=("arbitrary",)),
+        cost_estimate=pl.CostEstimate(flops=0, bytes_accessed=6 * value.size, transcendentals=0),
+        name="widen",
+    )(value)
 
 
 def unpair_columns(value):
@@ -1072,9 +1367,12 @@
         + [jnp.zeros((w_router.shape[0], LANES - EXPERTS - 2), BF)],
         axis=1,
     )
-    qkv_weight, out_weight, small = gather_weights(
-        w_query, key_projection, value_projection, w_out, small, n, 1
-    )
+    middle = D // 2
+    qkv_weight, out_weight, small, ct_low = gather_weights(
+        w_query, key_projection, value_projection, w_out, small, grad_output[:, :middle], n, 1
+    )
+    qkv_weight, ct_high = lax.optimization_barrier((qkv_weight, grad_output[:, middle:]))
+    ct_high = gather_rows(ct_high)
     router_weight = small[:, :EXPERTS]
     gain_one = small[:, EXPERTS].astype(F32)
     gain_two = small[:, EXPERTS + 1].astype(F32)
@@ -1102,25 +1400,38 @@
         unrotated_key.reshape(rows, KEY_VALUE_HEADS, HEAD_DIMENSION), cosine_lookup, sine_lookup
     ).astype(BF)
     local_keys = local_keys.reshape(rows, key_width)
-    kv_all, rank_all = line_gather(
-        [pair_columns(local_keys, value_pre.astype(BF)), rank], n, 2, "gather_kv"
-    )
-    rank_all = rank_all.reshape(n, EXPERTS, rows)
+    own_kv = jnp.stack(
+        [
+            jnp.concatenate([local_keys[:, cut], value_pre[:, cut].astype(BF)], axis=1)
+            for cut in [slice(i, i + LANES) for i in range(0, key_width, LANES)]
+        ]
+    )
+    mixed_low, log_total, kv_all, rank_all = attention(lengths, query_rows, own_kv, rank, n, 2)
     rank_row = jnp.transpose(rank_all, (1, 0, 2)).reshape(EXPERTS, n * rows).astype(F32)
     rank_col = jnp.transpose(rank_all, (0, 2, 1)).reshape(n * rows, EXPERTS)
-    grad_output_late, kv_all = lax.optimization_barrier((grad_output, kv_all))
-    ct_all = gather_rows(grad_output_late)
-    mixed_low, log_total = attention(lengths, query_rows, kv_all)
     residual = token_f32 + dot(mixed_low, out_weight)
     inverse_two = lax.rsqrt(jnp.mean(residual * residual, axis=-1, keepdims=True) + EPSILON)
     unit_two = residual * inverse_two
     second_norm = (unit_two * gain_two).astype(BF)
     (x_all,) = line_gather([second_norm], n, 3, "gather_rows")
 
-    y_part, gs_part, grad_gate, grad_up, grad_down = run_experts(
-        x_all, ct_all, router_weight.T, rank_row, rank_col, w_gate, w_up, w_down, rows, capacity, groups == 8, 7
-    )
-    gs = line_scatter(gs_part, n, F32, 4, "scatter_grads")
+    y_part, gs, grad_gate, grad_up, grad_down = run_experts(
+        x_all,
+        ct_low,
+        ct_high,
+        router_weight.T,
+        rank_row,
+        rank_col,
+        w_gate,
+        w_up,
+        w_down,
+        rows,
+        capacity,
+        groups == 8,
+        7,
+    )
+    if groups != 8:
+        gs = line_scatter(gs, n, F32, 4, "scatter_grads")
 
     logits = dot(second_norm, router_weight)
     chosen = jnp.where(hot, logits, NEGATIVE_LARGE)
@@ -1141,13 +1452,9 @@
     grad_attn = grad_residual.astype(BF)
     grad_out = dot_tn(mixed_low, grad_attn)
     mixed_gradient = dot_nt(grad_attn, out_weight).astype(BF)
-    grad_query_acc, kv_terms = attention_back(
-        lengths, query_rows, kv_all, mixed_gradient, log_total
-    )
-    kv_gradient = line_scatter(kv_terms, n, BF, 5, "scatter_kv")
-    kv_gradient, y_part = lax.optimization_barrier((kv_gradient, y_part))
-    expert_sum = scatter_rows(y_part).astype(F32)
-    mixed = (residual + expert_sum).astype(BF)
+    grad_query_acc, kv_gradient = attention_back(
+        lengths, query_rows, kv_all, mixed_gradient, log_total, n, 5
+    )
     own_key_gradient, own_value_gradient = unpair_columns(kv_gradient)
     grad_query_pre = (
         apply_rotation(
@@ -1179,15 +1486,17 @@
     )
     shares = (grad_qkv.astype(BF), grad_out.astype(BF), grad_small.astype(BF))
     if groups == 8:
-        shares = reduce_weights(*shares, query_width, n, 6)
+        *shares, expert_sum = reduce_weights(*shares, y_part, query_width, n, 6)
     else:
         shares = [lax.psum(scatter_rows(share), "group") for share in shares]
+        expert_sum = line_scatter(y_part, n, F32, 8, "scatter_outputs")
+    mixed = (residual + expert_sum).astype(BF)
     share_qkv, share_out, share_small = [share.astype(F32) for share in shares]
 
     def sum_over_groups(value):
         if groups != 8:
             value = lax.psum_scatter(value, "group", scatter_dimension=1, tiled=True)
-        return lax.all_gather(value, "group", axis=1, tiled=True).astype(F32)
+        return widen(lax.all_gather(value, "group", axis=1, tiled=True))
 
     return (
         mixed,

time: 685 us -> 579 us (0.85)
  waiting for transfers between devices: 82.2 us -> 1.25 us
  other arithmetic: 54.6 us -> 18.5 us
  Pallas kernels: 478 us -> 488 us
    all_gather x3, waiting for transfers between devices: 80.5 us -> 0.01 us  [sum_over_groups(): return widen(lax.all_gather(value, 'group', axis=1, tiled=True))]
    pallas_call x2 -> x1, Pallas kernels: 101 us -> 37 us  [line_gather(): pl.pallas_call(functools.partial(line_gather_kernel, n, count), out_shape...]
    convert_element_type x3 -> x0, other arithmetic: 36.7 us -> none  [sum_over_groups(): return lax.all_gather(value, 'group', axis=1, tiled=True).astype(F32)]
    pallas_call x4 -> x5, Pallas kernels: 123 us -> 154 us  [the longest x1 72.5 us: attention_back(): pl.pallas_call(functools.partial(attention_back_kernel, n), grid=(pairs +...]
    pallas_call x1, Pallas kernels: 126 us -> 156 us  [run_experts(): pl.pallas_call(functools.partial(expert_kernel, sizes, plane), grid=(loca...]
    pallas_call x1, Pallas kernels: 40.8 us -> 48.1 us  [gather_weights(): pl.pallas_call(functools.partial(weights_kernel, n, pieces, widths), out_...]
  transfers between devices with their start and end apart: 5 -> 4, of which waited for: 2 -> 0; matrix products, arithmetic and copies ran while one was open for 9% -> 11% of each run, Pallas kernels for 23% -> 48%
where the time goes in v5:
time: 579 us; the launch traced here: 572 us
  Pallas kernels  488 us (84%)
  local copies, waits for them, and re-layouts  28.7 us (5%)
  matrix products  20.6 us (4%)
  other arithmetic  18.5 us (3%)
  between operations  15.3 us (3%)
    pallas_call x1, Pallas kernels, run_experts(): pl.pallas_call(functools.partial(expert_kernel, sizes, plane), grid=(loca...  156 us
    pallas_call x1, Pallas kernels, reduce_weights(): pl.pallas_call(functools.partial(reduce_kernel, n, pieces), out_shape=[ja...  92.1 us
    pallas_call x1, Pallas kernels, attention_back(): pl.pallas_call(functools.partial(attention_back_kernel, n), grid=(pairs +...  72.5 us
    pallas_call x1, Pallas kernels, attention(): pl.pallas_call(functools.partial(attention_kernel, n), grid=(pairs,), out...  50.9 us
    pallas_call x1, Pallas kernels, gather_weights(): pl.pallas_call(functools.partial(weights_kernel, n, pieces, widths), out_...  48.1 us
    pallas_call x1, Pallas kernels, line_gather(): pl.pallas_call(functools.partial(line_gather_kernel, n, count), out_shape...  37 us
    pallas_call x3, Pallas kernels, widen(): pl.pallas_call(widen_kernel, grid=(value.shape[0],), out_shape=jax.ShapeD...  30.8 us
  transfers between devices with their start and end apart: 4, of which 0 were waited for; matrix products, arithmetic and copies ran while one was open for 11% of the time, Pallas kernels for 48%

profile of v5, /device:TPU:0, one launch (start us, length us, event | category | flops | bytes accessed | tf_op | source)
XLA Modules:
  0.0 572.3 jit_solution(11008520490806607638)
XLA Ops:
  13.1 48.1 %gather_weights.1 = (bf16[4,2,2,2,32,2048]{5,4,3,2,1,0:T(8,128)(2,1)}, bf16[4,2,2,2,32,1024]{5,4,3,2,1,0:T(8,128)(2,1)}, bf16[4,2,2,2,32,128]{5,4,3,2,1,0:T(8,128)(2,1)}, bf16[4,256,512]{2,1,0:T(8,128)(2,1)}) custom-call(bf16[256,1024]{1,0:T(8,128)(2,1)} %refs_0_.1, bf16[256,512]{1,0:T(8,128)(2,1)} %refs_1_.1, bf16[256,512]{1,0:T(8,128)(2,1)} %refs_2_.1, ...), custom_call_target="tpu_custom_call" | custom-call | bytes 100000000 | tf_op jit(solution)/shard_map/gather_weights/pallas_call | solution.py:476
  61.6 1.4 convert_reduce_fusion
  63.0 4.5 fusion.33
  72.0 1.6 copy.89
  76.7 50.9 %attention.1 = (bf16[256,1024]{1,0:T(8,128)(2,1)}, f32[4,2,512]{2,1,0:T(2,128)}, bf16[1024,1024]{1,0:T(8,128)(2,1)}, bf16[4,32,256]{2,1,0:T(8,128)(2,1)}) custom-call(s32[1]{0:T(128)} %copy.124.length_ref, bf16[256,1024]{1,0:T(8,128)(2,1)} %copy.95.q_ref, bf16[4,256,256]{2,1,0:T(8,128)(2,1)} %pad_maximum_fusion.2.kv_ref, bf16[32,256]{1,0:T(8,128)(2,1)} %fusion.4.rank_ref), custom_call_target="tpu_custom_call" | custom-call | flops 4294967296 | bytes 100000000 | tf_op jit(solution)/shard_map/attention/pallas_call | solution.py:1155
  129.1 1.7 copy.98
  130.8 2.6 multiply_reduce_fusion.2
  134.3 37.0 %gather_rows.1 = bf16[4,256,1024]{2,1,0:T(8,128)(2,1)} custom-call(bf16[256,1024]{1,0:T(8,128)(2,1)} %multiply_convert_fusion.refs_0_), custom_call_target="tpu_custom_call" | custom-call | bytes 100000000 | tf_op jit(solution)/shard_map/gather_rows/pallas_call | solution.py:152
  171.4 156.5 %experts.1 = (bf16[1024,1024]{1,0:T(8,128)(2,1)}, f32[256,1152]{1,0:T(8,128)}, bf16[8,128,512]{2,1,0:T(8,128)(2,1)}, bf16[8,128,512]{2,1,0:T(8,128)(2,1)}, bf16[8,64,1024]{2,1,0:T(8,128)(2,1)}) custom-call(bf16[1024,1024]{1,0:T(8,128)(2,1)} %bitcast.70, bf16[1024,512]{1,0:T(8,128)(2,1)} %bitcast.89, bf16[1024,512]{1,0:T(8,128)(2,1)} %all-gather.5.cloned.1.call-done.refs_2_, ...), custom_call_target="tpu_custom_call" | custom-call | flops 30601641984 | bytes 58720256 | tf_op jit(solution)/shard_map/experts/pallas_call | solution.py:977
  332.7 1.6 convolution_convert_fusion.2.grad_ref
  334.2 72.5 %attention_back.1 = (f32[256,1024]{1,0:T(8,128)}, bf16[256,1024]{1,0:T(8,128)(2,1)}) custom-call(s32[1]{0:T(128)} %copy.124.length_ref, bf16[256,1024]{1,0:T(8,128)(2,1)} %copy.95.q_ref, bf16[1024,1024]{1,0:T(8,128)(2,1)} %get-tuple-element.37.kv_ref, bf16[256,1024]{1,0:T(8,128)(2,1)} %convolution_convert_fusion.2.grad_ref, ...), custom_call_target="tpu_custom_call" | custom-call | flops 10737418240 | bytes 100000000 | tf_op jit(solution)/shard_map/attention_back/pallas_call | solution.py:1267
  406.7 2.5 copy.103
  410.8 1.6 reshape.232
  412.4 1.7 fusion.29
  416.1 1.9 copy.117
  419.2 1.5 subtract_convert_fusion
  420.8 4.8 fusion.7
  428.1 1.9 convolution_convert_fusion.1
  430.0 3.5 convolution_convert_fusion
  433.4 92.1 %reduce_weights.1 = (bf16[2,2,2,32,1664]{4,3,2,1,0:T(8,128)(2,1)S(1)}, bf16[2,2,2,32,1536]{4,3,2,1,0:T(8,128)(2,1)S(1)}, f32[256,1024]{1,0:T(8,128)S(1)}) custom-call(bf16[4,2,2,2,32,2048]{5,4,3,2,1,0:T(8,128)(2,1)} %bitcast.65, bf16[4,2,2,2,32,1024]{5,4,3,2,1,0:T(8,128)(2,1)S(1)} %bitcast.54, ...), custom_call_target="tpu_custom_call" | custom-call | bytes 100000000 | tf_op jit(solution)/shard_map/reduce_weights/pallas_call | solution.py:685
  527.3 1.4 maximum_convert_fusion
  534.8 10.3 %widen.5 = f32[8,512,1024]{2,1,0:T(8,128)} custom-call(bf16[8,512,1024]{2,1,0:T(8,128)(2,1)} %all-gather.11.cloned.1.call-done.value_ref), custom_call_target="tpu_custom_call" | custom-call | bytes 25165824 | tf_op jit(solution)/shard_map/widen/pallas_call | solution.py:1313
  545.1 10.3 %widen.4 = f32[8,1024,512]{2,1,0:T(8,128)} custom-call(bf16[8,1024,512]{2,1,0:T(8,128)(2,1)} %all-gather.9.cloned.1.call-done.value_ref), custom_call_target="tpu_custom_call" | custom-call | bytes 25165824 | tf_op jit(solution)/shard_map/widen/pallas_call | solution.py:1313
  555.4 10.3 %widen.3 = f32[8,1024,512]{2,1,0:T(8,128)} custom-call(bf16[8,1024,512]{2,1,0:T(8,128)(2,1)} %all-gather.7.cloned.1.call-done.value_ref), custom_call_target="tpu_custom_call" | custom-call | bytes 25165824 | tf_op jit(solution)/shard_map/widen/pallas_call | solution.py:1313
  (144 shorter events, 35.3 us)
Async XLA Ops:
  7.2 164.2 %all-gather.5.cloned.1.call-start = ((), (), s32[]{:S(2)}) async-start(), calls=%async_computation | async-start | bytes 1310720 | tf_op jit(solution)/shard_map/all_gather | solution.py:1332
  10.2 2.9 copy-start.30
  10.3 51.1 %copy-start.4 = (bf16[256,1024]{1,0:T(8,128)(2,1)S(1)}, bf16[256,1024]{1,0:T(8,128)(2,1)}, u32[]{:S(2)}) copy-start(bf16[256,1024]{1,0:T(8,128)(2,1)} %param.14) | copy-start | bytes 1572868
  61.3 473.5 %all-gather.11.cloned.1.call-start = ((), (), s32[]{:S(2)}) async-start(), calls=%async_computation.3 | async-start | bytes 9437184 | tf_op jit(solution)/shard_map/all_gather | solution.py:1499
  61.6 5.9 %copy-start.25 = (f32[256]{0:T(256)}, f32[256]{0:T(256)S(1)}, u32[]{:S(2)}) copy-start(f32[256]{0:T(256)S(1)} %add_rsqrt_fusion.1) | copy-start | bytes 3076
  63.0 4.5 copy-start.21
  63.0 70.3 %copy-start.19 = (f32[1024]{0:T(1024)}, f32[1024]{0:T(1024)S(1)}, u32[]{:S(2)}) copy-start(f32[1024]{0:T(1024)S(1)} %get-tuple-element.56) | copy-start | bytes 12292
  67.5 2.7 copy-start.8
  69.5 4.4 copy-start.23
  327.9 2.0 copy-start.9
  328.0 217.1 %all-gather.9.cloned.1.call-start = ((), (), s32[]{:S(2)}) async-start(), calls=%async_computation.2 | async-start | bytes 9437184 | tf_op jit(solution)/shard_map/all_gather | solution.py:1499
  328.0 2.5 copy-start.20
  328.7 226.7 %all-gather.7.cloned.1.call-start = ((), (), s32[]{:S(2)}) async-start(), calls=%async_computation.1 | async-start | bytes 9437184 | tf_op jit(solution)/shard_map/all_gather | solution.py:1499
  332.7 95.4 %copy-start = (f32[256,1024]{1,0:T(8,128)}, f32[256,1024]{1,0:T(8,128)S(1)}, u32[]{:S(2)}) copy-start(f32[256,1024]{1,0:T(8,128)S(1)} %multiply_add_fusion) | copy-start | bytes 3145732
  418.0 2.8 copy-start.5
  418.0 2.8 copy-start.15
  418.0 2.8 copy-start.22
  418.0 2.8 copy-start.26
  419.2 6.3 %copy-start.17 = (bf16[256,8,64]{0,2,1:T(8,128)(2,1)}, bf16[256,8,64]{0,2,1:T(8,128)(2,1)S(1)}, u32[]{:S(2)}) copy-start(bf16[256,8,64]{0,2,1:T(8,128)(2,1)S(1)} %pad_maximum_fusion.7) | copy-start | bytes 786436
  420.7 4.8 copy-start.13
  420.8 5.9 %copy-start.29 = (bf16[128]{0:T(256)(128)(2,1)S(1)}, bf16[128]{0:T(256)(128)(2,1)}, u32[]{:S(2)}) copy-start(bf16[128]{0:T(256)(128)(2,1)} %copy-done.28) | copy-start | bytes 772
  527.3 2.6 copy-start.7
  531.5 2.0 copy-start.6
  531.5 2.1 copy-start.12
  (12 other events, 18.4 us)
Sparse Core Ops, SparseCore 0:
  61.4 29.8 all-gather.4
  328.1 52.8 all-gather.10
  382.9 54.2 all-gather.8
  438.9 71.1 all-gather.6
